TPU v7x, 128 devices: a whole 4x4x4 slice. The times are simulated.
128 devices in a mesh: item: 4 (over z), user: 32 (over y, x, core).
Axes of the slice: x: 4, y: 4, z: 4, core: 2. Of those that a mesh axis runs over, the one named last changes fastest.
Arguments:
- interactions: bfloat16 [65536, 16384], P('user', 'item'), may hold values from 0 to 1, as said below
- omega: float32 [16384, 256], P('item'), may hold values from -6 to 6
Outputs:
- scaled_basis: float32 [16384, 256], P('item')
Inputs may be any that keep to these rules, and one draw needn't show every extreme that they name: `interactions`: every entry is 0 or 1.
All inputs are finite; a program needn't handle non-finite values.
Results may differ from a plain program's by a relative error of at most 0.0003.
Values sent between devices are 32-bit elements; how exact they have to be, the bound alone decides.
No kernel may reach another device: no remote copies, remote signals or barrier semaphores. Data moves between devices by JAX's collectives and lax.ppermute only.
A program may use at most 128 MiB of HBM per device.

v0:
```python
import jax
import jax.numpy as jnp
from jax import lax
from jax.experimental import pallas as pl
from jax.experimental.pallas import tpu as pltpu
from jax.sharding import PartitionSpec as P

ridge = 200.0
highest = lax.Precision.HIGHEST
f32 = jnp.float32
bf16 = jnp.bfloat16
side = 4
steps = (1, 3, 2)


def exact_dot(a, b, ca, cb):
    return lax.dot_general(a, b, (((ca,), (cb,)), ((), ())), precision=highest, preferred_element_type=f32)


def fast_dot(a, b):
    return lax.dot_general(a, b, (((1,), (0,)), ((), ())), preferred_element_type=f32)


def good_dot(a, b, ca, cb):
    dims = (((ca,), (cb,)), ((), ()))
    dot = lambda l, r: lax.dot_general(l, r, dims, preferred_element_type=f32)
    (a0, a1), (b0, b1) = slices(a), slices(b)
    return dot(a0, b0) + (dot(a0, b1) + dot(a1, b0))


def slices(x):
    high = x.astype(bf16)
    return high, (x - high.astype(f32)).astype(bf16)


def pairs_of(axis, step):
    pairs = []
    for u in range(2 * side * side):
        y, x, core = u // (2 * side), u // 2 % side, u % 2
        if axis == "core":
            core = 1 - core
        elif (axis == "first") == (core == 0):
            x = (x + step) % side
        else:
            y = (y + step) % side
        pairs.append((u, (y * side + x) * 2 + core))
    return pairs


def shift(a, axis, step=1):
    if axis == "item":
        return lax.ppermute(a, "item", [(i, (i + step) % side) for i in range(side)])
    return lax.ppermute(a, "user", pairs_of(axis, step))


vmem = pl.BlockSpec(memory_space=pltpu.VMEM)
smem = pl.BlockSpec(memory_space=pltpu.SMEM)
hbm = pl.BlockSpec(memory_space=pl.ANY)


def rows_kernel(place_ref, a_ref, omega_ref, *refs):
    outs, (high, low) = refs[:-2], refs[-2:]
    at = pl.program_id(0)

    @pl.when(at == 0)
    def _():
        high[...], low[...] = slices(omega_ref[...])

    a = a_ref[...]
    y = (fast_dot(a, high[...]) + fast_dot(a, low[...])).T
    per = pl.num_programs(0) // len(outs)
    for k, out in enumerate(outs):

        @pl.when(at // per == k)
        def _():
            out[...] = y


def user_rows(places, a, omega, block=256):
    users, items = a.shape
    rank = omega.shape[1]
    span = users // side
    per = span // block
    count = len(places)
    return pl.pallas_call(
        rows_kernel,
        out_shape=(jax.ShapeDtypeStruct((rank, span), f32),) * count,
        grid_spec=pltpu.PrefetchScalarGridSpec(
            num_scalar_prefetch=1,
            grid=(per * count,),
            in_specs=[pl.BlockSpec((block, items), lambda i, s: (s[i // per] * per + i % per, 0)), vmem],
            out_specs=tuple(
                pl.BlockSpec((rank, block), lambda i, s, k=k: (0, jnp.clip(i - k * per, 0, per - 1)))
                for k in range(count)
            ),
            scratch_shapes=[pltpu.VMEM((items, rank), bf16)] * 2,
        ),
        name="user_rows",
    )(jnp.stack(places).astype(jnp.int32), a, omega)


def columns_kernel(count, adds, place_ref, *refs):
    ys, blocks = refs[:count], refs[count : 2 * count]
    z_ref, both = refs[-2], refs[-1]
    rank, span = ys[0].shape

    @pl.when(pl.program_id(0) == 0)
    def _():
        for d, ref in enumerate(ys):
            both[:rank, d * span : d * span + span], both[rank:, d * span : d * span + span] = slices(ref[...])

    out = None
    for d, ref in enumerate(blocks):
        term = fast_dot(both[:, d * span : d * span + span], ref[...])
        out = term if out is None else out + term
    z = out[:rank] + out[rank:]
    width = z_ref.shape[2]
    for k in range(z_ref.shape[0]):
        part = z[:, k * width : k * width + width]
        z_ref[k] = part + refs[2 * count][k] if adds else part


def item_columns(place, ys, a, total=None, only=None, block=512):
    users, items = a.shape
    rank, span = ys[0].shape
    count = len(ys)
    width = items // 8
    per = block // width
    grid = items // block // (1 if only is None else 2)
    start = 0 if not only else grid
    in_half = items // block // 2

    def of_items(i, s):
        at = i + start
        core = s[count]
        return (at // in_half + 1 + core) % 2 * in_half + at % in_half

    ins = [pl.BlockSpec((rank, span), lambda i, s: (0, 0), pipeline_mode=pl.Buffered(1))] * count
    for d in range(count):
        ins.append(pl.BlockSpec((span, block), lambda i, s, d=d: (s[d], of_items(i, s))))
    args = [*ys, *[a] * count]
    if total is not None:
        ins.append(pl.BlockSpec((per, rank, width), lambda i, s: (i + start, 0, 0)))
        args.append(total)
    return pl.pallas_call(
        lambda *refs: columns_kernel(count, total is not None, *refs),
        out_shape=jax.ShapeDtypeStruct((grid * per, rank, width), f32),
        grid_spec=pltpu.PrefetchScalarGridSpec(
            num_scalar_prefetch=1,
            grid=(grid,),
            in_specs=ins,
            out_specs=pl.BlockSpec((per, rank, width), lambda i, s: (i, 0, 0)),
            scratch_shapes=[pltpu.VMEM((2 * rank, count * span), bf16)],
        ),
        name="item_columns",
    )(place, *args)


def inverse_factor_half(block):
    n = block.shape[0]
    count = n // 8
    tile = (8, n)
    lanes = lax.broadcasted_iota(jnp.int32, tile, 1)
    subs = lax.broadcasted_iota(jnp.int32, tile, 0)
    spread = lambda v: jnp.broadcast_to(v, tile)
    rows = [block[8 * k : 8 * k + 8, :] for k in range(count)]
    out = []
    for p in range(count):
        c = 8 * p
        panel = rows[p]
        mine = [spread(panel[:, c + t : c + t + 1]) for t in range(8)]
        invs, leads, tops, scale = [], [], [], jnp.ones(tile, f32)
        for j in range(8):
            pivot = spread(mine[j][j : j + 1, :])
            inv = 1.0 / pivot
            invs.append(inv)
            scale = jnp.where(subs == j, pivot, scale)
            factor = jnp.where(subs > j, mine[j] * inv, 0.0)
            tops.append([None] * (j + 1) + [spread(mine[t][j : j + 1, :]) for t in range(j + 1, 8)])
            for t in range(j + 1, 8):
                mine[t] = mine[t] - factor * tops[j][t]
            panel = jnp.where((lanes == c + j) & (subs >= j), jnp.where(subs == j, 1.0, 0.0), panel)
            lead = spread(panel[j : j + 1, :])
            panel = panel - factor * lead
            leads.append(jnp.where((lanes > c + j) & (lanes < c + 8), 0.0, lead))
        out.append(jnp.where(lanes <= subs + c, panel, 0.0) * lax.rsqrt(scale))
        cleared = (lanes >= c) & (lanes < c + 8)
        for k in range(p + 1, count):
            his = [spread(rows[k][:, c + t : c + t + 1]) for t in range(8)]
            new = jnp.where(cleared, 0.0, rows[k])
            for j in range(8):
                factor = his[j] * invs[j]
                for t in range(j + 1, 8):
                    his[t] = his[t] - factor * tops[j][t]
                new = new - factor * leads[j]
            rows[k] = new
    return jnp.concatenate(out, axis=0)


def inverse_factor(gram, out, block, firsts, belows):
    h = block.shape[0]
    block[...] = gram[:h, :h]

    def half(i, carry):
        first = inverse_factor_half(block[...])
        below = exact_dot(gram[h:, :h], first, 1, 1)
        firsts[i] = first
        belows[i] = below
        block[...] = gram[h:, h:] - exact_dot(below, below, 1, 1)
        return carry

    lax.fori_loop(0, 2, half, 0)
    out[:h, :h] = firsts[0]
    out[:h, h:] = jnp.zeros((h, h), f32)
    out[h:, :h] = -exact_dot(firsts[1], exact_dot(belows[0], firsts[0], 1, 0), 1, 0)
    out[h:, h:] = firsts[1]


def factor_scratch(rank):
    h = rank // 2
    return [pltpu.VMEM(shape, f32) for shape in ((rank, rank), (h, h), (2, h, h), (2, h, h))]


def of_ring(own, one, three, two):
    return (own + two) + (one + three)


def mine_of(core_ref, gram):
    h = gram.shape[0] // 2
    return jnp.where(core_ref[0] == 0, gram[:h], gram[h:])


def pair_kernel(near_ref, far_ref, out_ref):
    for k, ref in enumerate((near_ref, far_ref)):
        part = ref[...]
        out_ref[k] = exact_dot(part, part, 1, 1)


def last_pair_kernel(core_ref, near_ref, far_ref, own, one, three, out_ref):
    total = None
    for k, ref in enumerate((near_ref, far_ref)):
        part = ref[...]
        half = of_ring(own[k], one[k], three[k], exact_dot(part, part, 1, 1))
        total = half if total is None else total + half
    out_ref[...] = mine_of(core_ref, total)


def first_gram(core, near, far):
    rank = near[0].shape[0]
    some = [
        pl.pallas_call(
            pair_kernel,
            out_shape=jax.ShapeDtypeStruct((2, rank, rank), f32),
            in_specs=[vmem] * 2,
            out_specs=vmem,
            name="pair_gram",
        )(near[k], far[k])
        for k in range(3)
    ]
    return pl.pallas_call(
        last_pair_kernel,
        out_shape=jax.ShapeDtypeStruct((rank // 2, rank), f32),
        in_specs=[smem] + [vmem] * 5,
        out_specs=vmem,
        name="last_pair_gram",
    )(core, near[3], far[3], *some)


def whole_gram(core_ref, mine_ref, other_ref, gram):
    h = mine_ref.shape[0]
    first = core_ref[0] == 0
    mine, other = mine_ref[...], other_ref[...]
    gram[:h] = jnp.where(first, mine, other)
    gram[h:] = jnp.where(first, other, mine)


def first_kernel(core_ref, mine_ref, other_ref, *refs):
    parts, (basis_ref, out_ref), (held, grams, sems, gram, inverse), scratch = refs[:8], refs[8:10], refs[10:15], refs[15:]
    copies = [pltpu.make_async_copy(ref, held.at[k], sems.at[k]) for k, ref in enumerate(parts)]
    for copy in copies:
        copy.start()
    whole_gram(core_ref, mine_ref, other_ref, gram)
    inverse_factor(gram, inverse, *scratch)
    for copy in copies:
        copy.wait()

    def sweep(k, carry):
        block = exact_dot(inverse[...], held[k], 1, 0)
        basis_ref[k] = block
        grams[k] = good_dot(block, block, 1, 1)
        return carry

    lax.fori_loop(0, 8, sweep, 0)
    halves = [of_ring(*(grams[h * 4 + k] for k in range(4))) for h in range(2)]
    out_ref[...] = mine_of(core_ref, halves[0] + halves[1])


def first_sweep(core, mine, other, parts):
    h, rank = mine.shape
    width = parts[0].shape[1]
    scratch = [pltpu.VMEM((8, rank, width), f32), pltpu.VMEM((8, rank, rank), f32), pltpu.SemaphoreType.DMA((8,))]
    return pl.pallas_call(
        first_kernel,
        out_shape=(jax.ShapeDtypeStruct((8, rank, width), f32), jax.ShapeDtypeStruct((h, rank), f32)),
        in_specs=[smem, vmem, vmem] + [hbm] * 8,
        out_specs=(vmem, vmem),
        scratch_shapes=scratch + [pltpu.VMEM((rank, rank), f32)] + factor_scratch(rank),
        name="first_sweep",
    )(core, mine, other, *parts)


def second_kernel(scale, place_ref, core_ref, mine_ref, other_ref, basis_ref, out_ref, gram, inverse, *scratch):
    @pl.when(pl.program_id(0) == 0)
    def _():
        whole_gram(core_ref, mine_ref, other_ref, gram)
        inverse_factor(gram, inverse, *scratch)

    out_ref[...] = good_dot(inverse[...], basis_ref[0], 1, 0).T * scale


def second_sweep(place, core, mine, other, basis, scale):
    count, rank, width = basis.shape
    return pl.pallas_call(
        lambda *refs: second_kernel(scale, *refs),
        out_shape=jax.ShapeDtypeStruct((count * width, rank), f32),
        grid_spec=pltpu.PrefetchScalarGridSpec(
            num_scalar_prefetch=1,
            grid=(count,),
            in_specs=[smem, vmem, vmem, pl.BlockSpec((1, rank, width), lambda i, s: (i, 0, 0))],
            out_specs=pl.BlockSpec((width, rank), lambda i, s: (s[i], 0)),
            scratch_shapes=[pltpu.VMEM((rank, rank), f32)] + factor_scratch(rank),
        ),
        name="second_sweep",
    )(place, core, mine, other, basis)


def local(interactions, omega):
    user = lax.axis_index("user")
    z, core, x, y = lax.axis_index("item"), user % 2, user // 2 % side, user // (2 * side)
    a = jnp.where(core == 0, x, y)
    b = jnp.where(core == 0, y, x)
    item_count = omega.shape[0] * lax.axis_size("item")
    width = omega.shape[0] // 8
    from_ring = lambda v, axis: [v] + [shift(v, axis, d) for d in steps]

    two, one = user_rows([(z + 2) % side, (z + 1) % side], interactions, omega)
    two, one = shift(two, "item", 2), shift(one, "item", 1)
    three, own = user_rows([(z + 3) % side, z], interactions, omega)
    ys = from_ring(of_ring(own, one, shift(three, "item", 3), two), "item")
    place = lambda *d: jnp.stack([*((z - k) % side for k in d), core])

    total = item_columns(place(0, 1, 3), ys[:3], interactions)
    away = shift(item_columns(place(2), ys[3:], interactions, total, 0), "core")
    kept = item_columns(place(2), ys[3:], interactions, total, 1)

    def block_at(k):
        return lax.dynamic_index_in_dim(kept, k, 0, False) + lax.dynamic_index_in_dim(away, k, 0, False)

    block = of_ring(block_at(a), *(shift(block_at((a + d) % side), "first", d) for d in steps))
    own_omega = lax.dynamic_slice_in_dim(omega, (core * side + a) * width, width, 0)
    block = of_ring(*from_ring(block, "second")) + ridge * own_omega.T

    near = from_ring(block, "first")
    far = [shift(part, "core") for part in near]
    flag = core.reshape(1).astype(jnp.int32)

    def over_items(mine):
        mine = of_ring(*from_ring(mine, "item"))
        return mine, shift(mine, "core")

    basis, gram = first_sweep(flag, *over_items(first_gram(flag, near, far)), [*near, *far])
    offsets = jnp.asarray((0, *steps))
    place = jnp.concatenate([core * side + (a - offsets) % side, (1 - core) * side + (b - offsets) % side])
    return second_sweep(place.astype(jnp.int32), flag, *over_items(gram), basis, float(item_count) ** 0.5)


def solution(mesh):
    in_specs = (P("user", "item"), P("item", None))
    out_specs = P("item", None)
    return jax.shard_map(local, mesh=mesh, in_specs=in_specs, out_specs=out_specs, check_vma=False)
```

profile of v0, /device:TPU:1, one launch (start us, length us, event | category | flops | bytes accessed | tf_op | source)
XLA Modules:
  0.0 237.0 jit_solution(13911303587500972415)
XLA Ops:
  0.7 10.8 %user_rows.3 = (f32[256,512]{1,0:T(8,128)}, f32[256,512]{1,0:T(8,128)}) custom-call(s32[2]{0:T(128)} %get-tuple-element.23.place_ref, bf16[2048,4096]{1,0:T(8,128)(2,1)} %refs_2_.3, f32[4096,256]{1,0:T(8,128)} %omega_ref.3), custom_call_target="tpu_custom_call" | custom-call | tf_op jit(solution)/shard_map/user_rows/pallas_call | solution.py:85
  11.5 4.4 %collective-permute-start = (f32[256,512]{1,0:T(8,128)}, f32[256,512]{1,0:T(8,128)S(1)}, u32[]{:S(2)}, u32[]{:S(2)}) collective-permute-start(f32[256,512]{1,0:T(8,128)} %get-tuple-element.12), channel_id=1, source_target_pairs={{0,64},{32,96},{64,0},{96,32},{1,65},{33,97},{65,1},{97,33},{2,66}... | collective-permute-start | bytes 1572872 | tf_op jit(solution)/shard_map/ppermute | solution.py:52
  16.6 10.9 %user_rows.2 = (f32[256,512]{1,0:T(8,128)}, f32[256,512]{1,0:T(8,128)}) custom-call(s32[2]{0:T(128)} %get-tuple-element.22.place_ref, bf16[2048,4096]{1,0:T(8,128)(2,1)} %refs_2_.3, f32[4096,256]{1,0:T(8,128)} %omega_ref.3), custom_call_target="tpu_custom_call" | custom-call | tf_op jit(solution)/shard_map/user_rows/pallas_call | solution.py:85
  29.4 10.3 %collective-permute-done.1 = f32[256,512]{1,0:T(8,128)S(1)} collective-permute-done((f32[256,512]{1,0:T(8,128)}, f32[256,512]{1,0:T(8,128)S(1)}, u32[]{:S(2)}, u32[]{:S(2)}) %collective-permute-start.1) | collective-permute-done | bytes 524320 | tf_op jit(solution)/shard_map/ppermute | solution.py:52
  41.6 2.9 %collective-permute-start.5 = (f32[256,512]{1,0:T(8,128)S(1)}, f32[256,512]{1,0:T(8,128)S(1)}, u32[]{:S(2)}, u32[]{:S(2)}) collective-permute-start(f32[256,512]{1,0:T(8,128)S(1)} %add_add_fusion.refs_1_), channel_id=1, source_target_pairs={{0,96},{32,0},{64,32},{96,64},{1,97},{33,1},{65,33},{97,65},{2,98}... | collective-permute-start | bytes 1572872 | tf_op jit(solution)/shard_map/ppermute | solution.py:52
  46.9 7.8 %collective-permute-done.4.refs_2_ = f32[256,512]{1,0:T(8,128)S(1)} collective-permute-done((f32[256,512]{1,0:T(8,128)S(1)}, f32[256,512]{1,0:T(8,128)S(1)}, u32[]{:S(2)}, u32[]{:S(2)}) %collective-permute-start.4) | collective-permute-done | bytes 524320 | tf_op jit(solution)/shard_map/ppermute | solution.py:52
  56.3 13.8 %item_columns.3.refs_3_ = f32[8,256,512]{2,1,0:T(8,128)} custom-call(s32[4]{0:T(128)} %pad_add_fusion.4.refs_0_, f32[256,512]{1,0:T(8,128)} %copy-done.1, f32[256,512]{1,0:T(8,128)} %copy-done.8, f32[256,512]{1,0:T(8,128)} %copy-done.9, bf16[2048,4096]{1,0:T(8,128)(2,1)} %refs_2_.3, bf16[2048,4096]{1,0:T(8,128)(2,1)} %refs_2_.3, bf16[2048,4096]{1,0:T(8,128)(2,1)} %refs_2_.3), custom_call_target="tpu_custom_call" | custom-call | tf_op jit(solution)/shard_map/item_columns/pallas_call | solution.py:145
  70.9 5.9 %item_columns.5 = f32[4,256,512]{2,1,0:T(8,128)} custom-call(s32[2]{0:T(128)} %pad_add_fusion.1.refs_0_, f32[256,512]{1,0:T(8,128)} %copy-done.2, bf16[2048,4096]{1,0:T(8,128)(2,1)} %refs_2_.3, f32[8,256,512]{2,1,0:T(8,128)} %item_columns.3.refs_3_), custom_call_target="tpu_custom_call" | custom-call | tf_op jit(solution)/shard_map/item_columns/pallas_call | solution.py:145
  76.8 12.4 %collective-permute-start.6 = (f32[4,256,512]{2,1,0:T(8,128)}, f32[4,256,512]{2,1,0:T(8,128)S(1)}, u32[]{:S(2)}, u32[]{:S(2)}) collective-permute-start(f32[4,256,512]{2,1,0:T(8,128)} %item_columns.5), channel_id=1, source_target_pairs={{0,1},{1,0},{2,3},{3,2},{4,5},{5,4},{6,7},{7,6},{8,9},{9,8},{10,11... | collective-permute-start | bytes 6291464 | tf_op jit(solution)/shard_map/ppermute | solution.py:53
  89.2 5.9 %item_columns.4 = f32[4,256,512]{2,1,0:T(8,128)} custom-call(s32[2]{0:T(128)} %pad_add_fusion.1.refs_0_, f32[256,512]{1,0:T(8,128)} %copy-done.2, bf16[2048,4096]{1,0:T(8,128)(2,1)} %refs_2_.3, f32[8,256,512]{2,1,0:T(8,128)} %item_columns.3.refs_3_), custom_call_target="tpu_custom_call" | custom-call | tf_op jit(solution)/shard_map/item_columns/pallas_call | solution.py:145
  103.3 4.5 %collective-permute-done.7 = f32[256,512]{1,0:T(8,128)S(1)} collective-permute-done((f32[256,512]{1,0:T(8,128)}, f32[256,512]{1,0:T(8,128)S(1)}, u32[]{:S(2)}, u32[]{:S(2)}) %collective-permute-start.7) | collective-permute-done | bytes 524320 | tf_op jit(solution)/shard_map/ppermute | solution.py:53
  107.8 5.6 %collective-permute-done.8 = f32[256,512]{1,0:T(8,128)S(1)} collective-permute-done((f32[256,512]{1,0:T(8,128)}, f32[256,512]{1,0:T(8,128)S(1)}, u32[]{:S(2)}, u32[]{:S(2)}) %collective-permute-start.8) | collective-permute-done | bytes 524320 | tf_op jit(solution)/shard_map/ppermute | solution.py:53
  122.3 3.5 %collective-permute-done.10 = f32[256,512]{1,0:T(8,128)S(1)} collective-permute-done((f32[256,512]{1,0:T(8,128)S(1)}, f32[256,512]{1,0:T(8,128)S(1)}, u32[]{:S(2)}, u32[]{:S(2)}) %collective-permute-start.10) | collective-permute-done | bytes 524320 | tf_op jit(solution)/shard_map/ppermute | solution.py:53
  125.8 5.6 %collective-permute-done.11 = f32[256,512]{1,0:T(8,128)S(1)} collective-permute-done((f32[256,512]{1,0:T(8,128)S(1)}, f32[256,512]{1,0:T(8,128)S(1)}, u32[]{:S(2)}, u32[]{:S(2)}) %collective-permute-start.11) | collective-permute-done | bytes 524320 | tf_op jit(solution)/shard_map/ppermute | solution.py:53
  139.2 7.6 %collective-permute-done.18.near_ref.refs_2_ = f32[256,512]{1,0:T(8,128)S(1)} collective-permute-done((f32[256,512]{1,0:T(8,128)S(1)}, f32[256,512]{1,0:T(8,128)S(1)}, u32[]{:S(2)}, u32[]{:S(2)}) %collective-permute-start.18) | collective-permute-done | bytes 524320 | tf_op jit(solution)/shard_map/ppermute | solution.py:53
  154.0 3.0 %pair_gram.3.own = f32[2,256,256]{2,1,0:T(8,128)} custom-call(f32[256,512]{1,0:T(8,128)} %copy-done, f32[256,512]{1,0:T(8,128)} %copy-done.5), custom_call_target="tpu_custom_call" | custom-call | tf_op jit(solution)/shard_map/pair_gram/pallas_call | solution.py:251
  157.8 3.0 %pair_gram.5.three = f32[2,256,256]{2,1,0:T(8,128)} custom-call(f32[256,512]{1,0:T(8,128)} %copy-done.3, f32[256,512]{1,0:T(8,128)} %copy-done.6), custom_call_target="tpu_custom_call" | custom-call | tf_op jit(solution)/shard_map/pair_gram/pallas_call | solution.py:251
  161.7 3.0 %pair_gram.4.one = f32[2,256,256]{2,1,0:T(8,128)} custom-call(f32[256,512]{1,0:T(8,128)} %copy-done.4, f32[256,512]{1,0:T(8,128)} %copy-done.7), custom_call_target="tpu_custom_call" | custom-call | tf_op jit(solution)/shard_map/pair_gram/pallas_call | solution.py:251
  164.8 3.4 %last_pair_gram.1 = f32[128,256]{1,0:T(8,128)} custom-call(s32[1]{0:T(128)} %bitcast.core_ref.refs_1_, f32[256,512]{1,0:T(8,128)} %collective-permute-done.13.near_ref.refs_3_, f32[256,512]{1,0:T(8,128)} %collective-permute-done.14.far_ref.refs_7_, f32[2,256,256]{2,1,0:T(8,128)} %pair_gram.3.own, f32[2,256,256]{2,1,0:T(8,128)} %pair_gram.4.one, ...), custom_call_target="tpu_custom_call" | custom-call | tf_op jit(solution)/shard_map/last_pair_gram/pallas_call | solution.py:260
  174.5 3.4 %collective-permute-done.21 = f32[128,256]{1,0:T(8,128)S(1)} collective-permute-done((f32[128,256]{1,0:T(8,128)}, f32[128,256]{1,0:T(8,128)S(1)}, u32[]{:S(2)}, u32[]{:S(2)}) %collective-permute-start.21) | collective-permute-done | bytes 131104 | tf_op jit(solution)/shard_map/ppermute | solution.py:52
  182.3 22.5 %first_sweep.1 = (f32[8,256,512]{2,1,0:T(8,128)}, f32[128,256]{1,0:T(8,128)}) custom-call(s32[1]{0:T(128)} %bitcast.core_ref.refs_1_, f32[128,256]{1,0:T(8,128)} %copy-done.11, f32[128,256]{1,0:T(8,128)} %copy-done.14, f32[256,512]{1,0:T(8,128)} %copy-done, f32[256,512]{1,0:T(8,128)} %copy-done.4, f32[256,512]{1,0:T(8,128)} %copy-done.3, ...), custom_call_target="tpu_custom_call" | custom-call | tf_op jit(solution)/shard_map/first_sweep/pallas_call | solution.py:302
  208.3 3.0 %collective-permute-done.24 = f32[128,256]{1,0:T(8,128)S(1)} collective-permute-done((f32[128,256]{1,0:T(8,128)}, f32[128,256]{1,0:T(8,128)S(1)}, u32[]{:S(2)}, u32[]{:S(2)}) %collective-permute-start.24) | collective-permute-done | bytes 131104 | tf_op jit(solution)/shard_map/ppermute | solution.py:52
  211.3 3.5 %collective-permute-done.25 = f32[128,256]{1,0:T(8,128)S(1)} collective-permute-done((f32[128,256]{1,0:T(8,128)}, f32[128,256]{1,0:T(8,128)S(1)}, u32[]{:S(2)}, u32[]{:S(2)}) %collective-permute-start.25) | collective-permute-done | bytes 131104 | tf_op jit(solution)/shard_map/ppermute | solution.py:52
  218.0 19.0 %second_sweep.1 = f32[4096,256]{1,0:T(8,128)} custom-call(s32[8]{0:T(128)} %pad_add_fusion.refs_0_, s32[1]{0:T(128)} %bitcast.core_ref.refs_1_, f32[128,256]{1,0:T(8,128)} %copy-done.10, f32[128,256]{1,0:T(8,128)} %copy-done.13, f32[8,256,512]{2,1,0:T(8,128)} %get-tuple-element.16.refs_4_), custom_call_target="tpu_custom_call" | custom-call | tf_op jit(solution)/shard_map/second_sweep/pallas_call | solution.py:323
  (88 shorter events, 61.0 us)
Async XLA Ops:
  11.5 18.0 %collective-permute-start = (f32[256,512]{1,0:T(8,128)}, f32[256,512]{1,0:T(8,128)S(1)}, u32[]{:S(2)}, u32[]{:S(2)}) collective-permute-start(f32[256,512]{1,0:T(8,128)} %get-tuple-element.12), channel_id=1, source_target_pairs={{0,64},{32,96},{64,0},{96,32},{1,65},{33,97},{65,1},{97,33},{2,66}... | collective-permute-start | bytes 1572872 | tf_op jit(solution)/shard_map/ppermute | solution.py:52
  15.9 23.8 %collective-permute-start.1 = (f32[256,512]{1,0:T(8,128)}, f32[256,512]{1,0:T(8,128)S(1)}, u32[]{:S(2)}, u32[]{:S(2)}) collective-permute-start(f32[256,512]{1,0:T(8,128)} %get-tuple-element.13), channel_id=1, source_target_pairs={{0,32},{32,64},{64,96},{96,0},{1,33},{33,65},{65,97},{97,1},{2,34}... | collective-permute-start | bytes 1572872 | tf_op jit(solution)/shard_map/ppermute | solution.py:52
  27.5 12.5 %collective-permute-start.2 = (f32[256,512]{1,0:T(8,128)}, f32[256,512]{1,0:T(8,128)S(1)}, u32[]{:S(2)}, u32[]{:S(2)}) collective-permute-start(f32[256,512]{1,0:T(8,128)} %get-tuple-element.14), channel_id=1, source_target_pairs={{0,96},{32,0},{64,32},{96,64},{1,97},{33,1},{65,33},{97,65},{2,98}... | collective-permute-start | bytes 1572872 | tf_op jit(solution)/shard_map/ppermute | solution.py:52
  41.2 13.4 %collective-permute-start.4 = (f32[256,512]{1,0:T(8,128)S(1)}, f32[256,512]{1,0:T(8,128)S(1)}, u32[]{:S(2)}, u32[]{:S(2)}) collective-permute-start(f32[256,512]{1,0:T(8,128)S(1)} %add_add_fusion.refs_1_), channel_id=1, source_target_pairs={{0,32},{32,64},{64,96},{96,0},{1,33},{33,65},{65,97},{97,1},{2,34}... | collective-permute-start | bytes 1572872 | tf_op jit(solution)/shard_map/ppermute | solution.py:52
  41.6 13.4 %collective-permute-start.5 = (f32[256,512]{1,0:T(8,128)S(1)}, f32[256,512]{1,0:T(8,128)S(1)}, u32[]{:S(2)}, u32[]{:S(2)}) collective-permute-start(f32[256,512]{1,0:T(8,128)S(1)} %add_add_fusion.refs_1_), channel_id=1, source_target_pairs={{0,96},{32,0},{64,32},{96,64},{1,97},{33,1},{65,33},{97,65},{2,98}... | collective-permute-start | bytes 1572872 | tf_op jit(solution)/shard_map/ppermute | solution.py:52
  44.5 25.5 %collective-permute-start.3 = (f32[256,512]{1,0:T(8,128)S(1)}, f32[256,512]{1,0:T(8,128)S(1)}, u32[]{:S(2)}, u32[]{:S(2)}) collective-permute-start(f32[256,512]{1,0:T(8,128)S(1)} %add_add_fusion.refs_1_), channel_id=1, source_target_pairs={{0,64},{32,96},{64,0},{96,32},{1,65},{33,97},{65,1},{97,33},{2,66}... | collective-permute-start | bytes 1572872 | tf_op jit(solution)/shard_map/ppermute | solution.py:52
  76.8 18.4 %collective-permute-start.6 = (f32[4,256,512]{2,1,0:T(8,128)}, f32[4,256,512]{2,1,0:T(8,128)S(1)}, u32[]{:S(2)}, u32[]{:S(2)}) collective-permute-start(f32[4,256,512]{2,1,0:T(8,128)} %item_columns.5), channel_id=1, source_target_pairs={{0,1},{1,0},{2,3},{3,2},{4,5},{5,4},{6,7},{7,6},{8,9},{9,8},{10,11... | collective-permute-start | bytes 6291464 | tf_op jit(solution)/shard_map/ppermute | solution.py:53
  97.7 10.1 %collective-permute-start.7 = (f32[256,512]{1,0:T(8,128)}, f32[256,512]{1,0:T(8,128)S(1)}, u32[]{:S(2)}, u32[]{:S(2)}) collective-permute-start(f32[256,512]{1,0:T(8,128)} %get-tuple-element.19), channel_id=1, source_target_pairs={{0,4},{1,17},{2,6},{3,19},{4,0},{5,21},{6,2},{7,23},{8,12},{9,25},... | collective-permute-start | bytes 1572872 | tf_op jit(solution)/shard_map/ppermute | solution.py:53
  100.7 12.8 %collective-permute-start.8 = (f32[256,512]{1,0:T(8,128)}, f32[256,512]{1,0:T(8,128)S(1)}, u32[]{:S(2)}, u32[]{:S(2)}) collective-permute-start(f32[256,512]{1,0:T(8,128)} %get-tuple-element.18), channel_id=1, source_target_pairs={{0,2},{1,9},{2,4},{3,11},{4,6},{5,13},{6,0},{7,15},{8,10},{9,17},{... | collective-permute-start | bytes 1572872 | tf_op jit(solution)/shard_map/ppermute | solution.py:53
  101.1 13.2 %collective-permute-start.9 = (f32[256,512]{1,0:T(8,128)}, f32[256,512]{1,0:T(8,128)}, u32[]{:S(2)}, u32[]{:S(2)}) collective-permute-start(f32[256,512]{1,0:T(8,128)} %get-tuple-element.17), channel_id=1, source_target_pairs={{0,6},{1,25},{2,0},{3,27},{4,2},{5,29},{6,4},{7,31},{8,14},{9,1},{... | collective-permute-start | bytes 1572872 | tf_op jit(solution)/shard_map/ppermute | solution.py:53
  115.8 10.0 %collective-permute-start.10 = (f32[256,512]{1,0:T(8,128)S(1)}, f32[256,512]{1,0:T(8,128)S(1)}, u32[]{:S(2)}, u32[]{:S(2)}) collective-permute-start(f32[256,512]{1,0:T(8,128)S(1)} %fusion), channel_id=1, source_target_pairs={{0,16},{1,5},{2,18},{3,7},{4,20},{5,1},{6,22},{7,3},{8,24},{9,13},... | collective-permute-start | bytes 1572872 | tf_op jit(solution)/shard_map/ppermute | solution.py:53
  118.4 13.0 %collective-permute-start.11 = (f32[256,512]{1,0:T(8,128)S(1)}, f32[256,512]{1,0:T(8,128)S(1)}, u32[]{:S(2)}, u32[]{:S(2)}) collective-permute-start(f32[256,512]{1,0:T(8,128)S(1)} %fusion), channel_id=1, source_target_pairs={{0,8},{1,3},{2,10},{3,5},{4,12},{5,7},{6,14},{7,1},{8,16},{9,11},{... | collective-permute-start | bytes 1572872 | tf_op jit(solution)/shard_map/ppermute | solution.py:53
  119.1 12.6 %collective-permute-start.12 = (f32[256,512]{1,0:T(8,128)S(1)}, f32[256,512]{1,0:T(8,128)}, u32[]{:S(2)}, u32[]{:S(2)}) collective-permute-start(f32[256,512]{1,0:T(8,128)S(1)} %fusion), channel_id=1, source_target_pairs={{0,24},{1,7},{2,26},{3,1},{4,28},{5,3},{6,30},{7,5},{8,0},{9,15},{... | collective-permute-start | bytes 1572872 | tf_op jit(solution)/shard_map/ppermute | solution.py:53
  133.1 13.7 %collective-permute-start.18 = (f32[256,512]{1,0:T(8,128)S(1)}, f32[256,512]{1,0:T(8,128)S(1)}, u32[]{:S(2)}, u32[]{:S(2)}) collective-permute-start(f32[256,512]{1,0:T(8,128)S(1)} %bitcast_add_fusion.near_ref.refs_0_), channel_id=1, source_target_pairs={{0,6},{1,25},{2,0},{3,27},{4,2},{5,29},{6,4},{7,31},{8,14},{9,1},{... | collective-permute-start | bytes 1572872 | tf_op jit(solution)/shard_map/ppermute | solution.py:53
  135.1 15.3 %collective-permute-start.16 = (f32[256,512]{1,0:T(8,128)S(1)}, f32[256,512]{1,0:T(8,128)S(1)}, u32[]{:S(2)}, u32[]{:S(2)}) collective-permute-start(f32[256,512]{1,0:T(8,128)S(1)} %bitcast_add_fusion.near_ref.refs_0_), channel_id=1, source_target_pairs={{0,2},{1,9},{2,4},{3,11},{4,6},{5,13},{6,0},{7,15},{8,10},{9,17},{... | collective-permute-start | bytes 1572872 | tf_op jit(solution)/shard_map/ppermute | solution.py:53
  135.1 18.0 %collective-permute-start.13 = (f32[256,512]{1,0:T(8,128)S(1)}, f32[256,512]{1,0:T(8,128)}, u32[]{:S(2)}, u32[]{:S(2)}) collective-permute-start(f32[256,512]{1,0:T(8,128)S(1)} %bitcast_add_fusion.near_ref.refs_0_), channel_id=1, source_target_pairs={{0,4},{1,17},{2,6},{3,19},{4,0},{5,21},{6,2},{7,23},{8,12},{9,25},... | collective-permute-start | bytes 1572872 | tf_op jit(solution)/shard_map/ppermute | solution.py:53
  136.7 16.4 %collective-permute-start.15 = (f32[256,512]{1,0:T(8,128)S(1)}, f32[256,512]{1,0:T(8,128)S(1)}, u32[]{:S(2)}, u32[]{:S(2)}) collective-permute-start(f32[256,512]{1,0:T(8,128)S(1)} %bitcast_add_fusion.near_ref.refs_0_), channel_id=1, source_target_pairs={{0,1},{1,0},{2,3},{3,2},{4,5},{5,4},{6,7},{7,6},{8,9},{9,8},{10,11... | collective-permute-start | bytes 1572872 | tf_op jit(solution)/shard_map/ppermute | solution.py:53
  146.8 10.2 %collective-permute-start.19 = (f32[256,512]{1,0:T(8,128)S(1)}, f32[256,512]{1,0:T(8,128)S(1)}, u32[]{:S(2)}, u32[]{:S(2)}) collective-permute-start(f32[256,512]{1,0:T(8,128)S(1)} %collective-permute-done.18.near_ref.refs_2_), channel_id=1, source_target_pairs={{0,1},{1,0},{2,3},{3,2},{4,5},{5,4},{6,7},{7,6},{8,9},{9,8},{10,11... | collective-permute-start | bytes 1572872 | tf_op jit(solution)/shard_map/ppermute | solution.py:53
  150.3 10.5 %collective-permute-start.17 = (f32[256,512]{1,0:T(8,128)S(1)}, f32[256,512]{1,0:T(8,128)S(1)}, u32[]{:S(2)}, u32[]{:S(2)}) collective-permute-start(f32[256,512]{1,0:T(8,128)S(1)} %collective-permute-done.16.near_ref.refs_1_), channel_id=1, source_target_pairs={{0,1},{1,0},{2,3},{3,2},{4,5},{5,4},{6,7},{7,6},{8,9},{9,8},{10,11... | collective-permute-start | bytes 1572872 | tf_op jit(solution)/shard_map/ppermute | solution.py:53
  153.1 11.7 %collective-permute-start.14 = (f32[256,512]{1,0:T(8,128)}, f32[256,512]{1,0:T(8,128)}, u32[]{:S(2)}, u32[]{:S(2)}) collective-permute-start(f32[256,512]{1,0:T(8,128)} %collective-permute-done.13.near_ref.refs_3_), channel_id=1, source_target_pairs={{0,1},{1,0},{2,3},{3,2},{4,5},{5,4},{6,7},{7,6},{8,9},{9,8},{10,11... | collective-permute-start | bytes 1572872 | tf_op jit(solution)/shard_map/ppermute | solution.py:53
  169.8 8.0 %collective-permute-start.21 = (f32[128,256]{1,0:T(8,128)}, f32[128,256]{1,0:T(8,128)S(1)}, u32[]{:S(2)}, u32[]{:S(2)}) collective-permute-start(f32[128,256]{1,0:T(8,128)} %last_pair_gram.1), channel_id=1, source_target_pairs={{0,32},{32,64},{64,96},{96,0},{1,33},{33,65},{65,97},{97,1},{2,34}... | collective-permute-start | bytes 393224 | tf_op jit(solution)/shard_map/ppermute | solution.py:52
  204.8 6.5 %collective-permute-start.24 = (f32[128,256]{1,0:T(8,128)}, f32[128,256]{1,0:T(8,128)S(1)}, u32[]{:S(2)}, u32[]{:S(2)}) collective-permute-start(f32[128,256]{1,0:T(8,128)} %get-tuple-element.15), channel_id=1, source_target_pairs={{0,64},{32,96},{64,0},{96,32},{1,65},{33,97},{65,1},{97,33},{2,66}... | collective-permute-start | bytes 393224 | tf_op jit(solution)/shard_map/ppermute | solution.py:52
  205.6 9.2 %collective-permute-start.25 = (f32[128,256]{1,0:T(8,128)}, f32[128,256]{1,0:T(8,128)S(1)}, u32[]{:S(2)}, u32[]{:S(2)}) collective-permute-start(f32[128,256]{1,0:T(8,128)} %get-tuple-element.15), channel_id=1, source_target_pairs={{0,32},{32,64},{64,96},{96,0},{1,33},{33,65},{65,97},{97,1},{2,34}... | collective-permute-start | bytes 393224 | tf_op jit(solution)/shard_map/ppermute | solution.py:52
  207.8 7.0 %collective-permute-start.26 = (f32[128,256]{1,0:T(8,128)}, f32[128,256]{1,0:T(8,128)S(1)}, u32[]{:S(2)}, u32[]{:S(2)}) collective-permute-start(f32[128,256]{1,0:T(8,128)} %get-tuple-element.15), channel_id=1, source_target_pairs={{0,96},{32,0},{64,32},{96,64},{1,97},{33,1},{65,33},{97,65},{2,98}... | collective-permute-start | bytes 393224 | tf_op jit(solution)/shard_map/ppermute | solution.py:52
  (20 other events, 119.1 us)
where the time goes:
time: 238 us; the launch traced here: 237 us
  Pallas kernels  101 us (42%)
  waiting for transfers between devices  60.2 us (25%)
  starting transfers between devices  56 us (24%)
  other arithmetic  11.3 us (5%)
  local copies, waits for them, and re-layouts  7.96 us (3%)
    ppermute x16, starting transfers between devices, shift(): return lax.ppermute(a, 'user', pairs_of(axis, step))  36.7 us
    ppermute x12, waiting for transfers between devices, shift(): lax.ppermute(a, 'item', [(i, (i + step) % side) for i in range(side)])  30.9 us
    ppermute x16, waiting for transfers between devices, shift(): return lax.ppermute(a, 'user', pairs_of(axis, step))  29.3 us
    pallas_call x3, Pallas kernels, item_columns(): pl.pallas_call(lambda *refs: columns_kernel(count, total is not None, *re...  25.6 us
    pallas_call x1, Pallas kernels, first_sweep(): pl.pallas_call(first_kernel, out_shape=(jax.ShapeDtypeStruct((8, rank, wi...  22.5 us
    pallas_call x2, Pallas kernels, user_rows(): pl.pallas_call(rows_kernel, out_shape=(jax.ShapeDtypeStruct((rank, span),...  21.7 us
    ppermute x12, starting transfers between devices, shift(): lax.ppermute(a, 'item', [(i, (i + step) % side) for i in range(side)])  19.4 us
    pallas_call x1, Pallas kernels, second_sweep(): pl.pallas_call(lambda *refs: second_kernel(scale, *refs), out_shape=jax.S...  19 us
  transfers between devices with their start and end apart: 28, of which 18 were waited for; matrix products, arithmetic and copies ran while one was open for 1% of the time, Pallas kernels for 17%

commit v1 on v0

--- a/solution.py
+++ b/solution.py
@@ -4,6 +4,7 @@
 from jax.experimental import pallas as pl
 from jax.experimental.pallas import tpu as pltpu
 from jax.sharding import PartitionSpec as P
+
 
 ridge = 200.0
 highest = lax.Precision.HIGHEST
@@ -58,56 +59,58 @@
 hbm = pl.BlockSpec(memory_space=pl.ANY)
 
 
-def rows_kernel(place_ref, a_ref, omega_ref, *refs):
-    outs, (high, low) = refs[:-2], refs[-2:]
-    at = pl.program_id(0)
-
-    @pl.when(at == 0)
-    def _():
-        high[...], low[...] = slices(omega_ref[...])
-
-    a = a_ref[...]
-    y = (fast_dot(a, high[...]) + fast_dot(a, low[...])).T
-    per = pl.num_programs(0) // len(outs)
-    for k, out in enumerate(outs):
-
-        @pl.when(at // per == k)
+def rows_kernel(place_ref, a0, a1, omega_ref, out0, out1, sum0, sum1):
+    at, last = pl.program_id(0), pl.num_programs(0) - 1
+    high, low = slices(omega_ref[...])
+    for ref, total, out in ((a0, sum0, out0), (a1, sum1, out1)):
+        a = ref[...]
+        y = fast_dot(a, high) + fast_dot(a, low)
+
+        @pl.when(at == 0)
         def _():
-            out[...] = y
-
-
-def user_rows(places, a, omega, block=256):
+            total[...] = y
+
+        @pl.when((at > 0) & (at < last))
+        def _():
+            total[...] += y
+
+        @pl.when(at == last)
+        def _():
+            out[...] = (total[...] + y).T
+
+
+def user_rows(places, a, omega, depth=1024):
     users, items = a.shape
     rank = omega.shape[1]
     span = users // side
-    per = span // block
-    count = len(places)
+    out = pl.BlockSpec((rank, span), lambda k, s: (0, 0))
     return pl.pallas_call(
         rows_kernel,
-        out_shape=(jax.ShapeDtypeStruct((rank, span), f32),) * count,
+        out_shape=(jax.ShapeDtypeStruct((rank, span), f32),) * 2,
         grid_spec=pltpu.PrefetchScalarGridSpec(
             num_scalar_prefetch=1,
-            grid=(per * count,),
-            in_specs=[pl.BlockSpec((block, items), lambda i, s: (s[i // per] * per + i % per, 0)), vmem],
-            out_specs=tuple(
-                pl.BlockSpec((rank, block), lambda i, s, k=k: (0, jnp.clip(i - k * per, 0, per - 1)))
-                for k in range(count)
-            ),
-            scratch_shapes=[pltpu.VMEM((items, rank), bf16)] * 2,
+            grid=(items // depth,),
+            in_specs=[pl.BlockSpec((span, depth), lambda k, s, d=d: (s[d], k)) for d in range(2)]
+            + [pl.BlockSpec((depth, rank), lambda k, s: (k, 0))],
+            out_specs=(out, out),
+            scratch_shapes=[pltpu.VMEM((span, rank), f32)] * 2,
         ),
         name="user_rows",
-    )(jnp.stack(places).astype(jnp.int32), a, omega)
-
-
-def columns_kernel(count, adds, place_ref, *refs):
-    ys, blocks = refs[:count], refs[count : 2 * count]
+    )(jnp.stack(places).astype(jnp.int32), a, a, omega)
+
+
+def columns_kernel(count, splits, adds, place_ref, *refs):
+    ys, blocks = refs[: count * splits], refs[count * splits : count * splits + count]
     z_ref, both = refs[-2], refs[-1]
-    rank, span = ys[0].shape
+    rows, span = ys[0].shape
+    rank = rows * splits
 
     @pl.when(pl.program_id(0) == 0)
     def _():
         for d, ref in enumerate(ys):
-            both[:rank, d * span : d * span + span], both[rank:, d * span : d * span + span] = slices(ref[...])
+            at = slice(d // splits * span, d // splits * span + span)
+            row = d % splits * rows
+            both[row : row + rows, at], both[rank + row : rank + row + rows, at] = slices(ref[...])
 
     out = None
     for d, ref in enumerate(blocks):
@@ -117,13 +120,14 @@
     width = z_ref.shape[2]
     for k in range(z_ref.shape[0]):
         part = z[:, k * width : k * width + width]
-        z_ref[k] = part + refs[2 * count][k] if adds else part
-
-
-def item_columns(place, ys, a, total=None, only=None, block=512):
-    users, items = a.shape
-    rank, span = ys[0].shape
-    count = len(ys)
+        z_ref[k] = part + refs[-3][k] if adds else part
+
+
+def item_columns(place, ys, a, total=None, only=None, splits=1, block=1024):
+    _, items = a.shape
+    rows, span = ys[0].shape
+    rank = rows * splits
+    count = len(ys) // splits
     width = items // 8
     per = block // width
     grid = items // block // (1 if only is None else 2)
@@ -135,7 +139,7 @@
         core = s[count]
         return (at // in_half + 1 + core) % 2 * in_half + at % in_half
 
-    ins = [pl.BlockSpec((rank, span), lambda i, s: (0, 0), pipeline_mode=pl.Buffered(1))] * count
+    ins = [vmem] * len(ys)
     for d in range(count):
         ins.append(pl.BlockSpec((span, block), lambda i, s, d=d: (s[d], of_items(i, s))))
     args = [*ys, *[a] * count]
@@ -143,7 +147,7 @@
         ins.append(pl.BlockSpec((per, rank, width), lambda i, s: (i + start, 0, 0)))
         args.append(total)
     return pl.pallas_call(
-        lambda *refs: columns_kernel(count, total is not None, *refs),
+        lambda *refs: columns_kernel(count, splits, total is not None, *refs),
         out_shape=jax.ShapeDtypeStruct((grid * per, rank, width), f32),
         grid_spec=pltpu.PrefetchScalarGridSpec(
             num_scalar_prefetch=1,
@@ -216,6 +220,26 @@
     out[h:, h:] = firsts[1]
 
 
+def inverse_factor_near_one(gram, out):
+    n = gram.shape[0]
+    row = lax.broadcasted_iota(jnp.int32, (n, n), 0)
+    column = lax.broadcasted_iota(jnp.int32, (n, n), 1)
+    one = jnp.where(row == column, 1.0, 0.0)
+    lower = jnp.where(row > column, 1.0, jnp.where(row == column, 0.5, 0.0))
+    out[...] = one - lower * (gram[...] - one)
+
+    def more(state):
+        return (state[1] > 1e-7) & (state[0] < 6)
+
+    def step(state):
+        inverse = out[...]
+        residual = exact_dot(exact_dot(inverse, gram[...], 1, 0), inverse, 1, 1) - one
+        out[...] = inverse - exact_dot(lower * residual, inverse, 1, 0)
+        return state[0] + 1, jnp.sum(residual * residual)
+
+    return lax.while_loop(more, step, (0, jnp.float32(1.0)))[1] <= 1e-7
+
+
 def factor_scratch(rank):
     h = rank // 2
     return [pltpu.VMEM(shape, f32) for shape in ((rank, rank), (h, h), (2, h, h), (2, h, h))]
@@ -226,8 +250,14 @@
 
 
 def mine_of(core_ref, gram):
-    h = gram.shape[0] // 2
-    return jnp.where(core_ref[0] == 0, gram[:h], gram[h:])
+    h, q = gram.shape[0] // 2, gram.shape[0] // 4
+    one = jnp.concatenate([gram[:h, :h], gram[h : h + q, :h]], axis=0)
+    two = jnp.concatenate([gram[h:, h:], gram[h + q :, :h]], axis=0)
+    return jnp.where(core_ref[0] == 0, one, two)
+
+
+def packed(rank):
+    return jax.ShapeDtypeStruct((rank // 2 + rank // 4, rank // 2), f32)
 
 
 def pair_kernel(near_ref, far_ref, out_ref):
@@ -236,42 +266,42 @@
         out_ref[k] = exact_dot(part, part, 1, 1)
 
 
-def last_pair_kernel(core_ref, near_ref, far_ref, own, one, three, out_ref):
+def last_pairs_kernel(core_ref, own_ref, *refs):
+    near, far, out_ref = refs[:3], refs[3:6], refs[6]
     total = None
-    for k, ref in enumerate((near_ref, far_ref)):
-        part = ref[...]
-        half = of_ring(own[k], one[k], three[k], exact_dot(part, part, 1, 1))
+    for k, parts in enumerate((near, far)):
+        grams = [exact_dot(ref[...], ref[...], 1, 1) for ref in parts]
+        half = of_ring(own_ref[k], *grams)
         total = half if total is None else total + half
     out_ref[...] = mine_of(core_ref, total)
 
 
 def first_gram(core, near, far):
     rank = near[0].shape[0]
-    some = [
-        pl.pallas_call(
-            pair_kernel,
-            out_shape=jax.ShapeDtypeStruct((2, rank, rank), f32),
-            in_specs=[vmem] * 2,
-            out_specs=vmem,
-            name="pair_gram",
-        )(near[k], far[k])
-        for k in range(3)
-    ]
+    own = pl.pallas_call(
+        pair_kernel,
+        out_shape=jax.ShapeDtypeStruct((2, rank, rank), f32),
+        in_specs=[vmem] * 2,
+        out_specs=vmem,
+        name="pair_gram",
+    )(near[0], far[0])
     return pl.pallas_call(
-        last_pair_kernel,
-        out_shape=jax.ShapeDtypeStruct((rank // 2, rank), f32),
-        in_specs=[smem] + [vmem] * 5,
+        last_pairs_kernel,
+        out_shape=packed(rank),
+        in_specs=[smem] + [vmem] * 7,
         out_specs=vmem,
-        name="last_pair_gram",
-    )(core, near[3], far[3], *some)
+        name="last_pair_grams",
+    )(core, own, *near[1:], *far[1:])
 
 
 def whole_gram(core_ref, mine_ref, other_ref, gram):
-    h = mine_ref.shape[0]
-    first = core_ref[0] == 0
+    h = gram.shape[0] // 2
     mine, other = mine_ref[...], other_ref[...]
-    gram[:h] = jnp.where(first, mine, other)
-    gram[h:] = jnp.where(first, other, mine)
+    one = jnp.where(core_ref[0] == 0, mine, other)
+    two = jnp.where(core_ref[0] == 0, other, mine)
+    below = jnp.concatenate([one[h:], two[h:]], axis=0)
+    gram[:h, :h], gram[:h, h:] = one[:h], below.T
+    gram[h:, :h], gram[h:, h:] = below, two[:h]
 
 
 def first_kernel(core_ref, mine_ref, other_ref, *refs):
@@ -290,18 +320,17 @@
         grams[k] = good_dot(block, block, 1, 1)
         return carry
 
-    lax.fori_loop(0, 8, sweep, 0)
+    lax.fori_loop(0, 8, sweep, 0, unroll=2)
     halves = [of_ring(*(grams[h * 4 + k] for k in range(4))) for h in range(2)]
     out_ref[...] = mine_of(core_ref, halves[0] + halves[1])
 
 
 def first_sweep(core, mine, other, parts):
-    h, rank = mine.shape
-    width = parts[0].shape[1]
+    rank, width = parts[0].shape
     scratch = [pltpu.VMEM((8, rank, width), f32), pltpu.VMEM((8, rank, rank), f32), pltpu.SemaphoreType.DMA((8,))]
     return pl.pallas_call(
         first_kernel,
-        out_shape=(jax.ShapeDtypeStruct((8, rank, width), f32), jax.ShapeDtypeStruct((h, rank), f32)),
+        out_shape=(jax.ShapeDtypeStruct((8, rank, width), f32), packed(rank)),
         in_specs=[smem, vmem, vmem] + [hbm] * 8,
         out_specs=(vmem, vmem),
         scratch_shapes=scratch + [pltpu.VMEM((rank, rank), f32)] + factor_scratch(rank),
@@ -313,7 +342,11 @@
     @pl.when(pl.program_id(0) == 0)
     def _():
         whole_gram(core_ref, mine_ref, other_ref, gram)
-        inverse_factor(gram, inverse, *scratch)
+        converged = inverse_factor_near_one(gram, inverse)
+
+        @pl.when(jnp.logical_not(converged))
+        def _():
+            inverse_factor(gram, inverse, *scratch)
 
     out_ref[...] = good_dot(inverse[...], basis_ref[0], 1, 0).T * scale
 
@@ -334,7 +367,7 @@
     )(place, core, mine, other, basis)
 
 
-def local(interactions, omega):
+def program(interactions, omega):
     user = lax.axis_index("user")
     z, core, x, y = lax.axis_index("item"), user % 2, user // 2 % side, user // (2 * side)
     a = jnp.where(core == 0, x, y)
@@ -346,12 +379,15 @@
     two, one = user_rows([(z + 2) % side, (z + 1) % side], interactions, omega)
     two, one = shift(two, "item", 2), shift(one, "item", 1)
     three, own = user_rows([(z + 3) % side, z], interactions, omega)
-    ys = from_ring(of_ring(own, one, shift(three, "item", 3), two), "item")
+    own = of_ring(own, one, shift(three, "item", 3), two)
+    one, three = shift(own, "item", 1), shift(own, "item", 3)
+    half = own.shape[0] // 2
+    two = [shift(one[:half], "item", 1), shift(three[half:], "item", 3)]
     place = lambda *d: jnp.stack([*((z - k) % side for k in d), core])
 
-    total = item_columns(place(0, 1, 3), ys[:3], interactions)
-    away = shift(item_columns(place(2), ys[3:], interactions, total, 0), "core")
-    kept = item_columns(place(2), ys[3:], interactions, total, 1)
+    total = item_columns(place(0, 1, 3), [own, one, three], interactions)
+    away = shift(item_columns(place(2), two, interactions, total, 0, 2), "core")
+    kept = item_columns(place(2), two, interactions, total, 1, 2)
 
     def block_at(k):
         return lax.dynamic_index_in_dim(kept, k, 0, False) + lax.dynamic_index_in_dim(away, k, 0, False)
@@ -377,4 +413,4 @@
 def solution(mesh):
     in_specs = (P("user", "item"), P("item", None))
     out_specs = P("item", None)
-    return jax.shard_map(local, mesh=mesh, in_specs=in_specs, out_specs=out_specs, check_vma=False)
+    return jax.shard_map(program, mesh=mesh, in_specs=in_specs, out_specs=out_specs, check_vma=False)

time: 238 us -> 216 us (0.908)
  starting transfers between devices: 56 us -> 41.7 us
  Pallas kernels: 101 us -> 91.4 us
  waiting for transfers between devices: 60.2 us -> 65.5 us
    ppermute x16, starting transfers between devices: 36.7 us -> 22.8 us  [shift(): return lax.ppermute(a, 'user', pairs_of(axis, step))]
    pallas_call x1, Pallas kernels: 19 us -> 11.9 us  [second_sweep(): pl.pallas_call(lambda *refs: second_kernel(scale, *refs), out_shape=jax.S...]
    pallas_call x2, Pallas kernels: 21.7 us -> 28.3 us  [user_rows(): pl.pallas_call(rows_kernel, out_shape=(jax.ShapeDtypeStruct((rank, span),...]
    pallas_call x3 -> x1, Pallas kernels: 9.12 us -> 3.02 us  [first_gram(): pl.pallas_call(pair_kernel, out_shape=jax.ShapeDtypeStruct((2, rank, rank...]
    ppermute x16, waiting for transfers between devices: 29.3 us -> 34.1 us  [shift(): return lax.ppermute(a, 'user', pairs_of(axis, step))]
    unnamed x33 -> x35, local copies, waits for them, and re-layouts: 6.88 us -> 5.27 us
    ppermute x12 -> x13, waiting for transfers between devices: 30.9 us -> 31.5 us  [shift(): lax.ppermute(a, 'item', [(i, (i + step) % side) for i in range(side)])]
    ppermute x12 -> x13, starting transfers between devices: 19.4 us -> 18.9 us  [shift(): lax.ppermute(a, 'item', [(i, (i + step) % side) for i in range(side)])]
  transfers between devices with their start and end apart: 28 -> 29, of which waited for: 18 -> 14; matrix products, arithmetic and copies ran while one was open for 1% -> 2% of each run, Pallas kernels for 17% -> 16%
where the time goes in v1:
time: 216 us; the launch traced here: 215 us
  Pallas kernels  91.4 us (42%)
  waiting for transfers between devices  65.5 us (30%)
  starting transfers between devices  41.7 us (19%)
  other arithmetic  10.2 us (5%)
  local copies, waits for them, and re-layouts  6.38 us (3%)
    ppermute x16, waiting for transfers between devices, shift(): return lax.ppermute(a, 'user', pairs_of(axis, step))  34.1 us
    ppermute x13, waiting for transfers between devices, shift(): lax.ppermute(a, 'item', [(i, (i + step) % side) for i in range(side)])  31.5 us
    pallas_call x2, Pallas kernels, user_rows(): pl.pallas_call(rows_kernel, out_shape=(jax.ShapeDtypeStruct((rank, span),...  28.3 us
    ppermute x16, starting transfers between devices, shift(): return lax.ppermute(a, 'user', pairs_of(axis, step))  22.8 us
    pallas_call x3, Pallas kernels, item_columns(): pl.pallas_call(lambda *refs: columns_kernel(count, splits, total is not N...  22.2 us
    pallas_call x1, Pallas kernels, first_sweep(): pl.pallas_call(first_kernel, out_shape=(jax.ShapeDtypeStruct((8, rank, wi...  20.7 us
    ppermute x13, starting transfers between devices, shift(): lax.ppermute(a, 'item', [(i, (i + step) % side) for i in range(side)])  18.9 us
    pallas_call x1, Pallas kernels, second_sweep(): pl.pallas_call(lambda *refs: second_kernel(scale, *refs), out_shape=jax.S...  11.9 us
  transfers between devices with their start and end apart: 29, of which 14 were waited for; matrix products, arithmetic and copies ran while one was open for 2% of the time, Pallas kernels for 16%

profile of v1, /device:TPU:1, one launch (start us, length us, event | category | flops | bytes accessed | tf_op | source)
XLA Modules:
  0.0 215.4 jit_solution(13279638763783759873)
XLA Ops:
  0.6 14.1 %user_rows.3 = (f32[256,512]{1,0:T(8,128)}, f32[256,512]{1,0:T(8,128)}) custom-call(s32[2]{0:T(128)} %get-tuple-element.23.place_ref, bf16[2048,4096]{1,0:T(8,128)(2,1)} %refs_3_.3, bf16[2048,4096]{1,0:T(8,128)(2,1)} %refs_3_.3, f32[4096,256]{1,0:T(8,128)} %omega_ref.3), custom_call_target="tpu_custom_call" | custom-call | tf_op jit(solution)/shard_map/user_rows/pallas_call | solution.py:87
  14.7 4.4 %collective-permute-start = (f32[256,512]{1,0:T(8,128)}, f32[256,512]{1,0:T(8,128)S(1)}, u32[]{:S(2)}, u32[]{:S(2)}) collective-permute-start(f32[256,512]{1,0:T(8,128)} %get-tuple-element.12), channel_id=1, source_target_pairs={{0,64},{32,96},{64,0},{96,32},{1,65},{33,97},{65,1},{97,33},{2,66}... | collective-permute-start | bytes 1572872 | tf_op jit(solution)/shard_map/ppermute | solution.py:53
  19.9 14.1 %user_rows.2 = (f32[256,512]{1,0:T(8,128)}, f32[256,512]{1,0:T(8,128)}) custom-call(s32[2]{0:T(128)} %get-tuple-element.22.place_ref, bf16[2048,4096]{1,0:T(8,128)(2,1)} %refs_3_.3, bf16[2048,4096]{1,0:T(8,128)(2,1)} %refs_3_.3, f32[4096,256]{1,0:T(8,128)} %omega_ref.3), custom_call_target="tpu_custom_call" | custom-call | tf_op jit(solution)/shard_map/user_rows/pallas_call | solution.py:87
  36.0 7.0 %collective-permute-done.1 = f32[256,512]{1,0:T(8,128)S(1)} collective-permute-done((f32[256,512]{1,0:T(8,128)}, f32[256,512]{1,0:T(8,128)S(1)}, u32[]{:S(2)}, u32[]{:S(2)}) %collective-permute-start.1) | collective-permute-done | bytes 524320 | tf_op jit(solution)/shard_map/ppermute | solution.py:53
  43.0 3.5 %collective-permute-done.2 = f32[256,512]{1,0:T(8,128)S(1)} collective-permute-done((f32[256,512]{1,0:T(8,128)}, f32[256,512]{1,0:T(8,128)S(1)}, u32[]{:S(2)}, u32[]{:S(2)}) %collective-permute-start.2) | collective-permute-done | bytes 524320 | tf_op jit(solution)/shard_map/ppermute | solution.py:53
  48.1 2.9 %collective-permute-start.5 = (f32[256,512]{1,0:T(8,128)S(1)}, f32[256,512]{1,0:T(8,128)S(1)}, u32[]{:S(2)}, u32[]{:S(2)}) collective-permute-start(f32[256,512]{1,0:T(8,128)S(1)} %add_add_fusion.refs_1_), channel_id=1, source_target_pairs={{0,96},{32,0},{64,32},{96,64},{1,97},{33,1},{65,33},{97,65},{2,98}... | collective-permute-start | bytes 1572872 | tf_op jit(solution)/shard_map/ppermute | solution.py:53
  51.1 10.1 %collective-permute-done.3.refs_2_ = f32[256,512]{1,0:T(8,128)S(1)} collective-permute-done((f32[256,512]{1,0:T(8,128)S(1)}, f32[256,512]{1,0:T(8,128)S(1)}, u32[]{:S(2)}, u32[]{:S(2)}) %collective-permute-start.3) | collective-permute-done | bytes 524320 | tf_op jit(solution)/shard_map/ppermute | solution.py:53
  65.4 12.4 %item_columns.3.refs_4_ = f32[8,256,512]{2,1,0:T(8,128)} custom-call(s32[4]{0:T(128)} %pad_add_fusion.4.refs_0_, f32[256,512]{1,0:T(8,128)} %copy-done.1, f32[256,512]{1,0:T(8,128)} %copy-done.7, f32[256,512]{1,0:T(8,128)} %copy-done.8, bf16[2048,4096]{1,0:T(8,128)(2,1)} %refs_3_.3, bf16[2048,4096]{1,0:T(8,128)(2,1)} %refs_3_.3, bf16[2048,4096]{1,0:T(8,128)(2,1)} %refs_3_.3), custom_call_target="tpu_custom_call" | custom-call | tf_op jit(solution)/shard_map/item_columns/pallas_call | solution.py:149
  79.2 4.9 %item_columns.5 = f32[4,256,512]{2,1,0:T(8,128)} custom-call(s32[2]{0:T(128)} %pad_add_fusion.1.refs_0_, f32[128,512]{1,0:T(8,128)} %copy-done.9, f32[128,512]{1,0:T(8,128)} %copy-done.10, bf16[2048,4096]{1,0:T(8,128)(2,1)} %refs_3_.3, f32[8,256,512]{2,1,0:T(8,128)} %item_columns.3.refs_4_), custom_call_target="tpu_custom_call" | custom-call | tf_op jit(solution)/shard_map/item_columns/pallas_call | solution.py:149
  84.1 3.2 %collective-permute-start.7 = (f32[4,256,512]{2,1,0:T(8,128)}, f32[4,256,512]{2,1,0:T(8,128)S(1)}, u32[]{:S(2)}, u32[]{:S(2)}) collective-permute-start(f32[4,256,512]{2,1,0:T(8,128)} %item_columns.5), channel_id=1, source_target_pairs={{0,1},{1,0},{2,3},{3,2},{4,5},{5,4},{6,7},{7,6},{8,9},{9,8},{10,11... | collective-permute-start | bytes 6291464 | tf_op jit(solution)/shard_map/ppermute | solution.py:54
  87.3 4.9 %item_columns.4 = f32[4,256,512]{2,1,0:T(8,128)} custom-call(s32[2]{0:T(128)} %pad_add_fusion.1.refs_0_, f32[128,512]{1,0:T(8,128)} %copy-done.9, f32[128,512]{1,0:T(8,128)} %copy-done.10, bf16[2048,4096]{1,0:T(8,128)(2,1)} %refs_3_.3, f32[8,256,512]{2,1,0:T(8,128)} %item_columns.3.refs_4_), custom_call_target="tpu_custom_call" | custom-call | tf_op jit(solution)/shard_map/item_columns/pallas_call | solution.py:149
  94.8 2.7 %collective-permute-start.10 = (f32[256,512]{1,0:T(8,128)}, f32[256,512]{1,0:T(8,128)S(1)}, u32[]{:S(2)}, u32[]{:S(2)}) collective-permute-start(f32[256,512]{1,0:T(8,128)} %get-tuple-element.17), channel_id=1, source_target_pairs={{0,6},{1,25},{2,0},{3,27},{4,2},{5,29},{6,4},{7,31},{8,14},{9,1},{... | collective-permute-start | bytes 1572872 | tf_op jit(solution)/shard_map/ppermute | solution.py:54
  98.6 11.0 %collective-permute-done.10 = f32[256,512]{1,0:T(8,128)S(1)} collective-permute-done((f32[256,512]{1,0:T(8,128)}, f32[256,512]{1,0:T(8,128)S(1)}, u32[]{:S(2)}, u32[]{:S(2)}) %collective-permute-start.10) | collective-permute-done | bytes 524320 | tf_op jit(solution)/shard_map/ppermute | solution.py:54
  110.4 2.9 %collective-permute-done.9 = f32[256,512]{1,0:T(8,128)} collective-permute-done((f32[256,512]{1,0:T(8,128)}, f32[256,512]{1,0:T(8,128)}, u32[]{:S(2)}, u32[]{:S(2)}) %collective-permute-start.9) | collective-permute-done | bytes 524320 | tf_op jit(solution)/shard_map/ppermute | solution.py:54
  121.5 3.5 %collective-permute-done.11 = f32[256,512]{1,0:T(8,128)S(1)} collective-permute-done((f32[256,512]{1,0:T(8,128)S(1)}, f32[256,512]{1,0:T(8,128)S(1)}, u32[]{:S(2)}, u32[]{:S(2)}) %collective-permute-start.11) | collective-permute-done | bytes 524320 | tf_op jit(solution)/shard_map/ppermute | solution.py:54
  124.9 5.6 %collective-permute-done.12 = f32[256,512]{1,0:T(8,128)S(1)} collective-permute-done((f32[256,512]{1,0:T(8,128)S(1)}, f32[256,512]{1,0:T(8,128)S(1)}, u32[]{:S(2)}, u32[]{:S(2)}) %collective-permute-start.12) | collective-permute-done | bytes 524320 | tf_op jit(solution)/shard_map/ppermute | solution.py:54
  136.2 9.8 %collective-permute-done.15.refs_0_.refs_1_ = f32[256,512]{1,0:T(8,128)S(1)} collective-permute-done((f32[256,512]{1,0:T(8,128)S(1)}, f32[256,512]{1,0:T(8,128)S(1)}, u32[]{:S(2)}, u32[]{:S(2)}) %collective-permute-start.15) | collective-permute-done | bytes 524320 | tf_op jit(solution)/shard_map/ppermute | solution.py:54
  146.0 3.0 %collective-permute-start.18 = (f32[256,512]{1,0:T(8,128)S(1)}, f32[256,512]{1,0:T(8,128)S(1)}, u32[]{:S(2)}, u32[]{:S(2)}) collective-permute-start(f32[256,512]{1,0:T(8,128)S(1)} %collective-permute-done.15.refs_0_.refs_1_), channel_id=1, source_target_pairs={{0,1},{1,0},{2,3},{3,2},{4,5},{5,4},{6,7},{7,6},{8,9},{9,8},{10,11... | collective-permute-start | bytes 1572872 | tf_op jit(solution)/shard_map/ppermute | solution.py:54
  150.3 3.0 %pair_gram.1.own_ref = f32[2,256,256]{2,1,0:T(8,128)} custom-call(f32[256,512]{1,0:T(8,128)} %copy-done, f32[256,512]{1,0:T(8,128)} %copy-done.2), custom_call_target="tpu_custom_call" | custom-call | tf_op jit(solution)/shard_map/pair_gram/pallas_call | solution.py:281
  154.2 5.3 %last_pair_grams.1 = f32[192,128]{1,0:T(8,128)} custom-call(s32[1]{0:T(128)} %bitcast.core_ref.refs_1_, f32[2,256,256]{2,1,0:T(8,128)} %pair_gram.1.own_ref, f32[256,512]{1,0:T(8,128)} %copy-done.3, f32[256,512]{1,0:T(8,128)} %copy-done.4, f32[256,512]{1,0:T(8,128)} %copy-done.5, f32[256,512]{1,0:T(8,128)} %copy-done.6, ...), custom_call_target="tpu_custom_call" | custom-call | tf_op jit(solution)/shard_map/last_pair_grams/pallas_call | solution.py:288
  162.2 3.2 %collective-permute-done.21 = f32[192,128]{1,0:T(8,128)S(1)} collective-permute-done((f32[192,128]{1,0:T(8,128)}, f32[192,128]{1,0:T(8,128)S(1)}, u32[]{:S(2)}, u32[]{:S(2)}) %collective-permute-start.21) | collective-permute-done | bytes 98336 | tf_op jit(solution)/shard_map/ppermute | solution.py:53
  171.1 20.7 %first_sweep.1 = (f32[8,256,512]{2,1,0:T(8,128)}, f32[192,128]{1,0:T(8,128)}) custom-call(s32[1]{0:T(128)} %bitcast.core_ref.refs_1_, f32[192,128]{1,0:T(8,128)} %copy-done.13, f32[192,128]{1,0:T(8,128)} %copy-done.15, f32[256,512]{1,0:T(8,128)} %copy-done, f32[256,512]{1,0:T(8,128)} %copy-done.3, f32[256,512]{1,0:T(8,128)} %copy-done.4, ...), custom_call_target="tpu_custom_call" | custom-call | tf_op jit(solution)/shard_map/first_sweep/pallas_call | solution.py:331
  197.6 2.8 %collective-permute-done.26 = f32[192,128]{1,0:T(8,128)S(1)} collective-permute-done((f32[192,128]{1,0:T(8,128)}, f32[192,128]{1,0:T(8,128)S(1)}, u32[]{:S(2)}, u32[]{:S(2)}) %collective-permute-start.26) | collective-permute-done | bytes 98336 | tf_op jit(solution)/shard_map/ppermute | solution.py:53
  203.5 11.9 %second_sweep.1 = f32[4096,256]{1,0:T(8,128)} custom-call(s32[8]{0:T(128)} %pad_add_fusion.refs_0_, s32[1]{0:T(128)} %bitcast.core_ref.refs_1_, f32[192,128]{1,0:T(8,128)} %copy-done.12, f32[192,128]{1,0:T(8,128)} %copy-done.14, f32[8,256,512]{2,1,0:T(8,128)} %get-tuple-element.16.refs_4_), custom_call_target="tpu_custom_call" | custom-call | tf_op jit(solution)/shard_map/second_sweep/pallas_call | solution.py:356
  (92 shorter events, 48.0 us)
Async XLA Ops:
  14.7 21.2 %collective-permute-start = (f32[256,512]{1,0:T(8,128)}, f32[256,512]{1,0:T(8,128)S(1)}, u32[]{:S(2)}, u32[]{:S(2)}) collective-permute-start(f32[256,512]{1,0:T(8,128)} %get-tuple-element.12), channel_id=1, source_target_pairs={{0,64},{32,96},{64,0},{96,32},{1,65},{33,97},{65,1},{97,33},{2,66}... | collective-permute-start | bytes 1572872 | tf_op jit(solution)/shard_map/ppermute | solution.py:53
  19.2 23.8 %collective-permute-start.1 = (f32[256,512]{1,0:T(8,128)}, f32[256,512]{1,0:T(8,128)S(1)}, u32[]{:S(2)}, u32[]{:S(2)}) collective-permute-start(f32[256,512]{1,0:T(8,128)} %get-tuple-element.13), channel_id=1, source_target_pairs={{0,32},{32,64},{64,96},{96,0},{1,33},{33,65},{65,97},{97,1},{2,34}... | collective-permute-start | bytes 1572872 | tf_op jit(solution)/shard_map/ppermute | solution.py:53
  34.0 12.5 %collective-permute-start.2 = (f32[256,512]{1,0:T(8,128)}, f32[256,512]{1,0:T(8,128)S(1)}, u32[]{:S(2)}, u32[]{:S(2)}) collective-permute-start(f32[256,512]{1,0:T(8,128)} %get-tuple-element.14), channel_id=1, source_target_pairs={{0,96},{32,0},{64,32},{96,64},{1,97},{33,1},{65,33},{97,65},{2,98}... | collective-permute-start | bytes 1572872 | tf_op jit(solution)/shard_map/ppermute | solution.py:53
  47.8 13.4 %collective-permute-start.3 = (f32[256,512]{1,0:T(8,128)S(1)}, f32[256,512]{1,0:T(8,128)S(1)}, u32[]{:S(2)}, u32[]{:S(2)}) collective-permute-start(f32[256,512]{1,0:T(8,128)S(1)} %add_add_fusion.refs_1_), channel_id=1, source_target_pairs={{0,32},{32,64},{64,96},{96,0},{1,33},{33,65},{65,97},{97,1},{2,34}... | collective-permute-start | bytes 1572872 | tf_op jit(solution)/shard_map/ppermute | solution.py:53
  48.1 13.2 %collective-permute-start.5 = (f32[256,512]{1,0:T(8,128)S(1)}, f32[256,512]{1,0:T(8,128)S(1)}, u32[]{:S(2)}, u32[]{:S(2)}) collective-permute-start(f32[256,512]{1,0:T(8,128)S(1)} %add_add_fusion.refs_1_), channel_id=1, source_target_pairs={{0,96},{32,0},{64,32},{96,64},{1,97},{33,1},{65,33},{97,65},{2,98}... | collective-permute-start | bytes 1572872 | tf_op jit(solution)/shard_map/ppermute | solution.py:53
  61.2 16.6 %collective-permute-start.4 = (f32[128,512]{1,0:T(8,128)S(1)}, f32[128,512]{1,0:T(8,128)S(1)}, u32[]{:S(2)}, u32[]{:S(2)}) collective-permute-start(f32[128,512]{1,0:T(8,128)S(1)} %slice.8), channel_id=1, source_target_pairs={{0,32},{32,64},{64,96},{96,0},{1,33},{33,65},{65,97},{97,1},{2,34}... | collective-permute-start | bytes 786440 | tf_op jit(solution)/shard_map/ppermute | solution.py:53
  61.4 16.4 %collective-permute-start.6 = (f32[128,512]{1,0:T(8,128)S(1)}, f32[128,512]{1,0:T(8,128)S(1)}, u32[]{:S(2)}, u32[]{:S(2)}) collective-permute-start(f32[128,512]{1,0:T(8,128)S(1)} %slice.9), channel_id=1, source_target_pairs={{0,96},{32,0},{64,32},{96,64},{1,97},{33,1},{65,33},{97,65},{2,98}... | collective-permute-start | bytes 786440 | tf_op jit(solution)/shard_map/ppermute | solution.py:53
  84.1 8.2 %collective-permute-start.7 = (f32[4,256,512]{2,1,0:T(8,128)}, f32[4,256,512]{2,1,0:T(8,128)S(1)}, u32[]{:S(2)}, u32[]{:S(2)}) collective-permute-start(f32[4,256,512]{2,1,0:T(8,128)} %item_columns.5), channel_id=1, source_target_pairs={{0,1},{1,0},{2,3},{3,2},{4,5},{5,4},{6,7},{7,6},{8,9},{9,8},{10,11... | collective-permute-start | bytes 6291464 | tf_op jit(solution)/shard_map/ppermute | solution.py:54
  94.8 14.8 %collective-permute-start.10 = (f32[256,512]{1,0:T(8,128)}, f32[256,512]{1,0:T(8,128)S(1)}, u32[]{:S(2)}, u32[]{:S(2)}) collective-permute-start(f32[256,512]{1,0:T(8,128)} %get-tuple-element.17), channel_id=1, source_target_pairs={{0,6},{1,25},{2,0},{3,27},{4,2},{5,29},{6,4},{7,31},{8,14},{9,1},{... | collective-permute-start | bytes 1572872 | tf_op jit(solution)/shard_map/ppermute | solution.py:54
  97.6 12.1 %collective-permute-start.8 = (f32[256,512]{1,0:T(8,128)}, f32[256,512]{1,0:T(8,128)S(1)}, u32[]{:S(2)}, u32[]{:S(2)}) collective-permute-start(f32[256,512]{1,0:T(8,128)} %get-tuple-element.19), channel_id=1, source_target_pairs={{0,4},{1,17},{2,6},{3,19},{4,0},{5,21},{6,2},{7,23},{8,12},{9,25},... | collective-permute-start | bytes 1572872 | tf_op jit(solution)/shard_map/ppermute | solution.py:54
  97.9 15.4 %collective-permute-start.9 = (f32[256,512]{1,0:T(8,128)}, f32[256,512]{1,0:T(8,128)}, u32[]{:S(2)}, u32[]{:S(2)}) collective-permute-start(f32[256,512]{1,0:T(8,128)} %get-tuple-element.18), channel_id=1, source_target_pairs={{0,2},{1,9},{2,4},{3,11},{4,6},{5,13},{6,0},{7,15},{8,10},{9,17},{... | collective-permute-start | bytes 1572872 | tf_op jit(solution)/shard_map/ppermute | solution.py:54
  115.0 10.0 %collective-permute-start.11 = (f32[256,512]{1,0:T(8,128)S(1)}, f32[256,512]{1,0:T(8,128)S(1)}, u32[]{:S(2)}, u32[]{:S(2)}) collective-permute-start(f32[256,512]{1,0:T(8,128)S(1)} %fusion), channel_id=1, source_target_pairs={{0,16},{1,5},{2,18},{3,7},{4,20},{5,1},{6,22},{7,3},{8,24},{9,13},... | collective-permute-start | bytes 1572872 | tf_op jit(solution)/shard_map/ppermute | solution.py:54
  117.5 13.0 %collective-permute-start.12 = (f32[256,512]{1,0:T(8,128)S(1)}, f32[256,512]{1,0:T(8,128)S(1)}, u32[]{:S(2)}, u32[]{:S(2)}) collective-permute-start(f32[256,512]{1,0:T(8,128)S(1)} %fusion), channel_id=1, source_target_pairs={{0,8},{1,3},{2,10},{3,5},{4,12},{5,7},{6,14},{7,1},{8,16},{9,11},{... | collective-permute-start | bytes 1572872 | tf_op jit(solution)/shard_map/ppermute | solution.py:54
  117.8 12.7 %collective-permute-start.13 = (f32[256,512]{1,0:T(8,128)S(1)}, f32[256,512]{1,0:T(8,128)S(1)}, u32[]{:S(2)}, u32[]{:S(2)}) collective-permute-start(f32[256,512]{1,0:T(8,128)S(1)} %fusion), channel_id=1, source_target_pairs={{0,24},{1,7},{2,26},{3,1},{4,28},{5,3},{6,30},{7,5},{8,0},{9,15},{... | collective-permute-start | bytes 1572872 | tf_op jit(solution)/shard_map/ppermute | solution.py:54
  130.8 15.2 %collective-permute-start.15 = (f32[256,512]{1,0:T(8,128)S(1)}, f32[256,512]{1,0:T(8,128)S(1)}, u32[]{:S(2)}, u32[]{:S(2)}) collective-permute-start(f32[256,512]{1,0:T(8,128)S(1)} %bitcast_add_fusion.near_ref.refs_0_), channel_id=1, source_target_pairs={{0,2},{1,9},{2,4},{3,11},{4,6},{5,13},{6,0},{7,15},{8,10},{9,17},{... | collective-permute-start | bytes 1572872 | tf_op jit(solution)/shard_map/ppermute | solution.py:54
  130.9 18.1 %collective-permute-start.16 = (f32[256,512]{1,0:T(8,128)S(1)}, f32[256,512]{1,0:T(8,128)S(1)}, u32[]{:S(2)}, u32[]{:S(2)}) collective-permute-start(f32[256,512]{1,0:T(8,128)S(1)} %bitcast_add_fusion.near_ref.refs_0_), channel_id=1, source_target_pairs={{0,6},{1,25},{2,0},{3,27},{4,2},{5,29},{6,4},{7,31},{8,14},{9,1},{... | collective-permute-start | bytes 1572872 | tf_op jit(solution)/shard_map/ppermute | solution.py:54
  133.5 15.6 %collective-permute-start.17 = (f32[256,512]{1,0:T(8,128)S(1)}, f32[256,512]{1,0:T(8,128)S(1)}, u32[]{:S(2)}, u32[]{:S(2)}) collective-permute-start(f32[256,512]{1,0:T(8,128)S(1)} %bitcast_add_fusion.near_ref.refs_0_), channel_id=1, source_target_pairs={{0,4},{1,17},{2,6},{3,19},{4,0},{5,21},{6,2},{7,23},{8,12},{9,25},... | collective-permute-start | bytes 1572872 | tf_op jit(solution)/shard_map/ppermute | solution.py:54
  133.6 16.0 %collective-permute-start.14 = (f32[256,512]{1,0:T(8,128)S(1)}, f32[256,512]{1,0:T(8,128)S(1)}, u32[]{:S(2)}, u32[]{:S(2)}) collective-permute-start(f32[256,512]{1,0:T(8,128)S(1)} %bitcast_add_fusion.near_ref.refs_0_), channel_id=1, source_target_pairs={{0,1},{1,0},{2,3},{3,2},{4,5},{5,4},{6,7},{7,6},{8,9},{9,8},{10,11... | collective-permute-start | bytes 1572872 | tf_op jit(solution)/shard_map/ppermute | solution.py:54
  146.0 7.3 %collective-permute-start.18 = (f32[256,512]{1,0:T(8,128)S(1)}, f32[256,512]{1,0:T(8,128)S(1)}, u32[]{:S(2)}, u32[]{:S(2)}) collective-permute-start(f32[256,512]{1,0:T(8,128)S(1)} %collective-permute-done.15.refs_0_.refs_1_), channel_id=1, source_target_pairs={{0,1},{1,0},{2,3},{3,2},{4,5},{5,4},{6,7},{7,6},{8,9},{9,8},{10,11... | collective-permute-start | bytes 1572872 | tf_op jit(solution)/shard_map/ppermute | solution.py:54
  159.5 5.9 %collective-permute-start.21 = (f32[192,128]{1,0:T(8,128)}, f32[192,128]{1,0:T(8,128)S(1)}, u32[]{:S(2)}, u32[]{:S(2)}) collective-permute-start(f32[192,128]{1,0:T(8,128)} %last_pair_grams.1), channel_id=1, source_target_pairs={{0,64},{32,96},{64,0},{96,32},{1,65},{33,97},{65,1},{97,33},{2,66}... | collective-permute-start | bytes 294920 | tf_op jit(solution)/shard_map/ppermute | solution.py:53
  159.5 8.0 %collective-permute-start.22 = (f32[192,128]{1,0:T(8,128)}, f32[192,128]{1,0:T(8,128)S(1)}, u32[]{:S(2)}, u32[]{:S(2)}) collective-permute-start(f32[192,128]{1,0:T(8,128)} %last_pair_grams.1), channel_id=1, source_target_pairs={{0,32},{32,64},{64,96},{96,0},{1,33},{33,65},{65,97},{97,1},{2,34}... | collective-permute-start | bytes 294920 | tf_op jit(solution)/shard_map/ppermute | solution.py:53
  160.3 7.1 %collective-permute-start.23 = (f32[192,128]{1,0:T(8,128)}, f32[192,128]{1,0:T(8,128)S(1)}, u32[]{:S(2)}, u32[]{:S(2)}) collective-permute-start(f32[192,128]{1,0:T(8,128)} %last_pair_grams.1), channel_id=1, source_target_pairs={{0,96},{32,0},{64,32},{96,64},{1,97},{33,1},{65,33},{97,65},{2,98}... | collective-permute-start | bytes 294920 | tf_op jit(solution)/shard_map/ppermute | solution.py:53
  192.2 8.2 %collective-permute-start.26 = (f32[192,128]{1,0:T(8,128)}, f32[192,128]{1,0:T(8,128)S(1)}, u32[]{:S(2)}, u32[]{:S(2)}) collective-permute-start(f32[192,128]{1,0:T(8,128)} %get-tuple-element.15), channel_id=1, source_target_pairs={{0,32},{32,64},{64,96},{96,0},{1,33},{33,65},{65,97},{97,1},{2,34}... | collective-permute-start | bytes 294920 | tf_op jit(solution)/shard_map/ppermute | solution.py:53
  193.1 7.3 %collective-permute-start.27 = (f32[192,128]{1,0:T(8,128)}, f32[192,128]{1,0:T(8,128)S(1)}, u32[]{:S(2)}, u32[]{:S(2)}) collective-permute-start(f32[192,128]{1,0:T(8,128)} %get-tuple-element.15), channel_id=1, source_target_pairs={{0,96},{32,0},{64,32},{96,64},{1,97},{33,1},{65,33},{97,65},{2,98}... | collective-permute-start | bytes 294920 | tf_op jit(solution)/shard_map/ppermute | solution.py:53
  (22 other events, 112.7 us)

commit v2 on v1

--- a/solution.py
+++ b/solution.py
@@ -59,27 +59,28 @@
 hbm = pl.BlockSpec(memory_space=pl.ANY)
 
 
-def rows_kernel(place_ref, a0, a1, omega_ref, out0, out1, sum0, sum1):
+def rows_kernel(place_ref, a0, a1, omega_ref, out0, out1, total):
     at, last = pl.program_id(0), pl.num_programs(0) - 1
+    span = a0.shape[0]
     high, low = slices(omega_ref[...])
-    for ref, total, out in ((a0, sum0, out0), (a1, sum1, out1)):
-        a = ref[...]
-        y = fast_dot(a, high) + fast_dot(a, low)
-
-        @pl.when(at == 0)
-        def _():
-            total[...] = y
-
-        @pl.when((at > 0) & (at < last))
-        def _():
-            total[...] += y
-
-        @pl.when(at == last)
-        def _():
-            out[...] = (total[...] + y).T
-
-
-def user_rows(places, a, omega, depth=1024):
+    a = jnp.concatenate([a0[...], a1[...]], axis=0)
+    y = fast_dot(a, high) + fast_dot(a, low)
+
+    @pl.when(at == 0)
+    def _():
+        total[...] = y
+
+    @pl.when((at > 0) & (at < last))
+    def _():
+        total[...] += y
+
+    @pl.when(at == last)
+    def _():
+        whole = total[...] + y
+        out0[...], out1[...] = whole[:span].T, whole[span:].T
+
+
+def user_rows(place, at, a, omega, depth=1024):
     users, items = a.shape
     rank = omega.shape[1]
     span = users // side
@@ -90,13 +91,13 @@
         grid_spec=pltpu.PrefetchScalarGridSpec(
             num_scalar_prefetch=1,
             grid=(items // depth,),
-            in_specs=[pl.BlockSpec((span, depth), lambda k, s, d=d: (s[d], k)) for d in range(2)]
+            in_specs=[pl.BlockSpec((span, depth), lambda k, s, d=d: (s[at + d], k)) for d in range(2)]
             + [pl.BlockSpec((depth, rank), lambda k, s: (k, 0))],
             out_specs=(out, out),
-            scratch_shapes=[pltpu.VMEM((span, rank), f32)] * 2,
+            scratch_shapes=[pltpu.VMEM((2 * span, rank), f32)],
         ),
         name="user_rows",
-    )(jnp.stack(places).astype(jnp.int32), a, a, omega)
+    )(place, a, a, omega)
 
 
 def columns_kernel(count, splits, adds, place_ref, *refs):
@@ -123,7 +124,7 @@
         z_ref[k] = part + refs[-3][k] if adds else part
 
 
-def item_columns(place, ys, a, total=None, only=None, splits=1, block=1024):
+def item_columns(place, start_at, ys, a, total=None, only=None, splits=1, block=1024):
     _, items = a.shape
     rows, span = ys[0].shape
     rank = rows * splits
@@ -136,12 +137,12 @@
 
     def of_items(i, s):
         at = i + start
-        core = s[count]
+        core = s[place.shape[0] - 1]
         return (at // in_half + 1 + core) % 2 * in_half + at % in_half
 
-    ins = [vmem] * len(ys)
+    ins = [pl.BlockSpec((rows, span), lambda i, s: (0, 0), pipeline_mode=pl.Buffered(1))] * len(ys)
     for d in range(count):
-        ins.append(pl.BlockSpec((span, block), lambda i, s, d=d: (s[d], of_items(i, s))))
+        ins.append(pl.BlockSpec((span, block), lambda i, s, d=d: (s[start_at + d], of_items(i, s))))
     args = [*ys, *[a] * count]
     if total is not None:
         ins.append(pl.BlockSpec((per, rank, width), lambda i, s: (i + start, 0, 0)))
@@ -304,7 +305,7 @@
     gram[h:, :h], gram[h:, h:] = below, two[:h]
 
 
-def first_kernel(core_ref, mine_ref, other_ref, *refs):
+def first_kernel(core_ref, slot_ref, mine_ref, other_ref, *refs):
     parts, (basis_ref, out_ref), (held, grams, sems, gram, inverse), scratch = refs[:8], refs[8:10], refs[10:15], refs[15:]
     copies = [pltpu.make_async_copy(ref, held.at[k], sems.at[k]) for k, ref in enumerate(parts)]
     for copy in copies:
@@ -316,29 +317,29 @@
 
     def sweep(k, carry):
         block = exact_dot(inverse[...], held[k], 1, 0)
-        basis_ref[k] = block
+        basis_ref[slot_ref[k]] = block
         grams[k] = good_dot(block, block, 1, 1)
         return carry
 
-    lax.fori_loop(0, 8, sweep, 0, unroll=2)
+    lax.fori_loop(0, 8, sweep, 0, unroll=4)
     halves = [of_ring(*(grams[h * 4 + k] for k in range(4))) for h in range(2)]
     out_ref[...] = mine_of(core_ref, halves[0] + halves[1])
 
 
-def first_sweep(core, mine, other, parts):
+def first_sweep(core, slots, mine, other, parts):
     rank, width = parts[0].shape
     scratch = [pltpu.VMEM((8, rank, width), f32), pltpu.VMEM((8, rank, rank), f32), pltpu.SemaphoreType.DMA((8,))]
     return pl.pallas_call(
         first_kernel,
         out_shape=(jax.ShapeDtypeStruct((8, rank, width), f32), packed(rank)),
-        in_specs=[smem, vmem, vmem] + [hbm] * 8,
+        in_specs=[smem, smem, vmem, vmem] + [hbm] * 8,
         out_specs=(vmem, vmem),
         scratch_shapes=scratch + [pltpu.VMEM((rank, rank), f32)] + factor_scratch(rank),
         name="first_sweep",
-    )(core, mine, other, *parts)
-
-
-def second_kernel(scale, place_ref, core_ref, mine_ref, other_ref, basis_ref, out_ref, gram, inverse, *scratch):
+    )(core, slots, mine, other, *parts)
+
+
+def second_kernel(scale, core_ref, mine_ref, other_ref, basis_ref, out_ref, gram, inverse, *scratch):
     @pl.when(pl.program_id(0) == 0)
     def _():
         whole_gram(core_ref, mine_ref, other_ref, gram)
@@ -348,23 +349,22 @@
         def _():
             inverse_factor(gram, inverse, *scratch)
 
-    out_ref[...] = good_dot(inverse[...], basis_ref[0], 1, 0).T * scale
-
-
-def second_sweep(place, core, mine, other, basis, scale):
+    width = basis_ref.shape[2]
+    for k in range(basis_ref.shape[0]):
+        out_ref[k * width : k * width + width] = good_dot(basis_ref[k], inverse[...], 0, 1) * scale
+
+
+def second_sweep(core, mine, other, basis, scale, per=2):
     count, rank, width = basis.shape
     return pl.pallas_call(
         lambda *refs: second_kernel(scale, *refs),
         out_shape=jax.ShapeDtypeStruct((count * width, rank), f32),
-        grid_spec=pltpu.PrefetchScalarGridSpec(
-            num_scalar_prefetch=1,
-            grid=(count,),
-            in_specs=[smem, vmem, vmem, pl.BlockSpec((1, rank, width), lambda i, s: (i, 0, 0))],
-            out_specs=pl.BlockSpec((width, rank), lambda i, s: (s[i], 0)),
-            scratch_shapes=[pltpu.VMEM((rank, rank), f32)] + factor_scratch(rank),
-        ),
+        grid=(count // per,),
+        in_specs=[smem, vmem, vmem, pl.BlockSpec((per, rank, width), lambda i: (i, 0, 0))],
+        out_specs=pl.BlockSpec((per * width, rank), lambda i: (i, 0)),
+        scratch_shapes=[pltpu.VMEM((rank, rank), f32)] + factor_scratch(rank),
         name="second_sweep",
-    )(place, core, mine, other, basis)
+    )(core, mine, other, basis)
 
 
 def program(interactions, omega):
@@ -376,18 +376,22 @@
     width = omega.shape[0] // 8
     from_ring = lambda v, axis: [v] + [shift(v, axis, d) for d in steps]
 
-    two, one = user_rows([(z + 2) % side, (z + 1) % side], interactions, omega)
+    place = jnp.stack([*((z + k) % side for k in (2, 1, 3, 0, 3, 1, 2)), core]).astype(jnp.int32)
+    offsets = jnp.asarray((0, *steps))
+    slots = jnp.concatenate([core * side + (a - offsets) % side, (1 - core) * side + (b - offsets) % side])
+
+    two, one = user_rows(place, 0, interactions, omega)
     two, one = shift(two, "item", 2), shift(one, "item", 1)
-    three, own = user_rows([(z + 3) % side, z], interactions, omega)
+    three, own = user_rows(place, 2, interactions, omega)
     own = of_ring(own, one, shift(three, "item", 3), two)
     one, three = shift(own, "item", 1), shift(own, "item", 3)
     half = own.shape[0] // 2
     two = [shift(one[:half], "item", 1), shift(three[half:], "item", 3)]
-    place = lambda *d: jnp.stack([*((z - k) % side for k in d), core])
-
-    total = item_columns(place(0, 1, 3), [own, one, three], interactions)
-    away = shift(item_columns(place(2), two, interactions, total, 0, 2), "core")
-    kept = item_columns(place(2), two, interactions, total, 1, 2)
+
+    total = item_columns(place, 3, [own], interactions)
+    total = item_columns(place, 4, [one, three], interactions, total)
+    away = shift(item_columns(place, 6, two, interactions, total, 0, 2), "core")
+    kept = item_columns(place, 6, two, interactions, total, 1, 2)
 
     def block_at(k):
         return lax.dynamic_index_in_dim(kept, k, 0, False) + lax.dynamic_index_in_dim(away, k, 0, False)
@@ -404,10 +408,8 @@
         mine = of_ring(*from_ring(mine, "item"))
         return mine, shift(mine, "core")
 
-    basis, gram = first_sweep(flag, *over_items(first_gram(flag, near, far)), [*near, *far])
-    offsets = jnp.asarray((0, *steps))
-    place = jnp.concatenate([core * side + (a - offsets) % side, (1 - core) * side + (b - offsets) % side])
-    return second_sweep(place.astype(jnp.int32), flag, *over_items(gram), basis, float(item_count) ** 0.5)
+    basis, gram = first_sweep(flag, slots.astype(jnp.int32), *over_items(first_gram(flag, near, far)), [*near, *far])
+    return second_sweep(flag, *over_items(gram), basis, float(item_count) ** 0.5)
 
 
 def solution(mesh):

time: 216 us -> 208 us (0.963)
  Pallas kernels: 91.4 us -> 84.2 us
    pallas_call x2, Pallas kernels: 28.3 us -> 19.7 us  [user_rows(): pl.pallas_call(rows_kernel, out_shape=(jax.ShapeDtypeStruct((rank, span),...]
    pallas_call x3 -> x4, Pallas kernels: 22.2 us -> 27.4 us  [item_columns(): pl.pallas_call(lambda *refs: columns_kernel(count, splits, total is not N...]
    pallas_call x1, Pallas kernels: 11.9 us -> 8.65 us  [second_sweep(): pl.pallas_call(lambda *refs: second_kernel(scale, *refs), out_shape=jax.S...]
  transfers between devices with their start and end apart: 29 -> 29, of which waited for: 14 -> 13; matrix products, arithmetic and copies ran while one was open for 2% -> 1% of each run, Pallas kernels for 16% -> 17%
where the time goes in v2:
time: 208 us
  Pallas kernels  84.2 us (40%)
  waiting for transfers between devices  66.7 us (32%)
  starting transfers between devices  41.2 us (20%)
  other arithmetic  8.23 us (4%)
  local copies, waits for them, and re-layouts  7.03 us (3%)
    ppermute x16, waiting for transfers between devices, shift(): return lax.ppermute(a, 'user', pairs_of(axis, step))  34.1 us
    ppermute x13, waiting for transfers between devices, shift(): lax.ppermute(a, 'item', [(i, (i + step) % side) for i in range(side)])  32.7 us
    pallas_call x4, Pallas kernels, item_columns(): pl.pallas_call(lambda *refs: columns_kernel(count, splits, total is not N...  27.4 us
    ppermute x16, starting transfers between devices, shift(): return lax.ppermute(a, 'user', pairs_of(axis, step))  22.9 us
    pallas_call x1, Pallas kernels, first_sweep(): pl.pallas_call(first_kernel, out_shape=(jax.ShapeDtypeStruct((8, rank, wi...  20.1 us
    pallas_call x2, Pallas kernels, user_rows(): pl.pallas_call(rows_kernel, out_shape=(jax.ShapeDtypeStruct((rank, span),...  19.7 us
    ppermute x13, starting transfers between devices, shift(): lax.ppermute(a, 'item', [(i, (i + step) % side) for i in range(side)])  18.3 us
    pallas_call x1, Pallas kernels, second_sweep(): pl.pallas_call(lambda *refs: second_kernel(scale, *refs), out_shape=jax.S...  8.65 us
  transfers between devices with their start and end apart: 29, of which 13 were waited for; matrix products, arithmetic and copies ran while one was open for 1% of the time, Pallas kernels for 17%

profile of v2, /device:TPU:1, one launch (start us, length us, event | category | flops | bytes accessed | tf_op | source)
XLA Modules:
  0.0 207.7 jit_solution(5584436643468226818)
XLA Ops:
  0.6 9.8 %user_rows.3 = (f32[256,512]{1,0:T(8,128)}, f32[256,512]{1,0:T(8,128)}) custom-call(s32[8]{0:T(128)} %stack.23.place_ref.refs_0_, bf16[2048,4096]{1,0:T(8,128)(2,1)} %refs_3_.5, bf16[2048,4096]{1,0:T(8,128)(2,1)} %refs_3_.5, f32[4096,256]{1,0:T(8,128)} %omega_ref.3), custom_call_target="tpu_custom_call" | custom-call | tf_op jit(solution)/shard_map/user_rows/pallas_call | solution.py:88
  10.4 4.4 %collective-permute-start = (f32[256,512]{1,0:T(8,128)}, f32[256,512]{1,0:T(8,128)S(1)}, u32[]{:S(2)}, u32[]{:S(2)}) collective-permute-start(f32[256,512]{1,0:T(8,128)} %get-tuple-element.12), channel_id=1, source_target_pairs={{0,64},{32,96},{64,0},{96,32},{1,65},{33,97},{65,1},{97,33},{2,66}... | collective-permute-start | bytes 1572872 | tf_op jit(solution)/shard_map/ppermute | solution.py:53
  15.6 9.8 %user_rows.2 = (f32[256,512]{1,0:T(8,128)}, f32[256,512]{1,0:T(8,128)}) custom-call(s32[8]{0:T(128)} %stack.23.place_ref.refs_0_, bf16[2048,4096]{1,0:T(8,128)(2,1)} %refs_3_.5, bf16[2048,4096]{1,0:T(8,128)(2,1)} %refs_3_.5, f32[4096,256]{1,0:T(8,128)} %omega_ref.3), custom_call_target="tpu_custom_call" | custom-call | tf_op jit(solution)/shard_map/user_rows/pallas_call | solution.py:88
  27.4 11.3 %collective-permute-done.1 = f32[256,512]{1,0:T(8,128)S(1)} collective-permute-done((f32[256,512]{1,0:T(8,128)}, f32[256,512]{1,0:T(8,128)S(1)}, u32[]{:S(2)}, u32[]{:S(2)}) %collective-permute-start.1) | collective-permute-done | bytes 524320 | tf_op jit(solution)/shard_map/ppermute | solution.py:53
  42.7 10.5 %collective-permute-done.3.refs_1_ = f32[256,512]{1,0:T(8,128)S(1)} collective-permute-done((f32[256,512]{1,0:T(8,128)S(1)}, f32[256,512]{1,0:T(8,128)S(1)}, u32[]{:S(2)}, u32[]{:S(2)}) %collective-permute-start.3) | collective-permute-done | bytes 524320 | tf_op jit(solution)/shard_map/ppermute | solution.py:53
  56.1 7.0 %item_columns.4.refs_5_ = f32[8,256,512]{2,1,0:T(8,128)} custom-call(s32[8]{0:T(128)} %stack.23.place_ref.refs_0_, f32[256,512]{1,0:T(8,128)} %copy-done.2, bf16[2048,4096]{1,0:T(8,128)(2,1)} %refs_3_.5), custom_call_target="tpu_custom_call" | custom-call | tf_op jit(solution)/shard_map/item_columns/pallas_call | solution.py:150
  63.1 10.7 %item_columns.5.refs_4_ = f32[8,256,512]{2,1,0:T(8,128)} custom-call(s32[8]{0:T(128)} %stack.23.place_ref.refs_0_, f32[256,512]{1,0:T(8,128)} %copy-done.7, f32[256,512]{1,0:T(8,128)} %copy-done.8, bf16[2048,4096]{1,0:T(8,128)(2,1)} %refs_3_.5, bf16[2048,4096]{1,0:T(8,128)(2,1)} %refs_3_.5, f32[8,256,512]{2,1,0:T(8,128)} %item_columns.4.refs_5_), custom_call_target="tpu_custom_call" | custom-call | tf_op jit(solution)/shard_map/item_columns/pallas_call | solution.py:150
  75.1 4.9 %item_columns.7 = f32[4,256,512]{2,1,0:T(8,128)} custom-call(s32[8]{0:T(128)} %stack.23.place_ref.refs_0_, f32[128,512]{1,0:T(8,128)} %copy-done.9, f32[128,512]{1,0:T(8,128)} %copy-done.10, bf16[2048,4096]{1,0:T(8,128)(2,1)} %refs_3_.5, f32[8,256,512]{2,1,0:T(8,128)} %item_columns.5.refs_4_), custom_call_target="tpu_custom_call" | custom-call | tf_op jit(solution)/shard_map/item_columns/pallas_call | solution.py:150
  80.0 2.9 %collective-permute-start.7 = (f32[4,256,512]{2,1,0:T(8,128)}, f32[4,256,512]{2,1,0:T(8,128)S(1)}, u32[]{:S(2)}, u32[]{:S(2)}) collective-permute-start(f32[4,256,512]{2,1,0:T(8,128)} %item_columns.7), channel_id=1, source_target_pairs={{0,1},{1,0},{2,3},{3,2},{4,5},{5,4},{6,7},{7,6},{8,9},{9,8},{10,11... | collective-permute-start | bytes 6291464 | tf_op jit(solution)/shard_map/ppermute | solution.py:54
  82.9 4.9 %item_columns.6 = f32[4,256,512]{2,1,0:T(8,128)} custom-call(s32[8]{0:T(128)} %stack.23.place_ref.refs_0_, f32[128,512]{1,0:T(8,128)} %copy-done.9, f32[128,512]{1,0:T(8,128)} %copy-done.10, bf16[2048,4096]{1,0:T(8,128)(2,1)} %refs_3_.5, f32[8,256,512]{2,1,0:T(8,128)} %item_columns.5.refs_4_), custom_call_target="tpu_custom_call" | custom-call | tf_op jit(solution)/shard_map/item_columns/pallas_call | solution.py:150
  90.5 2.7 %collective-permute-start.10 = (f32[256,512]{1,0:T(8,128)}, f32[256,512]{1,0:T(8,128)S(1)}, u32[]{:S(2)}, u32[]{:S(2)}) collective-permute-start(f32[256,512]{1,0:T(8,128)} %get-tuple-element.17), channel_id=1, source_target_pairs={{0,6},{1,25},{2,0},{3,27},{4,2},{5,29},{6,4},{7,31},{8,14},{9,1},{... | collective-permute-start | bytes 1572872 | tf_op jit(solution)/shard_map/ppermute | solution.py:54
  94.3 11.0 %collective-permute-done.10 = f32[256,512]{1,0:T(8,128)S(1)} collective-permute-done((f32[256,512]{1,0:T(8,128)}, f32[256,512]{1,0:T(8,128)S(1)}, u32[]{:S(2)}, u32[]{:S(2)}) %collective-permute-start.10) | collective-permute-done | bytes 524320 | tf_op jit(solution)/shard_map/ppermute | solution.py:54
  106.1 2.9 %collective-permute-done.9 = f32[256,512]{1,0:T(8,128)} collective-permute-done((f32[256,512]{1,0:T(8,128)}, f32[256,512]{1,0:T(8,128)}, u32[]{:S(2)}, u32[]{:S(2)}) %collective-permute-start.9) | collective-permute-done | bytes 524320 | tf_op jit(solution)/shard_map/ppermute | solution.py:54
  117.1 3.5 %collective-permute-done.11 = f32[256,512]{1,0:T(8,128)S(1)} collective-permute-done((f32[256,512]{1,0:T(8,128)S(1)}, f32[256,512]{1,0:T(8,128)S(1)}, u32[]{:S(2)}, u32[]{:S(2)}) %collective-permute-start.11) | collective-permute-done | bytes 524320 | tf_op jit(solution)/shard_map/ppermute | solution.py:54
  120.6 5.6 %collective-permute-done.12 = f32[256,512]{1,0:T(8,128)S(1)} collective-permute-done((f32[256,512]{1,0:T(8,128)S(1)}, f32[256,512]{1,0:T(8,128)S(1)}, u32[]{:S(2)}, u32[]{:S(2)}) %collective-permute-start.12) | collective-permute-done | bytes 524320 | tf_op jit(solution)/shard_map/ppermute | solution.py:54
  132.1 9.8 %collective-permute-done.15.refs_0_.refs_1_ = f32[256,512]{1,0:T(8,128)S(1)} collective-permute-done((f32[256,512]{1,0:T(8,128)S(1)}, f32[256,512]{1,0:T(8,128)S(1)}, u32[]{:S(2)}, u32[]{:S(2)}) %collective-permute-start.15) | collective-permute-done | bytes 524320 | tf_op jit(solution)/shard_map/ppermute | solution.py:54
  141.9 3.0 %collective-permute-start.18 = (f32[256,512]{1,0:T(8,128)S(1)}, f32[256,512]{1,0:T(8,128)S(1)}, u32[]{:S(2)}, u32[]{:S(2)}) collective-permute-start(f32[256,512]{1,0:T(8,128)S(1)} %collective-permute-done.15.refs_0_.refs_1_), channel_id=1, source_target_pairs={{0,1},{1,0},{2,3},{3,2},{4,5},{5,4},{6,7},{7,6},{8,9},{9,8},{10,11... | collective-permute-start | bytes 1572872 | tf_op jit(solution)/shard_map/ppermute | solution.py:54
  146.2 3.0 %pair_gram.1.own_ref = f32[2,256,256]{2,1,0:T(8,128)} custom-call(f32[256,512]{1,0:T(8,128)} %copy-done, f32[256,512]{1,0:T(8,128)} %copy-done.1), custom_call_target="tpu_custom_call" | custom-call | tf_op jit(solution)/shard_map/pair_gram/pallas_call | solution.py:282
  150.1 5.3 %last_pair_grams.1 = f32[192,128]{1,0:T(8,128)} custom-call(s32[1]{0:T(128)} %bitcast.core_ref.refs_0_, f32[2,256,256]{2,1,0:T(8,128)} %pair_gram.1.own_ref, f32[256,512]{1,0:T(8,128)} %copy-done.3, f32[256,512]{1,0:T(8,128)} %copy-done.4, f32[256,512]{1,0:T(8,128)} %copy-done.5, f32[256,512]{1,0:T(8,128)} %copy-done.6, ...), custom_call_target="tpu_custom_call" | custom-call | tf_op jit(solution)/shard_map/last_pair_grams/pallas_call | solution.py:289
  158.1 3.2 %collective-permute-done.21 = f32[192,128]{1,0:T(8,128)S(1)} collective-permute-done((f32[192,128]{1,0:T(8,128)}, f32[192,128]{1,0:T(8,128)S(1)}, u32[]{:S(2)}, u32[]{:S(2)}) %collective-permute-start.21) | collective-permute-done | bytes 98336 | tf_op jit(solution)/shard_map/ppermute | solution.py:53
  166.9 20.1 %first_sweep.1 = (f32[8,256,512]{2,1,0:T(8,128)}, f32[192,128]{1,0:T(8,128)}) custom-call(s32[1]{0:T(128)} %bitcast.core_ref.refs_0_, s32[8]{0:T(128)} %pad_add_fusion.slot_ref, f32[192,128]{1,0:T(8,128)} %copy-done.13, f32[192,128]{1,0:T(8,128)} %copy-done.15, f32[256,512]{1,0:T(8,128)} %copy-done, f32[256,512]{1,0:T(8,128)} %copy-done.3, ...), custom_call_target="tpu_custom_call" | custom-call | tf_op jit(solution)/shard_map/first_sweep/pallas_call | solution.py:332
  190.1 2.8 %collective-permute-done.25 = f32[192,128]{1,0:T(8,128)S(1)} collective-permute-done((f32[192,128]{1,0:T(8,128)}, f32[192,128]{1,0:T(8,128)S(1)}, u32[]{:S(2)}, u32[]{:S(2)}) %collective-permute-start.25) | collective-permute-done | bytes 98336 | tf_op jit(solution)/shard_map/ppermute | solution.py:53
  192.9 2.8 %collective-permute-done.26 = f32[192,128]{1,0:T(8,128)S(1)} collective-permute-done((f32[192,128]{1,0:T(8,128)}, f32[192,128]{1,0:T(8,128)S(1)}, u32[]{:S(2)}, u32[]{:S(2)}) %collective-permute-start.26) | collective-permute-done | bytes 98336 | tf_op jit(solution)/shard_map/ppermute | solution.py:53
  199.1 8.7 %second_sweep.1 = f32[4096,256]{1,0:T(8,128)} custom-call(s32[1]{0:T(128)} %bitcast.core_ref.refs_0_, f32[192,128]{1,0:T(8,128)} %copy-done.12, f32[192,128]{1,0:T(8,128)} %copy-done.14, f32[8,256,512]{2,1,0:T(8,128)} %get-tuple-element.16.refs_3_), custom_call_target="tpu_custom_call" | custom-call | tf_op jit(solution)/shard_map/second_sweep/pallas_call | solution.py:359
  (91 shorter events, 46.9 us)
Async XLA Ops:
  10.4 16.9 %collective-permute-start = (f32[256,512]{1,0:T(8,128)}, f32[256,512]{1,0:T(8,128)S(1)}, u32[]{:S(2)}, u32[]{:S(2)}) collective-permute-start(f32[256,512]{1,0:T(8,128)} %get-tuple-element.12), channel_id=1, source_target_pairs={{0,64},{32,96},{64,0},{96,32},{1,65},{33,97},{65,1},{97,33},{2,66}... | collective-permute-start | bytes 1572872 | tf_op jit(solution)/shard_map/ppermute | solution.py:53
  14.8 23.8 %collective-permute-start.1 = (f32[256,512]{1,0:T(8,128)}, f32[256,512]{1,0:T(8,128)S(1)}, u32[]{:S(2)}, u32[]{:S(2)}) collective-permute-start(f32[256,512]{1,0:T(8,128)} %get-tuple-element.13), channel_id=1, source_target_pairs={{0,32},{32,64},{64,96},{96,0},{1,33},{33,65},{65,97},{97,1},{2,34}... | collective-permute-start | bytes 1572872 | tf_op jit(solution)/shard_map/ppermute | solution.py:53
  25.4 13.2 %collective-permute-start.2 = (f32[256,512]{1,0:T(8,128)}, f32[256,512]{1,0:T(8,128)S(1)}, u32[]{:S(2)}, u32[]{:S(2)}) collective-permute-start(f32[256,512]{1,0:T(8,128)} %get-tuple-element.14), channel_id=1, source_target_pairs={{0,96},{32,0},{64,32},{96,64},{1,97},{33,1},{65,33},{97,65},{2,98}... | collective-permute-start | bytes 1572872 | tf_op jit(solution)/shard_map/ppermute | solution.py:53
  39.9 13.3 %collective-permute-start.3 = (f32[256,512]{1,0:T(8,128)S(1)}, f32[256,512]{1,0:T(8,128)S(1)}, u32[]{:S(2)}, u32[]{:S(2)}) collective-permute-start(f32[256,512]{1,0:T(8,128)S(1)} %add_add_fusion.refs_1_), channel_id=1, source_target_pairs={{0,32},{32,64},{64,96},{96,0},{1,33},{33,65},{65,97},{97,1},{2,34}... | collective-permute-start | bytes 1572872 | tf_op jit(solution)/shard_map/ppermute | solution.py:53
  40.5 12.8 %collective-permute-start.5 = (f32[256,512]{1,0:T(8,128)S(1)}, f32[256,512]{1,0:T(8,128)S(1)}, u32[]{:S(2)}, u32[]{:S(2)}) collective-permute-start(f32[256,512]{1,0:T(8,128)S(1)} %add_add_fusion.refs_1_), channel_id=1, source_target_pairs={{0,96},{32,0},{64,32},{96,64},{1,97},{33,1},{65,33},{97,65},{2,98}... | collective-permute-start | bytes 1572872 | tf_op jit(solution)/shard_map/ppermute | solution.py:53
  53.2 20.5 %collective-permute-start.4 = (f32[128,512]{1,0:T(8,128)S(1)}, f32[128,512]{1,0:T(8,128)S(1)}, u32[]{:S(2)}, u32[]{:S(2)}) collective-permute-start(f32[128,512]{1,0:T(8,128)S(1)} %slice.8), channel_id=1, source_target_pairs={{0,32},{32,64},{64,96},{96,0},{1,33},{33,65},{65,97},{97,1},{2,34}... | collective-permute-start | bytes 786440 | tf_op jit(solution)/shard_map/ppermute | solution.py:53
  53.4 20.4 %collective-permute-start.6 = (f32[128,512]{1,0:T(8,128)S(1)}, f32[128,512]{1,0:T(8,128)S(1)}, u32[]{:S(2)}, u32[]{:S(2)}) collective-permute-start(f32[128,512]{1,0:T(8,128)S(1)} %slice.9), channel_id=1, source_target_pairs={{0,96},{32,0},{64,32},{96,64},{1,97},{33,1},{65,33},{97,65},{2,98}... | collective-permute-start | bytes 786440 | tf_op jit(solution)/shard_map/ppermute | solution.py:53
  80.0 7.8 %collective-permute-start.7 = (f32[4,256,512]{2,1,0:T(8,128)}, f32[4,256,512]{2,1,0:T(8,128)S(1)}, u32[]{:S(2)}, u32[]{:S(2)}) collective-permute-start(f32[4,256,512]{2,1,0:T(8,128)} %item_columns.7), channel_id=1, source_target_pairs={{0,1},{1,0},{2,3},{3,2},{4,5},{5,4},{6,7},{7,6},{8,9},{9,8},{10,11... | collective-permute-start | bytes 6291464 | tf_op jit(solution)/shard_map/ppermute | solution.py:54
  90.5 14.8 %collective-permute-start.10 = (f32[256,512]{1,0:T(8,128)}, f32[256,512]{1,0:T(8,128)S(1)}, u32[]{:S(2)}, u32[]{:S(2)}) collective-permute-start(f32[256,512]{1,0:T(8,128)} %get-tuple-element.17), channel_id=1, source_target_pairs={{0,6},{1,25},{2,0},{3,27},{4,2},{5,29},{6,4},{7,31},{8,14},{9,1},{... | collective-permute-start | bytes 1572872 | tf_op jit(solution)/shard_map/ppermute | solution.py:54
  93.2 12.1 %collective-permute-start.8 = (f32[256,512]{1,0:T(8,128)}, f32[256,512]{1,0:T(8,128)S(1)}, u32[]{:S(2)}, u32[]{:S(2)}) collective-permute-start(f32[256,512]{1,0:T(8,128)} %get-tuple-element.19), channel_id=1, source_target_pairs={{0,4},{1,17},{2,6},{3,19},{4,0},{5,21},{6,2},{7,23},{8,12},{9,25},... | collective-permute-start | bytes 1572872 | tf_op jit(solution)/shard_map/ppermute | solution.py:54
  93.6 15.4 %collective-permute-start.9 = (f32[256,512]{1,0:T(8,128)}, f32[256,512]{1,0:T(8,128)}, u32[]{:S(2)}, u32[]{:S(2)}) collective-permute-start(f32[256,512]{1,0:T(8,128)} %get-tuple-element.18), channel_id=1, source_target_pairs={{0,2},{1,9},{2,4},{3,11},{4,6},{5,13},{6,0},{7,15},{8,10},{9,17},{... | collective-permute-start | bytes 1572872 | tf_op jit(solution)/shard_map/ppermute | solution.py:54
  110.6 10.0 %collective-permute-start.11 = (f32[256,512]{1,0:T(8,128)S(1)}, f32[256,512]{1,0:T(8,128)S(1)}, u32[]{:S(2)}, u32[]{:S(2)}) collective-permute-start(f32[256,512]{1,0:T(8,128)S(1)} %fusion), channel_id=1, source_target_pairs={{0,16},{1,5},{2,18},{3,7},{4,20},{5,1},{6,22},{7,3},{8,24},{9,13},... | collective-permute-start | bytes 1572872 | tf_op jit(solution)/shard_map/ppermute | solution.py:54
  113.2 13.0 %collective-permute-start.12 = (f32[256,512]{1,0:T(8,128)S(1)}, f32[256,512]{1,0:T(8,128)S(1)}, u32[]{:S(2)}, u32[]{:S(2)}) collective-permute-start(f32[256,512]{1,0:T(8,128)S(1)} %fusion), channel_id=1, source_target_pairs={{0,8},{1,3},{2,10},{3,5},{4,12},{5,7},{6,14},{7,1},{8,16},{9,11},{... | collective-permute-start | bytes 1572872 | tf_op jit(solution)/shard_map/ppermute | solution.py:54
  113.5 12.7 %collective-permute-start.13 = (f32[256,512]{1,0:T(8,128)S(1)}, f32[256,512]{1,0:T(8,128)S(1)}, u32[]{:S(2)}, u32[]{:S(2)}) collective-permute-start(f32[256,512]{1,0:T(8,128)S(1)} %fusion), channel_id=1, source_target_pairs={{0,24},{1,7},{2,26},{3,1},{4,28},{5,3},{6,30},{7,5},{8,0},{9,15},{... | collective-permute-start | bytes 1572872 | tf_op jit(solution)/shard_map/ppermute | solution.py:54
  126.5 15.4 %collective-permute-start.15 = (f32[256,512]{1,0:T(8,128)S(1)}, f32[256,512]{1,0:T(8,128)S(1)}, u32[]{:S(2)}, u32[]{:S(2)}) collective-permute-start(f32[256,512]{1,0:T(8,128)S(1)} %bitcast_add_fusion.near_ref.refs_0_), channel_id=1, source_target_pairs={{0,2},{1,9},{2,4},{3,11},{4,6},{5,13},{6,0},{7,15},{8,10},{9,17},{... | collective-permute-start | bytes 1572872 | tf_op jit(solution)/shard_map/ppermute | solution.py:54
  126.7 18.1 %collective-permute-start.16 = (f32[256,512]{1,0:T(8,128)S(1)}, f32[256,512]{1,0:T(8,128)S(1)}, u32[]{:S(2)}, u32[]{:S(2)}) collective-permute-start(f32[256,512]{1,0:T(8,128)S(1)} %bitcast_add_fusion.near_ref.refs_0_), channel_id=1, source_target_pairs={{0,6},{1,25},{2,0},{3,27},{4,2},{5,29},{6,4},{7,31},{8,14},{9,1},{... | collective-permute-start | bytes 1572872 | tf_op jit(solution)/shard_map/ppermute | solution.py:54
  129.4 15.6 %collective-permute-start.17 = (f32[256,512]{1,0:T(8,128)S(1)}, f32[256,512]{1,0:T(8,128)S(1)}, u32[]{:S(2)}, u32[]{:S(2)}) collective-permute-start(f32[256,512]{1,0:T(8,128)S(1)} %bitcast_add_fusion.near_ref.refs_0_), channel_id=1, source_target_pairs={{0,4},{1,17},{2,6},{3,19},{4,0},{5,21},{6,2},{7,23},{8,12},{9,25},... | collective-permute-start | bytes 1572872 | tf_op jit(solution)/shard_map/ppermute | solution.py:54
  129.4 16.0 %collective-permute-start.14 = (f32[256,512]{1,0:T(8,128)S(1)}, f32[256,512]{1,0:T(8,128)S(1)}, u32[]{:S(2)}, u32[]{:S(2)}) collective-permute-start(f32[256,512]{1,0:T(8,128)S(1)} %bitcast_add_fusion.near_ref.refs_0_), channel_id=1, source_target_pairs={{0,1},{1,0},{2,3},{3,2},{4,5},{5,4},{6,7},{7,6},{8,9},{9,8},{10,11... | collective-permute-start | bytes 1572872 | tf_op jit(solution)/shard_map/ppermute | solution.py:54
  141.9 7.3 %collective-permute-start.18 = (f32[256,512]{1,0:T(8,128)S(1)}, f32[256,512]{1,0:T(8,128)S(1)}, u32[]{:S(2)}, u32[]{:S(2)}) collective-permute-start(f32[256,512]{1,0:T(8,128)S(1)} %collective-permute-done.15.refs_0_.refs_1_), channel_id=1, source_target_pairs={{0,1},{1,0},{2,3},{3,2},{4,5},{5,4},{6,7},{7,6},{8,9},{9,8},{10,11... | collective-permute-start | bytes 1572872 | tf_op jit(solution)/shard_map/ppermute | solution.py:54
  155.4 5.9 %collective-permute-start.21 = (f32[192,128]{1,0:T(8,128)}, f32[192,128]{1,0:T(8,128)S(1)}, u32[]{:S(2)}, u32[]{:S(2)}) collective-permute-start(f32[192,128]{1,0:T(8,128)} %last_pair_grams.1), channel_id=1, source_target_pairs={{0,64},{32,96},{64,0},{96,32},{1,65},{33,97},{65,1},{97,33},{2,66}... | collective-permute-start | bytes 294920 | tf_op jit(solution)/shard_map/ppermute | solution.py:53
  155.4 8.0 %collective-permute-start.22 = (f32[192,128]{1,0:T(8,128)}, f32[192,128]{1,0:T(8,128)S(1)}, u32[]{:S(2)}, u32[]{:S(2)}) collective-permute-start(f32[192,128]{1,0:T(8,128)} %last_pair_grams.1), channel_id=1, source_target_pairs={{0,32},{32,64},{64,96},{96,0},{1,33},{33,65},{65,97},{97,1},{2,34}... | collective-permute-start | bytes 294920 | tf_op jit(solution)/shard_map/ppermute | solution.py:53
  155.9 7.4 %collective-permute-start.23 = (f32[192,128]{1,0:T(8,128)}, f32[192,128]{1,0:T(8,128)S(1)}, u32[]{:S(2)}, u32[]{:S(2)}) collective-permute-start(f32[192,128]{1,0:T(8,128)} %last_pair_grams.1), channel_id=1, source_target_pairs={{0,96},{32,0},{64,32},{96,64},{1,97},{33,1},{65,33},{97,65},{2,98}... | collective-permute-start | bytes 294920 | tf_op jit(solution)/shard_map/ppermute | solution.py:53
  187.5 8.2 %collective-permute-start.26 = (f32[192,128]{1,0:T(8,128)}, f32[192,128]{1,0:T(8,128)S(1)}, u32[]{:S(2)}, u32[]{:S(2)}) collective-permute-start(f32[192,128]{1,0:T(8,128)} %get-tuple-element.15), channel_id=1, source_target_pairs={{0,32},{32,64},{64,96},{96,0},{1,33},{33,65},{65,97},{97,1},{2,34}... | collective-permute-start | bytes 294920 | tf_op jit(solution)/shard_map/ppermute | solution.py:53
  188.4 7.3 %collective-permute-start.27 = (f32[192,128]{1,0:T(8,128)}, f32[192,128]{1,0:T(8,128)S(1)}, u32[]{:S(2)}, u32[]{:S(2)}) collective-permute-start(f32[192,128]{1,0:T(8,128)} %get-tuple-element.15), channel_id=1, source_target_pairs={{0,96},{32,0},{64,32},{96,64},{1,97},{33,1},{65,33},{97,65},{2,98}... | collective-permute-start | bytes 294920 | tf_op jit(solution)/shard_map/ppermute | solution.py:53
  (22 other events, 138.9 us)

commit v3 on v2

--- a/solution.py
+++ b/solution.py
@@ -59,11 +59,12 @@
 hbm = pl.BlockSpec(memory_space=pl.ANY)
 
 
-def rows_kernel(place_ref, a0, a1, omega_ref, out0, out1, total):
+def rows_kernel(count, place_ref, *refs):
+    quarters, omega_ref, outs, total = refs[:count], refs[count], refs[count + 1 : -1], refs[-1]
     at, last = pl.program_id(0), pl.num_programs(0) - 1
-    span = a0.shape[0]
+    span = quarters[0].shape[0]
     high, low = slices(omega_ref[...])
-    a = jnp.concatenate([a0[...], a1[...]], axis=0)
+    a = jnp.concatenate([ref[...] for ref in quarters], axis=0)
     y = fast_dot(a, high) + fast_dot(a, low)
 
     @pl.when(at == 0)
@@ -77,27 +78,27 @@
     @pl.when(at == last)
     def _():
         whole = total[...] + y
-        out0[...], out1[...] = whole[:span].T, whole[span:].T
-
-
-def user_rows(place, at, a, omega, depth=1024):
+        for d, out in enumerate(outs):
+            out[...] = whole[d * span : d * span + span].T
+
+
+def user_rows(place, at, count, a, omega, depth=1024):
     users, items = a.shape
     rank = omega.shape[1]
     span = users // side
-    out = pl.BlockSpec((rank, span), lambda k, s: (0, 0))
-    return pl.pallas_call(
-        rows_kernel,
-        out_shape=(jax.ShapeDtypeStruct((rank, span), f32),) * 2,
+    return pl.pallas_call(
+        lambda *refs: rows_kernel(count, *refs),
+        out_shape=(jax.ShapeDtypeStruct((rank, span), f32),) * count,
         grid_spec=pltpu.PrefetchScalarGridSpec(
             num_scalar_prefetch=1,
             grid=(items // depth,),
-            in_specs=[pl.BlockSpec((span, depth), lambda k, s, d=d: (s[at + d], k)) for d in range(2)]
+            in_specs=[pl.BlockSpec((span, depth), lambda k, s, d=d: (s[at + d], k)) for d in range(count)]
             + [pl.BlockSpec((depth, rank), lambda k, s: (k, 0))],
-            out_specs=(out, out),
-            scratch_shapes=[pltpu.VMEM((2 * span, rank), f32)],
+            out_specs=(pl.BlockSpec((rank, span), lambda k, s: (0, 0)),) * count,
+            scratch_shapes=[pltpu.VMEM((count * span, rank), f32)],
         ),
         name="user_rows",
-    )(place, a, a, omega)
+    )(place, *[a] * count, omega)
 
 
 def columns_kernel(count, splits, adds, place_ref, *refs):
@@ -261,38 +262,43 @@
     return jax.ShapeDtypeStruct((rank // 2 + rank // 4, rank // 2), f32)
 
 
-def pair_kernel(near_ref, far_ref, out_ref):
-    for k, ref in enumerate((near_ref, far_ref)):
+def grams_kernel(*refs):
+    for k, ref in enumerate(refs[:-1]):
         part = ref[...]
-        out_ref[k] = exact_dot(part, part, 1, 1)
-
-
-def last_pairs_kernel(core_ref, own_ref, *refs):
-    near, far, out_ref = refs[:3], refs[3:6], refs[6]
+        refs[-1][k] = exact_dot(part, part, 1, 1)
+
+
+def grams_of(*parts):
+    rank = parts[0].shape[0]
+    return pl.pallas_call(
+        grams_kernel,
+        out_shape=jax.ShapeDtypeStruct((len(parts), rank, rank), f32),
+        in_specs=[vmem] * len(parts),
+        out_specs=vmem,
+        name="part_grams",
+    )(*parts)
+
+
+def last_grams_kernel(core_ref, own_ref, side_ref, *refs):
     total = None
-    for k, parts in enumerate((near, far)):
-        grams = [exact_dot(ref[...], ref[...], 1, 1) for ref in parts]
-        half = of_ring(own_ref[k], *grams)
+    for k in range(2):
+        part = jnp.concatenate([refs[2 * k][...], refs[2 * k + 1][...]], axis=0)
+        half = of_ring(own_ref[k], side_ref[2 * k], side_ref[2 * k + 1], exact_dot(part, part, 1, 1))
         total = half if total is None else total + half
-    out_ref[...] = mine_of(core_ref, total)
+    refs[-1][...] = mine_of(core_ref, total)
 
 
 def first_gram(core, near, far):
     rank = near[0].shape[0]
-    own = pl.pallas_call(
-        pair_kernel,
-        out_shape=jax.ShapeDtypeStruct((2, rank, rank), f32),
-        in_specs=[vmem] * 2,
+    own = grams_of(near[0], far[0])
+    sides = grams_of(*near[1:3], *far[1:3])
+    return pl.pallas_call(
+        last_grams_kernel,
+        out_shape=packed(rank),
+        in_specs=[smem] + [vmem] * 6,
         out_specs=vmem,
-        name="pair_gram",
-    )(near[0], far[0])
-    return pl.pallas_call(
-        last_pairs_kernel,
-        out_shape=packed(rank),
-        in_specs=[smem] + [vmem] * 7,
-        out_specs=vmem,
-        name="last_pair_grams",
-    )(core, own, *near[1:], *far[1:])
+        name="last_grams",
+    )(core, own, sides, *near[3:], *far[3:])
 
 
 def whole_gram(core_ref, mine_ref, other_ref, gram):
@@ -306,8 +312,13 @@
 
 
 def first_kernel(core_ref, slot_ref, mine_ref, other_ref, *refs):
-    parts, (basis_ref, out_ref), (held, grams, sems, gram, inverse), scratch = refs[:8], refs[8:10], refs[10:15], refs[15:]
-    copies = [pltpu.make_async_copy(ref, held.at[k], sems.at[k]) for k, ref in enumerate(parts)]
+    parts, (basis_ref, out_ref), (held, grams, sems, gram, inverse) = refs[:10], refs[10:12], refs[12:17]
+    scratch = refs[17:]
+    rows = parts[3].shape[0]
+    places = []
+    for k in (0, 4):
+        places += [held.at[k], held.at[k + 1], held.at[k + 2], held.at[k + 3, :rows], held.at[k + 3, rows:]]
+    copies = [pltpu.make_async_copy(ref, place, sems.at[k]) for k, (ref, place) in enumerate(zip(parts, places))]
     for copy in copies:
         copy.start()
     whole_gram(core_ref, mine_ref, other_ref, gram)
@@ -328,11 +339,11 @@
 
 def first_sweep(core, slots, mine, other, parts):
     rank, width = parts[0].shape
-    scratch = [pltpu.VMEM((8, rank, width), f32), pltpu.VMEM((8, rank, rank), f32), pltpu.SemaphoreType.DMA((8,))]
+    scratch = [pltpu.VMEM((8, rank, width), f32), pltpu.VMEM((8, rank, rank), f32), pltpu.SemaphoreType.DMA((10,))]
     return pl.pallas_call(
         first_kernel,
         out_shape=(jax.ShapeDtypeStruct((8, rank, width), f32), packed(rank)),
-        in_specs=[smem, smem, vmem, vmem] + [hbm] * 8,
+        in_specs=[smem, smem, vmem, vmem] + [hbm] * 10,
         out_specs=(vmem, vmem),
         scratch_shapes=scratch + [pltpu.VMEM((rank, rank), f32)] + factor_scratch(rank),
         name="first_sweep",
@@ -380,10 +391,12 @@
     offsets = jnp.asarray((0, *steps))
     slots = jnp.concatenate([core * side + (a - offsets) % side, (1 - core) * side + (b - offsets) % side])
 
-    two, one = user_rows(place, 0, interactions, omega)
-    two, one = shift(two, "item", 2), shift(one, "item", 1)
-    three, own = user_rows(place, 2, interactions, omega)
-    own = of_ring(own, one, shift(three, "item", 3), two)
+    (two,) = user_rows(place, 0, 1, interactions, omega)
+    two = shift(two, "item", 2)
+    one, three = user_rows(place, 1, 2, interactions, omega)
+    one, three = shift(one, "item", 1), shift(three, "item", 3)
+    (own,) = user_rows(place, 3, 1, interactions, omega)
+    own = of_ring(own, one, three, two)
     one, three = shift(own, "item", 1), shift(own, "item", 3)
     half = own.shape[0] // 2
     two = [shift(one[:half], "item", 1), shift(three[half:], "item", 3)]
@@ -393,14 +406,20 @@
     away = shift(item_columns(place, 6, two, interactions, total, 0, 2), "core")
     kept = item_columns(place, 6, two, interactions, total, 1, 2)
 
-    def block_at(k):
-        return lax.dynamic_index_in_dim(kept, k, 0, False) + lax.dynamic_index_in_dim(away, k, 0, False)
-
-    block = of_ring(block_at(a), *(shift(block_at((a + d) % side), "first", d) for d in steps))
+    def block_at(d, halves):
+        return sum(lax.dynamic_index_in_dim(h, (a + d) % side, 0, False) for h in halves)
+
+    two = block_at(2, (kept, away))
+    two, *halves = lax.optimization_barrier((two, kept, away))
+    two = shift(two, "first", 2)
+    one, three = block_at(1, halves), block_at(3, halves)
+    block = of_ring(block_at(0, halves), shift(one, "first", 1), shift(three, "first", 3), two)
     own_omega = lax.dynamic_slice_in_dim(omega, (core * side + a) * width, width, 0)
     block = of_ring(*from_ring(block, "second")) + ridge * own_omega.T
 
-    near = from_ring(block, "first")
+    half = block.shape[0] // 2
+    one, three = shift(block, "first", 1), shift(block, "first", 3)
+    near = [block, one, three, shift(one[:half], "first", 1), shift(three[half:], "first", 3)]
     far = [shift(part, "core") for part in near]
     flag = core.reshape(1).astype(jnp.int32)
 

time: 208 us -> 216 us (1.038)
  waiting for transfers between devices: 66.7 us -> 58.5 us
  Pallas kernels: 84.2 us -> 91.1 us
  starting transfers between devices: 41.2 us -> 47.2 us
    ppermute x16 -> x18, starting transfers between devices: 22.9 us -> 30.1 us  [shift(): return lax.ppermute(a, 'user', pairs_of(axis, step))]
    pallas_call x4 -> x6, Pallas kernels: 28 us -> 34.9 us  [the longest x3 24.2 us: user_rows(): pl.pallas_call(lambda *refs: rows_kernel(count, *refs), out_shape=(jax.Sh...]
    ppermute x16 -> x18, waiting for transfers between devices: 34.1 us -> 28.9 us  [shift(): return lax.ppermute(a, 'user', pairs_of(axis, step))]
    ppermute x13, waiting for transfers between devices: 32.7 us -> 29.6 us  [shift(): lax.ppermute(a, 'item', [(i, (i + step) % side) for i in range(side)])]
  transfers between devices with their start and end apart: 29 -> 31, of which waited for: 13 -> 14; matrix products, arithmetic and copies ran while one was open for 1% -> 1% of each run, Pallas kernels for 17% -> 21%
where the time goes in v3:
time: 216 us; the launch traced here: 214 us
  Pallas kernels  91.1 us (42%)
  waiting for transfers between devices  58.5 us (27%)
  starting transfers between devices  47.2 us (22%)
  other arithmetic  10.3 us (5%)
  local copies, waits for them, and re-layouts  7.1 us (3%)
    ppermute x18, starting transfers between devices, shift(): return lax.ppermute(a, 'user', pairs_of(axis, step))  30.1 us
    ppermute x13, waiting for transfers between devices, shift(): lax.ppermute(a, 'item', [(i, (i + step) % side) for i in range(side)])  29.6 us
    ppermute x18, waiting for transfers between devices, shift(): return lax.ppermute(a, 'user', pairs_of(axis, step))  28.9 us
    pallas_call x4, Pallas kernels, item_columns(): pl.pallas_call(lambda *refs: columns_kernel(count, splits, total is not N...  27.4 us
    pallas_call x3, Pallas kernels, user_rows(): pl.pallas_call(lambda *refs: rows_kernel(count, *refs), out_shape=(jax.Sh...  24.2 us
    pallas_call x1, Pallas kernels, first_sweep(): pl.pallas_call(first_kernel, out_shape=(jax.ShapeDtypeStruct((8, rank, wi...  20.2 us
    ppermute x13, starting transfers between devices, shift(): lax.ppermute(a, 'item', [(i, (i + step) % side) for i in range(side)])  17.1 us
    pallas_call x1, Pallas kernels, second_sweep(): pl.pallas_call(lambda *refs: second_kernel(scale, *refs), out_shape=jax.S...  8.65 us
  transfers between devices with their start and end apart: 31, of which 14 were waited for; matrix products, arithmetic and copies ran while one was open for 1% of the time, Pallas kernels for 21%

profile of v3, /device:TPU:1, one launch (start us, length us, event | category | flops | bytes accessed | tf_op | source)
XLA Modules:
  0.0 214.5 jit_solution(18369790335979476092)
XLA Ops:
  0.7 9.8 %user_rows.5 = (f32[256,512]{1,0:T(8,128)}, f32[256,512]{1,0:T(8,128)}) custom-call(s32[8]{0:T(128)} %stack.23.refs_0_, bf16[2048,4096]{1,0:T(8,128)(2,1)} %refs_3_.7, bf16[2048,4096]{1,0:T(8,128)(2,1)} %refs_3_.7, f32[4096,256]{1,0:T(8,128)} %refs_3_.4), custom_call_target="tpu_custom_call" | custom-call | tf_op jit(solution)/shard_map/user_rows/pallas_call | solution.py:89
  15.0 7.2 %user_rows.4 = f32[256,512]{1,0:T(8,128)} custom-call(s32[8]{0:T(128)} %stack.23.refs_0_, bf16[2048,4096]{1,0:T(8,128)(2,1)} %refs_3_.7, f32[4096,256]{1,0:T(8,128)} %refs_3_.4), custom_call_target="tpu_custom_call" | custom-call | tf_op jit(solution)/shard_map/user_rows/pallas_call | solution.py:89
  23.6 7.2 %user_rows.3 = f32[256,512]{1,0:T(8,128)} custom-call(s32[8]{0:T(128)} %stack.23.refs_0_, bf16[2048,4096]{1,0:T(8,128)(2,1)} %refs_3_.7, f32[4096,256]{1,0:T(8,128)} %refs_3_.4), custom_call_target="tpu_custom_call" | custom-call | tf_op jit(solution)/shard_map/user_rows/pallas_call | solution.py:89
  30.8 8.2 %collective-permute-done = f32[256,512]{1,0:T(8,128)S(1)} collective-permute-done((f32[256,512]{1,0:T(8,128)}, f32[256,512]{1,0:T(8,128)S(1)}, u32[]{:S(2)}, u32[]{:S(2)}) %collective-permute-start) | collective-permute-done | bytes 524320 | tf_op jit(solution)/shard_map/ppermute | solution.py:53
  43.0 10.5 %collective-permute-done.3.refs_1_ = f32[256,512]{1,0:T(8,128)S(1)} collective-permute-done((f32[256,512]{1,0:T(8,128)S(1)}, f32[256,512]{1,0:T(8,128)S(1)}, u32[]{:S(2)}, u32[]{:S(2)}) %collective-permute-start.3) | collective-permute-done | bytes 524320 | tf_op jit(solution)/shard_map/ppermute | solution.py:53
  56.4 7.0 %item_columns.4.refs_5_ = f32[8,256,512]{2,1,0:T(8,128)} custom-call(s32[8]{0:T(128)} %stack.23.refs_0_, f32[256,512]{1,0:T(8,128)} %copy-done.4, bf16[2048,4096]{1,0:T(8,128)(2,1)} %refs_3_.7), custom_call_target="tpu_custom_call" | custom-call | tf_op jit(solution)/shard_map/item_columns/pallas_call | solution.py:151
  63.4 10.6 %item_columns.5.refs_4_ = f32[8,256,512]{2,1,0:T(8,128)} custom-call(s32[8]{0:T(128)} %stack.23.refs_0_, f32[256,512]{1,0:T(8,128)} %copy-done.7, f32[256,512]{1,0:T(8,128)} %copy-done.8, bf16[2048,4096]{1,0:T(8,128)(2,1)} %refs_3_.7, bf16[2048,4096]{1,0:T(8,128)(2,1)} %refs_3_.7, f32[8,256,512]{2,1,0:T(8,128)} %item_columns.4.refs_5_), custom_call_target="tpu_custom_call" | custom-call | tf_op jit(solution)/shard_map/item_columns/pallas_call | solution.py:151
  75.4 4.9 %item_columns.7 = f32[4,256,512]{2,1,0:T(8,128)} custom-call(s32[8]{0:T(128)} %stack.23.refs_0_, f32[128,512]{1,0:T(8,128)} %copy-done.9, f32[128,512]{1,0:T(8,128)} %copy-done.10, bf16[2048,4096]{1,0:T(8,128)(2,1)} %refs_3_.7, f32[8,256,512]{2,1,0:T(8,128)} %item_columns.5.refs_4_), custom_call_target="tpu_custom_call" | custom-call | tf_op jit(solution)/shard_map/item_columns/pallas_call | solution.py:151
  80.3 3.0 %collective-permute-start.7 = (f32[4,256,512]{2,1,0:T(8,128)}, f32[4,256,512]{2,1,0:T(8,128)S(1)}, u32[]{:S(2)}, u32[]{:S(2)}) collective-permute-start(f32[4,256,512]{2,1,0:T(8,128)} %item_columns.7), channel_id=1, source_target_pairs={{0,1},{1,0},{2,3},{3,2},{4,5},{5,4},{6,7},{7,6},{8,9},{9,8},{10,11... | collective-permute-start | bytes 6291464 | tf_op jit(solution)/shard_map/ppermute | solution.py:54
  83.3 4.9 %item_columns.6 = f32[4,256,512]{2,1,0:T(8,128)} custom-call(s32[8]{0:T(128)} %stack.23.refs_0_, f32[128,512]{1,0:T(8,128)} %copy-done.9, f32[128,512]{1,0:T(8,128)} %copy-done.10, bf16[2048,4096]{1,0:T(8,128)(2,1)} %refs_3_.7, f32[8,256,512]{2,1,0:T(8,128)} %item_columns.5.refs_4_), custom_call_target="tpu_custom_call" | custom-call | tf_op jit(solution)/shard_map/item_columns/pallas_call | solution.py:151
  96.1 10.4 %collective-permute-done.10 = f32[256,512]{1,0:T(8,128)S(1)} collective-permute-done((f32[256,512]{1,0:T(8,128)}, f32[256,512]{1,0:T(8,128)S(1)}, u32[]{:S(2)}, u32[]{:S(2)}) %collective-permute-start.10) | collective-permute-done | bytes 524320 | tf_op jit(solution)/shard_map/ppermute | solution.py:54
  106.5 3.4 %collective-permute-done.9 = f32[256,512]{1,0:T(8,128)} collective-permute-done((f32[256,512]{1,0:T(8,128)}, f32[256,512]{1,0:T(8,128)}, u32[]{:S(2)}, u32[]{:S(2)}) %collective-permute-start.9) | collective-permute-done | bytes 524320 | tf_op jit(solution)/shard_map/ppermute | solution.py:54
  118.1 3.5 %collective-permute-done.11 = f32[256,512]{1,0:T(8,128)S(1)} collective-permute-done((f32[256,512]{1,0:T(8,128)S(1)}, f32[256,512]{1,0:T(8,128)S(1)}, u32[]{:S(2)}, u32[]{:S(2)}) %collective-permute-start.11) | collective-permute-done | bytes 524320 | tf_op jit(solution)/shard_map/ppermute | solution.py:54
  121.5 5.6 %collective-permute-done.12 = f32[256,512]{1,0:T(8,128)S(1)} collective-permute-done((f32[256,512]{1,0:T(8,128)S(1)}, f32[256,512]{1,0:T(8,128)S(1)}, u32[]{:S(2)}, u32[]{:S(2)}) %collective-permute-start.12) | collective-permute-done | bytes 524320 | tf_op jit(solution)/shard_map/ppermute | solution.py:54
  134.0 4.1 %collective-permute-done.15.refs_0_.refs_1_ = f32[256,512]{1,0:T(8,128)S(1)} collective-permute-done((f32[256,512]{1,0:T(8,128)S(1)}, f32[256,512]{1,0:T(8,128)S(1)}, u32[]{:S(2)}, u32[]{:S(2)}) %collective-permute-start.15) | collective-permute-done | bytes 524320 | tf_op jit(solution)/shard_map/ppermute | solution.py:54
  138.2 3.1 %collective-permute-start.17 = (f32[256,512]{1,0:T(8,128)S(1)}, f32[256,512]{1,0:T(8,128)S(1)}, u32[]{:S(2)}, u32[]{:S(2)}) collective-permute-start(f32[256,512]{1,0:T(8,128)S(1)} %collective-permute-done.15.refs_0_.refs_1_), channel_id=1, source_target_pairs={{0,1},{1,0},{2,3},{3,2},{4,5},{5,4},{6,7},{7,6},{8,9},{9,8},{10,11... | collective-permute-start | bytes 1572872 | tf_op jit(solution)/shard_map/ppermute | solution.py:54
  144.6 4.2 %collective-permute-start.21 = (f32[128,512]{1,0:T(8,128)S(1)}, f32[128,512]{1,0:T(8,128)}, u32[]{:S(2)}, u32[]{:S(2)}) collective-permute-start(f32[128,512]{1,0:T(8,128)S(1)} %collective-permute-done.19.refs_0_.refs_3_), channel_id=1, source_target_pairs={{0,1},{1,0},{2,3},{3,2},{4,5},{5,4},{6,7},{7,6},{8,9},{9,8},{10,11... | collective-permute-start | bytes 786440 | tf_op jit(solution)/shard_map/ppermute | solution.py:54
  149.8 3.0 %part_grams.2.own_ref = f32[2,256,256]{2,1,0:T(8,128)} custom-call(f32[256,512]{1,0:T(8,128)} %copy-done, f32[256,512]{1,0:T(8,128)} %copy-done.3), custom_call_target="tpu_custom_call" | custom-call | tf_op jit(solution)/shard_map/part_grams/pallas_call | solution.py:273
  154.4 4.3 %part_grams.3.side_ref = f32[4,256,256]{2,1,0:T(8,128)} custom-call(f32[256,512]{1,0:T(8,128)} %copy-done.1, f32[256,512]{1,0:T(8,128)} %copy-done.2, f32[256,512]{1,0:T(8,128)} %copy-done.5, f32[256,512]{1,0:T(8,128)} %copy-done.6), custom_call_target="tpu_custom_call" | custom-call | tf_op jit(solution)/shard_map/part_grams/pallas_call | solution.py:273
  158.8 3.3 %last_grams.1 = f32[192,128]{1,0:T(8,128)} custom-call(s32[1]{0:T(128)} %bitcast.core_ref.refs_0_, f32[2,256,256]{2,1,0:T(8,128)} %part_grams.2.own_ref, f32[4,256,256]{2,1,0:T(8,128)} %part_grams.3.side_ref, f32[128,512]{1,0:T(8,128)} %copy-done.11, f32[128,512]{1,0:T(8,128)} %collective-permute-done.20.refs_1_.refs_4_, ...), custom_call_target="tpu_custom_call" | custom-call | tf_op jit(solution)/shard_map/last_grams/pallas_call | solution.py:295
  164.8 3.1 %collective-permute-done.23 = f32[192,128]{1,0:T(8,128)S(1)} collective-permute-done((f32[192,128]{1,0:T(8,128)}, f32[192,128]{1,0:T(8,128)S(1)}, u32[]{:S(2)}, u32[]{:S(2)}) %collective-permute-start.23) | collective-permute-done | bytes 98336 | tf_op jit(solution)/shard_map/ppermute | solution.py:53
  173.7 20.2 %first_sweep.1 = (f32[8,256,512]{2,1,0:T(8,128)}, f32[192,128]{1,0:T(8,128)}) custom-call(s32[1]{0:T(128)} %bitcast.core_ref.refs_0_, s32[8]{0:T(128)} %pad_add_fusion.slot_ref, f32[192,128]{1,0:T(8,128)} %copy-done.13, f32[192,128]{1,0:T(8,128)} %copy-done.15, f32[256,512]{1,0:T(8,128)} %copy-done, f32[256,512]{1,0:T(8,128)} %copy-done.1, ...), custom_call_target="tpu_custom_call" | custom-call | tf_op jit(solution)/shard_map/first_sweep/pallas_call | solution.py:343
  196.9 2.8 %collective-permute-done.27 = f32[192,128]{1,0:T(8,128)S(1)} collective-permute-done((f32[192,128]{1,0:T(8,128)}, f32[192,128]{1,0:T(8,128)S(1)}, u32[]{:S(2)}, u32[]{:S(2)}) %collective-permute-start.27) | collective-permute-done | bytes 98336 | tf_op jit(solution)/shard_map/ppermute | solution.py:53
  205.8 8.6 %second_sweep.1 = f32[4096,256]{1,0:T(8,128)} custom-call(s32[1]{0:T(128)} %bitcast.core_ref.refs_0_, f32[192,128]{1,0:T(8,128)} %copy-done.12, f32[192,128]{1,0:T(8,128)} %copy-done.14, f32[8,256,512]{2,1,0:T(8,128)} %get-tuple-element.18.refs_3_), custom_call_target="tpu_custom_call" | custom-call | tf_op jit(solution)/shard_map/second_sweep/pallas_call | solution.py:370
  (100 shorter events, 61.3 us)
Async XLA Ops:
  10.5 20.3 %collective-permute-start.1 = (f32[256,512]{1,0:T(8,128)}, f32[256,512]{1,0:T(8,128)S(1)}, u32[]{:S(2)}, u32[]{:S(2)}) collective-permute-start(f32[256,512]{1,0:T(8,128)} %get-tuple-element.12), channel_id=1, source_target_pairs={{0,32},{32,64},{64,96},{96,0},{1,33},{33,65},{65,97},{97,1},{2,34}... | collective-permute-start | bytes 1572872 | tf_op jit(solution)/shard_map/ppermute | solution.py:53
  12.9 17.8 %collective-permute-start.2 = (f32[256,512]{1,0:T(8,128)}, f32[256,512]{1,0:T(8,128)S(1)}, u32[]{:S(2)}, u32[]{:S(2)}) collective-permute-start(f32[256,512]{1,0:T(8,128)} %get-tuple-element.13), channel_id=1, source_target_pairs={{0,96},{32,0},{64,32},{96,64},{1,97},{33,1},{65,33},{97,65},{2,98}... | collective-permute-start | bytes 1572872 | tf_op jit(solution)/shard_map/ppermute | solution.py:53
  22.2 16.8 %collective-permute-start = (f32[256,512]{1,0:T(8,128)}, f32[256,512]{1,0:T(8,128)S(1)}, u32[]{:S(2)}, u32[]{:S(2)}) collective-permute-start(f32[256,512]{1,0:T(8,128)} %user_rows.4), channel_id=1, source_target_pairs={{0,64},{32,96},{64,0},{96,32},{1,65},{33,97},{65,1},{97,33},{2,66}... | collective-permute-start | bytes 1572872 | tf_op jit(solution)/shard_map/ppermute | solution.py:53
  40.3 13.2 %collective-permute-start.3 = (f32[256,512]{1,0:T(8,128)S(1)}, f32[256,512]{1,0:T(8,128)S(1)}, u32[]{:S(2)}, u32[]{:S(2)}) collective-permute-start(f32[256,512]{1,0:T(8,128)S(1)} %add_add_fusion.refs_1_), channel_id=1, source_target_pairs={{0,32},{32,64},{64,96},{96,0},{1,33},{33,65},{65,97},{97,1},{2,34}... | collective-permute-start | bytes 1572872 | tf_op jit(solution)/shard_map/ppermute | solution.py:53
  40.9 12.7 %collective-permute-start.5 = (f32[256,512]{1,0:T(8,128)S(1)}, f32[256,512]{1,0:T(8,128)S(1)}, u32[]{:S(2)}, u32[]{:S(2)}) collective-permute-start(f32[256,512]{1,0:T(8,128)S(1)} %add_add_fusion.refs_1_), channel_id=1, source_target_pairs={{0,96},{32,0},{64,32},{96,64},{1,97},{33,1},{65,33},{97,65},{2,98}... | collective-permute-start | bytes 1572872 | tf_op jit(solution)/shard_map/ppermute | solution.py:53
  53.5 20.5 %collective-permute-start.4 = (f32[128,512]{1,0:T(8,128)S(1)}, f32[128,512]{1,0:T(8,128)S(1)}, u32[]{:S(2)}, u32[]{:S(2)}) collective-permute-start(f32[128,512]{1,0:T(8,128)S(1)} %slice.16), channel_id=1, source_target_pairs={{0,32},{32,64},{64,96},{96,0},{1,33},{33,65},{65,97},{97,1},{2,34}... | collective-permute-start | bytes 786440 | tf_op jit(solution)/shard_map/ppermute | solution.py:53
  53.7 20.4 %collective-permute-start.6 = (f32[128,512]{1,0:T(8,128)S(1)}, f32[128,512]{1,0:T(8,128)S(1)}, u32[]{:S(2)}, u32[]{:S(2)}) collective-permute-start(f32[128,512]{1,0:T(8,128)S(1)} %slice.17), channel_id=1, source_target_pairs={{0,96},{32,0},{64,32},{96,64},{1,97},{33,1},{65,33},{97,65},{2,98}... | collective-permute-start | bytes 786440 | tf_op jit(solution)/shard_map/ppermute | solution.py:53
  80.3 7.9 %collective-permute-start.7 = (f32[4,256,512]{2,1,0:T(8,128)}, f32[4,256,512]{2,1,0:T(8,128)S(1)}, u32[]{:S(2)}, u32[]{:S(2)}) collective-permute-start(f32[4,256,512]{2,1,0:T(8,128)} %item_columns.7), channel_id=1, source_target_pairs={{0,1},{1,0},{2,3},{3,2},{4,5},{5,4},{6,7},{7,6},{8,9},{9,8},{10,11... | collective-permute-start | bytes 6291464 | tf_op jit(solution)/shard_map/ppermute | solution.py:54
  91.7 14.8 %collective-permute-start.10 = (f32[256,512]{1,0:T(8,128)}, f32[256,512]{1,0:T(8,128)S(1)}, u32[]{:S(2)}, u32[]{:S(2)}) collective-permute-start(f32[256,512]{1,0:T(8,128)} %get-tuple-element.19), channel_id=1, source_target_pairs={{0,6},{1,25},{2,0},{3,27},{4,2},{5,29},{6,4},{7,31},{8,14},{9,1},{... | collective-permute-start | bytes 1572872 | tf_op jit(solution)/shard_map/ppermute | solution.py:54
  94.5 15.5 %collective-permute-start.9 = (f32[256,512]{1,0:T(8,128)}, f32[256,512]{1,0:T(8,128)}, u32[]{:S(2)}, u32[]{:S(2)}) collective-permute-start(f32[256,512]{1,0:T(8,128)} %get-tuple-element.20), channel_id=1, source_target_pairs={{0,2},{1,9},{2,4},{3,11},{4,6},{5,13},{6,0},{7,15},{8,10},{9,17},{... | collective-permute-start | bytes 1572872 | tf_op jit(solution)/shard_map/ppermute | solution.py:54
  94.5 15.5 %collective-permute-start.8 = (f32[256,512]{1,0:T(8,128)S(1)}, f32[256,512]{1,0:T(8,128)}, u32[]{:S(2)}, u32[]{:S(2)}) collective-permute-start(f32[256,512]{1,0:T(8,128)S(1)} %add_bitcast_fusion.2), channel_id=1, source_target_pairs={{0,4},{1,17},{2,6},{3,19},{4,0},{5,21},{6,2},{7,23},{8,12},{9,25},... | collective-permute-start | bytes 1572872 | tf_op jit(solution)/shard_map/ppermute | solution.py:54
  111.6 10.0 %collective-permute-start.11 = (f32[256,512]{1,0:T(8,128)S(1)}, f32[256,512]{1,0:T(8,128)S(1)}, u32[]{:S(2)}, u32[]{:S(2)}) collective-permute-start(f32[256,512]{1,0:T(8,128)S(1)} %fusion), channel_id=1, source_target_pairs={{0,16},{1,5},{2,18},{3,7},{4,20},{5,1},{6,22},{7,3},{8,24},{9,13},... | collective-permute-start | bytes 1572872 | tf_op jit(solution)/shard_map/ppermute | solution.py:54
  114.1 13.0 %collective-permute-start.12 = (f32[256,512]{1,0:T(8,128)S(1)}, f32[256,512]{1,0:T(8,128)S(1)}, u32[]{:S(2)}, u32[]{:S(2)}) collective-permute-start(f32[256,512]{1,0:T(8,128)S(1)} %fusion), channel_id=1, source_target_pairs={{0,8},{1,3},{2,10},{3,5},{4,12},{5,7},{6,14},{7,1},{8,16},{9,11},{... | collective-permute-start | bytes 1572872 | tf_op jit(solution)/shard_map/ppermute | solution.py:54
  114.4 12.7 %collective-permute-start.13 = (f32[256,512]{1,0:T(8,128)S(1)}, f32[256,512]{1,0:T(8,128)}, u32[]{:S(2)}, u32[]{:S(2)}) collective-permute-start(f32[256,512]{1,0:T(8,128)S(1)} %fusion), channel_id=1, source_target_pairs={{0,24},{1,7},{2,26},{3,1},{4,28},{5,3},{6,30},{7,5},{8,0},{9,15},{... | collective-permute-start | bytes 1572872 | tf_op jit(solution)/shard_map/ppermute | solution.py:54
  128.5 9.6 %collective-permute-start.15 = (f32[256,512]{1,0:T(8,128)S(1)}, f32[256,512]{1,0:T(8,128)S(1)}, u32[]{:S(2)}, u32[]{:S(2)}) collective-permute-start(f32[256,512]{1,0:T(8,128)S(1)} %bitcast_add_fusion.refs_0_), channel_id=1, source_target_pairs={{0,2},{1,9},{2,4},{3,11},{4,6},{5,13},{6,0},{7,15},{8,10},{9,17},{... | collective-permute-start | bytes 1572872 | tf_op jit(solution)/shard_map/ppermute | solution.py:54
  128.5 12.8 %collective-permute-start.16 = (f32[256,512]{1,0:T(8,128)S(1)}, f32[256,512]{1,0:T(8,128)S(1)}, u32[]{:S(2)}, u32[]{:S(2)}) collective-permute-start(f32[256,512]{1,0:T(8,128)S(1)} %bitcast_add_fusion.refs_0_), channel_id=1, source_target_pairs={{0,6},{1,25},{2,0},{3,27},{4,2},{5,29},{6,4},{7,31},{8,14},{9,1},{... | collective-permute-start | bytes 1572872 | tf_op jit(solution)/shard_map/ppermute | solution.py:54
  131.2 17.8 %collective-permute-start.14 = (f32[256,512]{1,0:T(8,128)S(1)}, f32[256,512]{1,0:T(8,128)S(1)}, u32[]{:S(2)}, u32[]{:S(2)}) collective-permute-start(f32[256,512]{1,0:T(8,128)S(1)} %bitcast_add_fusion.refs_0_), channel_id=1, source_target_pairs={{0,1},{1,0},{2,3},{3,2},{4,5},{5,4},{6,7},{7,6},{8,9},{9,8},{10,11... | collective-permute-start | bytes 1572872 | tf_op jit(solution)/shard_map/ppermute | solution.py:54
  138.2 14.7 %collective-permute-start.17 = (f32[256,512]{1,0:T(8,128)S(1)}, f32[256,512]{1,0:T(8,128)S(1)}, u32[]{:S(2)}, u32[]{:S(2)}) collective-permute-start(f32[256,512]{1,0:T(8,128)S(1)} %collective-permute-done.15.refs_0_.refs_1_), channel_id=1, source_target_pairs={{0,1},{1,0},{2,3},{3,2},{4,5},{5,4},{6,7},{7,6},{8,9},{9,8},{10,11... | collective-permute-start | bytes 1572872 | tf_op jit(solution)/shard_map/ppermute | solution.py:54
  141.3 11.5 %collective-permute-start.18 = (f32[256,512]{1,0:T(8,128)S(1)}, f32[256,512]{1,0:T(8,128)S(1)}, u32[]{:S(2)}, u32[]{:S(2)}) collective-permute-start(f32[256,512]{1,0:T(8,128)S(1)} %collective-permute-done.16.refs_1_.refs_2_), channel_id=1, source_target_pairs={{0,1},{1,0},{2,3},{3,2},{4,5},{5,4},{6,7},{7,6},{8,9},{9,8},{10,11... | collective-permute-start | bytes 1572872 | tf_op jit(solution)/shard_map/ppermute | solution.py:54
  144.6 14.2 %collective-permute-start.21 = (f32[128,512]{1,0:T(8,128)S(1)}, f32[128,512]{1,0:T(8,128)}, u32[]{:S(2)}, u32[]{:S(2)}) collective-permute-start(f32[128,512]{1,0:T(8,128)S(1)} %collective-permute-done.19.refs_0_.refs_3_), channel_id=1, source_target_pairs={{0,1},{1,0},{2,3},{3,2},{4,5},{5,4},{6,7},{7,6},{8,9},{9,8},{10,11... | collective-permute-start | bytes 786440 | tf_op jit(solution)/shard_map/ppermute | solution.py:54
  148.8 10.0 %collective-permute-start.22 = (f32[128,512]{1,0:T(8,128)}, f32[128,512]{1,0:T(8,128)}, u32[]{:S(2)}, u32[]{:S(2)}) collective-permute-start(f32[128,512]{1,0:T(8,128)} %collective-permute-done.20.refs_1_.refs_4_), channel_id=1, source_target_pairs={{0,1},{1,0},{2,3},{3,2},{4,5},{5,4},{6,7},{7,6},{8,9},{9,8},{10,11... | collective-permute-start | bytes 786440 | tf_op jit(solution)/shard_map/ppermute | solution.py:54
  162.1 8.0 %collective-permute-start.24 = (f32[192,128]{1,0:T(8,128)}, f32[192,128]{1,0:T(8,128)S(1)}, u32[]{:S(2)}, u32[]{:S(2)}) collective-permute-start(f32[192,128]{1,0:T(8,128)} %last_grams.1), channel_id=1, source_target_pairs={{0,32},{32,64},{64,96},{96,0},{1,33},{33,65},{65,97},{97,1},{2,34}... | collective-permute-start | bytes 294920 | tf_op jit(solution)/shard_map/ppermute | solution.py:53
  162.4 7.6 %collective-permute-start.25 = (f32[192,128]{1,0:T(8,128)}, f32[192,128]{1,0:T(8,128)S(1)}, u32[]{:S(2)}, u32[]{:S(2)}) collective-permute-start(f32[192,128]{1,0:T(8,128)} %last_grams.1), channel_id=1, source_target_pairs={{0,96},{32,0},{64,32},{96,64},{1,97},{33,1},{65,33},{97,65},{2,98}... | collective-permute-start | bytes 294920 | tf_op jit(solution)/shard_map/ppermute | solution.py:53
  194.2 8.2 %collective-permute-start.28 = (f32[192,128]{1,0:T(8,128)}, f32[192,128]{1,0:T(8,128)S(1)}, u32[]{:S(2)}, u32[]{:S(2)}) collective-permute-start(f32[192,128]{1,0:T(8,128)} %get-tuple-element.17), channel_id=1, source_target_pairs={{0,32},{32,64},{64,96},{96,0},{1,33},{33,65},{65,97},{97,1},{2,34}... | collective-permute-start | bytes 294920 | tf_op jit(solution)/shard_map/ppermute | solution.py:53
  (24 other events, 148.3 us)

commit v4 on v3

--- a/solution.py
+++ b/solution.py
@@ -59,6 +59,10 @@
 hbm = pl.BlockSpec(memory_space=pl.ANY)
 
 
+def room(mib):
+    return pltpu.CompilerParams(vmem_limit_bytes=mib << 20)
+
+
 def rows_kernel(count, place_ref, *refs):
     quarters, omega_ref, outs, total = refs[:count], refs[count], refs[count + 1 : -1], refs[-1]
     at, last = pl.program_id(0), pl.num_programs(0) - 1
@@ -98,6 +102,7 @@
             scratch_shapes=[pltpu.VMEM((count * span, rank), f32)],
         ),
         name="user_rows",
+        compiler_params=room(50),
     )(place, *[a] * count, omega)
 
 
@@ -159,6 +164,7 @@
             scratch_shapes=[pltpu.VMEM((2 * rank, count * span), bf16)],
         ),
         name="item_columns",
+        compiler_params=room(44),
     )(place, *args)
 
 
@@ -276,6 +282,7 @@
         in_specs=[vmem] * len(parts),
         out_specs=vmem,
         name="part_grams",
+        compiler_params=room(24),
     )(*parts)
 
 
@@ -298,6 +305,7 @@
         in_specs=[smem] + [vmem] * 6,
         out_specs=vmem,
         name="last_grams",
+        compiler_params=room(24),
     )(core, own, sides, *near[3:], *far[3:])
 
 
@@ -347,6 +355,7 @@
         out_specs=(vmem, vmem),
         scratch_shapes=scratch + [pltpu.VMEM((rank, rank), f32)] + factor_scratch(rank),
         name="first_sweep",
+        compiler_params=room(32),
     )(core, slots, mine, other, *parts)
 
 
@@ -375,6 +384,7 @@
         out_specs=pl.BlockSpec((per * width, rank), lambda i: (i, 0)),
         scratch_shapes=[pltpu.VMEM((rank, rank), f32)] + factor_scratch(rank),
         name="second_sweep",
+        compiler_params=room(32),
     )(core, mine, other, basis)
 
 

time: 216 us -> 192 us (0.89)
  Pallas kernels: 91.1 us -> 73.1 us
  other arithmetic: 10.3 us -> 5.98 us
  local copies, waits for them, and re-layouts: 7.1 us -> 3.63 us
    pallas_call x4, Pallas kernels: 27.4 us -> 21.7 us  [item_columns(): pl.pallas_call(lambda *refs: columns_kernel(count, splits, total is not N...]
    pallas_call x2, Pallas kernels: 7.37 us -> 2.89 us  [grams_of(): pl.pallas_call(grams_kernel, out_shape=jax.ShapeDtypeStruct((len(parts),...]
    pallas_call x3, Pallas kernels: 24.2 us -> 21.3 us  [user_rows(): pl.pallas_call(lambda *refs: rows_kernel(count, *refs), out_shape=(jax.Sh...]
    unnamed x35 -> x9, local copies, waits for them, and re-layouts: 5.3 us -> 2.4 us
    add x4, other arithmetic: 4.74 us -> 2.08 us  [of_ring(): return own + two + (one + three)]
  transfers between devices with their start and end apart: 31 -> 31, of which waited for: 14 -> 14; matrix products, arithmetic and copies ran while one was open for 1% -> 1% of each run, Pallas kernels for 21% -> 17%
where the time goes in v4:
time: 192 us; the launch traced here: 191 us
  Pallas kernels  73.1 us (38%)
  waiting for transfers between devices  60.4 us (31%)
  starting transfers between devices  47.3 us (25%)
  other arithmetic  5.98 us (3%)
  local copies, waits for them, and re-layouts  3.63 us (2%)
    ppermute x13, waiting for transfers between devices, shift(): lax.ppermute(a, 'item', [(i, (i + step) % side) for i in range(side)])  30.7 us
    ppermute x18, starting transfers between devices, shift(): return lax.ppermute(a, 'user', pairs_of(axis, step))  30 us
    ppermute x18, waiting for transfers between devices, shift(): return lax.ppermute(a, 'user', pairs_of(axis, step))  29.7 us
    pallas_call x4, Pallas kernels, item_columns(): pl.pallas_call(lambda *refs: columns_kernel(count, splits, total is not N...  21.7 us
    pallas_call x3, Pallas kernels, user_rows(): pl.pallas_call(lambda *refs: rows_kernel(count, *refs), out_shape=(jax.Sh...  21.3 us
    pallas_call x1, Pallas kernels, first_sweep(): pl.pallas_call(first_kernel, out_shape=(jax.ShapeDtypeStruct((8, rank, wi...  18.5 us
    ppermute x13, starting transfers between devices, shift(): lax.ppermute(a, 'item', [(i, (i + step) % side) for i in range(side)])  17.4 us
    pallas_call x1, Pallas kernels, second_sweep(): pl.pallas_call(lambda *refs: second_kernel(scale, *refs), out_shape=jax.S...  6.66 us
  transfers between devices with their start and end apart: 31, of which 14 were waited for; matrix products, arithmetic and copies ran while one was open for 1% of the time, Pallas kernels for 17%

profile of v4, /device:TPU:1, one launch (start us, length us, event | category | flops | bytes accessed | tf_op | source)
XLA Modules:
  0.0 190.7 jit_solution(1707274972987938264)
XLA Ops:
  0.1 8.7 %user_rows.5 = (f32[256,512]{1,0:T(8,128)S(1)}, f32[256,512]{1,0:T(8,128)S(1)}) custom-call(s32[8]{0:T(128)S(1)} %stack.23.refs_0_, bf16[2048,4096]{1,0:T(8,128)(2,1)} %refs_3_.7, bf16[2048,4096]{1,0:T(8,128)(2,1)} %refs_3_.7, f32[4096,256]{1,0:T(8,128)} %refs_3_.4), custom_call_target="tpu_custom_call" | custom-call | tf_op jit(solution)/shard_map/user_rows/pallas_call | solution.py:93
  13.5 6.3 %user_rows.4 = f32[256,512]{1,0:T(8,128)S(1)} custom-call(s32[8]{0:T(128)S(1)} %stack.23.refs_0_, bf16[2048,4096]{1,0:T(8,128)(2,1)} %refs_3_.7, f32[4096,256]{1,0:T(8,128)} %refs_3_.4), custom_call_target="tpu_custom_call" | custom-call | tf_op jit(solution)/shard_map/user_rows/pallas_call | solution.py:93
  21.1 6.3 %user_rows.3 = f32[256,512]{1,0:T(8,128)S(1)} custom-call(s32[8]{0:T(128)S(1)} %stack.23.refs_0_, bf16[2048,4096]{1,0:T(8,128)(2,1)} %refs_3_.7, f32[4096,256]{1,0:T(8,128)} %refs_3_.4), custom_call_target="tpu_custom_call" | custom-call | tf_op jit(solution)/shard_map/user_rows/pallas_call | solution.py:93
  27.4 9.8 %collective-permute-done = f32[256,512]{1,0:T(8,128)S(1)} collective-permute-done((f32[256,512]{1,0:T(8,128)S(1)}, f32[256,512]{1,0:T(8,128)S(1)}, u32[]{:S(2)}, u32[]{:S(2)}) %collective-permute-start) | collective-permute-done | bytes 524320 | tf_op jit(solution)/shard_map/ppermute | solution.py:53
  40.2 10.5 %collective-permute-done.3.refs_1_ = f32[256,512]{1,0:T(8,128)S(1)} collective-permute-done((f32[256,512]{1,0:T(8,128)S(1)}, f32[256,512]{1,0:T(8,128)S(1)}, u32[]{:S(2)}, u32[]{:S(2)}) %collective-permute-start.3) | collective-permute-done | bytes 524320 | tf_op jit(solution)/shard_map/ppermute | solution.py:53
  50.8 2.7 %collective-permute-start.6 = (f32[128,512]{1,0:T(8,128)S(1)}, f32[128,512]{1,0:T(8,128)S(1)}, u32[]{:S(2)}, u32[]{:S(2)}) collective-permute-start(f32[128,512]{1,0:T(8,128)S(1)} %slice.17), channel_id=1, source_target_pairs={{0,96},{32,0},{64,32},{96,64},{1,97},{33,1},{65,33},{97,65},{2,98}... | collective-permute-start | bytes 786440 | tf_op jit(solution)/shard_map/ppermute | solution.py:53
  53.5 5.4 %item_columns.4.refs_5_ = f32[8,256,512]{2,1,0:T(8,128)S(1)} custom-call(s32[8]{0:T(128)S(1)} %stack.23.refs_0_, f32[256,512]{1,0:T(8,128)S(1)} %add_add_fusion.refs_1_, bf16[2048,4096]{1,0:T(8,128)(2,1)} %refs_3_.7), custom_call_target="tpu_custom_call" | custom-call | tf_op jit(solution)/shard_map/item_columns/pallas_call | solution.py:156
  58.9 7.8 %item_columns.5.refs_4_ = f32[8,256,512]{2,1,0:T(8,128)S(1)} custom-call(s32[8]{0:T(128)S(1)} %stack.23.refs_0_, f32[256,512]{1,0:T(8,128)S(1)} %collective-permute-done.3.refs_1_, f32[256,512]{1,0:T(8,128)S(1)} %collective-permute-done.5.refs_2_, bf16[2048,4096]{1,0:T(8,128)(2,1)} %refs_3_.7, bf16[2048,4096]{1,0:T(8,128)(2,1)} %refs_3_.7, ...), custom_call_target="tpu_custom_call" | custom-call | tf_op jit(solution)/shard_map/item_columns/pallas_call | solution.py:156
  66.7 5.1 %item_columns.7 = f32[4,256,512]{2,1,0:T(8,128)} custom-call(s32[8]{0:T(128)S(1)} %stack.23.refs_0_, f32[128,512]{1,0:T(8,128)S(1)} %collective-permute-done.4.refs_1_, f32[128,512]{1,0:T(8,128)S(1)} %collective-permute-done.6.refs_2_, bf16[2048,4096]{1,0:T(8,128)(2,1)} %refs_3_.7, f32[8,256,512]{2,1,0:T(8,128)S(1)} %item_columns.5.refs_4_), custom_call_target="tpu_custom_call" | custom-call | tf_op jit(solution)/shard_map/item_columns/pallas_call | solution.py:156
  71.8 3.0 %collective-permute-start.7 = (f32[4,256,512]{2,1,0:T(8,128)}, f32[4,256,512]{2,1,0:T(8,128)}, u32[]{:S(2)}, u32[]{:S(2)}) collective-permute-start(f32[4,256,512]{2,1,0:T(8,128)} %item_columns.7), channel_id=1, source_target_pairs={{0,1},{1,0},{2,3},{3,2},{4,5},{5,4},{6,7},{7,6},{8,9},{9,8},{10,11... | collective-permute-start | bytes 6291464 | tf_op jit(solution)/shard_map/ppermute | solution.py:54
  77.0 3.4 %item_columns.6 = f32[4,256,512]{2,1,0:T(8,128)S(1)} custom-call(s32[8]{0:T(128)S(1)} %stack.23.refs_0_, f32[128,512]{1,0:T(8,128)S(1)} %collective-permute-done.4.refs_1_, f32[128,512]{1,0:T(8,128)S(1)} %collective-permute-done.6.refs_2_, bf16[2048,4096]{1,0:T(8,128)(2,1)} %refs_3_.7, f32[8,256,512]{2,1,0:T(8,128)S(1)} %copy-done.1), custom_call_target="tpu_custom_call" | custom-call | tf_op jit(solution)/shard_map/item_columns/pallas_call | solution.py:156
  83.9 2.8 %collective-permute-start.10 = (f32[256,512]{1,0:T(8,128)}, f32[256,512]{1,0:T(8,128)S(1)}, u32[]{:S(2)}, u32[]{:S(2)}) collective-permute-start(f32[256,512]{1,0:T(8,128)} %get-tuple-element.19), channel_id=1, source_target_pairs={{0,6},{1,25},{2,0},{3,27},{4,2},{5,29},{6,4},{7,31},{8,14},{9,1},{... | collective-permute-start | bytes 1572872 | tf_op jit(solution)/shard_map/ppermute | solution.py:54
  88.3 10.4 %collective-permute-done.10 = f32[256,512]{1,0:T(8,128)S(1)} collective-permute-done((f32[256,512]{1,0:T(8,128)}, f32[256,512]{1,0:T(8,128)S(1)}, u32[]{:S(2)}, u32[]{:S(2)}) %collective-permute-start.10) | collective-permute-done | bytes 524320 | tf_op jit(solution)/shard_map/ppermute | solution.py:54
  98.7 3.4 %collective-permute-done.9 = f32[256,512]{1,0:T(8,128)} collective-permute-done((f32[256,512]{1,0:T(8,128)}, f32[256,512]{1,0:T(8,128)}, u32[]{:S(2)}, u32[]{:S(2)}) %collective-permute-start.9) | collective-permute-done | bytes 524320 | tf_op jit(solution)/shard_map/ppermute | solution.py:54
  110.4 3.5 %collective-permute-done.11 = f32[256,512]{1,0:T(8,128)S(1)} collective-permute-done((f32[256,512]{1,0:T(8,128)S(1)}, f32[256,512]{1,0:T(8,128)S(1)}, u32[]{:S(2)}, u32[]{:S(2)}) %collective-permute-start.11) | collective-permute-done | bytes 524320 | tf_op jit(solution)/shard_map/ppermute | solution.py:54
  113.9 5.6 %collective-permute-done.12 = f32[256,512]{1,0:T(8,128)S(1)} collective-permute-done((f32[256,512]{1,0:T(8,128)S(1)}, f32[256,512]{1,0:T(8,128)S(1)}, u32[]{:S(2)}, u32[]{:S(2)}) %collective-permute-start.12) | collective-permute-done | bytes 524320 | tf_op jit(solution)/shard_map/ppermute | solution.py:54
  120.1 2.7 %collective-permute-start.16 = (f32[256,512]{1,0:T(8,128)S(1)}, f32[256,512]{1,0:T(8,128)S(1)}, u32[]{:S(2)}, u32[]{:S(2)}) collective-permute-start(f32[256,512]{1,0:T(8,128)S(1)} %bitcast_add_fusion.refs_0_), channel_id=1, source_target_pairs={{0,6},{1,25},{2,0},{3,27},{4,2},{5,29},{6,4},{7,31},{8,14},{9,1},{... | collective-permute-start | bytes 1572872 | tf_op jit(solution)/shard_map/ppermute | solution.py:54
  122.7 2.7 %collective-permute-start.14 = (f32[256,512]{1,0:T(8,128)S(1)}, f32[256,512]{1,0:T(8,128)S(1)}, u32[]{:S(2)}, u32[]{:S(2)}) collective-permute-start(f32[256,512]{1,0:T(8,128)S(1)} %bitcast_add_fusion.refs_0_), channel_id=1, source_target_pairs={{0,1},{1,0},{2,3},{3,2},{4,5},{5,4},{6,7},{7,6},{8,9},{9,8},{10,11... | collective-permute-start | bytes 1572872 | tf_op jit(solution)/shard_map/ppermute | solution.py:54
  125.4 4.2 %collective-permute-done.15.refs_0_.refs_1_ = f32[256,512]{1,0:T(8,128)S(1)} collective-permute-done((f32[256,512]{1,0:T(8,128)S(1)}, f32[256,512]{1,0:T(8,128)S(1)}, u32[]{:S(2)}, u32[]{:S(2)}) %collective-permute-start.15) | collective-permute-done | bytes 524320 | tf_op jit(solution)/shard_map/ppermute | solution.py:54
  129.7 3.0 %collective-permute-start.17 = (f32[256,512]{1,0:T(8,128)S(1)}, f32[256,512]{1,0:T(8,128)S(1)}, u32[]{:S(2)}, u32[]{:S(2)}) collective-permute-start(f32[256,512]{1,0:T(8,128)S(1)} %collective-permute-done.15.refs_0_.refs_1_), channel_id=1, source_target_pairs={{0,1},{1,0},{2,3},{3,2},{4,5},{5,4},{6,7},{7,6},{8,9},{9,8},{10,11... | collective-permute-start | bytes 1572872 | tf_op jit(solution)/shard_map/ppermute | solution.py:54
  136.1 4.1 %collective-permute-start.21 = (f32[128,512]{1,0:T(8,128)S(1)}, f32[128,512]{1,0:T(8,128)}, u32[]{:S(2)}, u32[]{:S(2)}) collective-permute-start(f32[128,512]{1,0:T(8,128)S(1)} %collective-permute-done.19.refs_0_.refs_3_), channel_id=1, source_target_pairs={{0,1},{1,0},{2,3},{3,2},{4,5},{5,4},{6,7},{7,6},{8,9},{9,8},{10,11... | collective-permute-start | bytes 786440 | tf_op jit(solution)/shard_map/ppermute | solution.py:54
  148.3 2.8 %collective-permute-done.23 = f32[192,128]{1,0:T(8,128)S(1)} collective-permute-done((f32[192,128]{1,0:T(8,128)S(1)}, f32[192,128]{1,0:T(8,128)S(1)}, u32[]{:S(2)}, u32[]{:S(2)}) %collective-permute-start.23) | collective-permute-done | bytes 98336 | tf_op jit(solution)/shard_map/ppermute | solution.py:53
  155.4 18.5 %first_sweep.1 = (f32[8,256,512]{2,1,0:T(8,128)S(1)}, f32[192,128]{1,0:T(8,128)S(1)}) custom-call(s32[1]{0:T(128)} %bitcast.core_ref.refs_0_, s32[8]{0:T(128)S(1)} %pad_add_fusion.slot_ref, f32[192,128]{1,0:T(8,128)S(1)} %add_add_fusion.2.mine_ref, f32[192,128]{1,0:T(8,128)S(1)} %collective-permute-done.26.other_ref, ...), custom_call_target="tpu_custom_call" | custom-call | tf_op jit(solution)/shard_map/first_sweep/pallas_call | solution.py:351
  184.1 6.7 %second_sweep.1 = f32[4096,256]{1,0:T(8,128)} custom-call(s32[1]{0:T(128)} %bitcast.core_ref.refs_0_, f32[192,128]{1,0:T(8,128)S(1)} %add_add_fusion.1.refs_1_, f32[192,128]{1,0:T(8,128)S(1)} %collective-permute-done.30.refs_2_, f32[8,256,512]{2,1,0:T(8,128)S(1)} %get-tuple-element.18.refs_3_), custom_call_target="tpu_custom_call" | custom-call | tf_op jit(solution)/shard_map/second_sweep/pallas_call | solution.py:379
  (74 shorter events, 51.4 us)
Async XLA Ops:
  8.8 18.6 %collective-permute-start.1 = (f32[256,512]{1,0:T(8,128)S(1)}, f32[256,512]{1,0:T(8,128)S(1)}, u32[]{:S(2)}, u32[]{:S(2)}) collective-permute-start(f32[256,512]{1,0:T(8,128)S(1)} %get-tuple-element.12), channel_id=1, source_target_pairs={{0,32},{32,64},{64,96},{96,0},{1,33},{33,65},{65,97},{97,1},{2,34}... | collective-permute-start | bytes 1572872 | tf_op jit(solution)/shard_map/ppermute | solution.py:53
  11.3 16.1 %collective-permute-start.2 = (f32[256,512]{1,0:T(8,128)S(1)}, f32[256,512]{1,0:T(8,128)S(1)}, u32[]{:S(2)}, u32[]{:S(2)}) collective-permute-start(f32[256,512]{1,0:T(8,128)S(1)} %get-tuple-element.13), channel_id=1, source_target_pairs={{0,96},{32,0},{64,32},{96,64},{1,97},{33,1},{65,33},{97,65},{2,98}... | collective-permute-start | bytes 1572872 | tf_op jit(solution)/shard_map/ppermute | solution.py:53
  19.8 17.4 %collective-permute-start = (f32[256,512]{1,0:T(8,128)S(1)}, f32[256,512]{1,0:T(8,128)S(1)}, u32[]{:S(2)}, u32[]{:S(2)}) collective-permute-start(f32[256,512]{1,0:T(8,128)S(1)} %user_rows.4), channel_id=1, source_target_pairs={{0,64},{32,96},{64,0},{96,32},{1,65},{33,97},{65,1},{97,33},{2,66}... | collective-permute-start | bytes 1572872 | tf_op jit(solution)/shard_map/ppermute | solution.py:53
  37.4 13.2 %collective-permute-start.3 = (f32[256,512]{1,0:T(8,128)S(1)}, f32[256,512]{1,0:T(8,128)S(1)}, u32[]{:S(2)}, u32[]{:S(2)}) collective-permute-start(f32[256,512]{1,0:T(8,128)S(1)} %add_add_fusion.refs_1_), channel_id=1, source_target_pairs={{0,32},{32,64},{64,96},{96,0},{1,33},{33,65},{65,97},{97,1},{2,34}... | collective-permute-start | bytes 1572872 | tf_op jit(solution)/shard_map/ppermute | solution.py:53
  38.1 12.7 %collective-permute-start.5 = (f32[256,512]{1,0:T(8,128)S(1)}, f32[256,512]{1,0:T(8,128)S(1)}, u32[]{:S(2)}, u32[]{:S(2)}) collective-permute-start(f32[256,512]{1,0:T(8,128)S(1)} %add_add_fusion.refs_1_), channel_id=1, source_target_pairs={{0,96},{32,0},{64,32},{96,64},{1,97},{33,1},{65,33},{97,65},{2,98}... | collective-permute-start | bytes 1572872 | tf_op jit(solution)/shard_map/ppermute | solution.py:53
  50.7 16.0 %collective-permute-start.4 = (f32[128,512]{1,0:T(8,128)S(1)}, f32[128,512]{1,0:T(8,128)S(1)}, u32[]{:S(2)}, u32[]{:S(2)}) collective-permute-start(f32[128,512]{1,0:T(8,128)S(1)} %slice.16), channel_id=1, source_target_pairs={{0,32},{32,64},{64,96},{96,0},{1,33},{33,65},{65,97},{97,1},{2,34}... | collective-permute-start | bytes 786440 | tf_op jit(solution)/shard_map/ppermute | solution.py:53
  50.8 15.9 %collective-permute-start.6 = (f32[128,512]{1,0:T(8,128)S(1)}, f32[128,512]{1,0:T(8,128)S(1)}, u32[]{:S(2)}, u32[]{:S(2)}) collective-permute-start(f32[128,512]{1,0:T(8,128)S(1)} %slice.17), channel_id=1, source_target_pairs={{0,96},{32,0},{64,32},{96,64},{1,97},{33,1},{65,33},{97,65},{2,98}... | collective-permute-start | bytes 786440 | tf_op jit(solution)/shard_map/ppermute | solution.py:53
  71.8 8.5 %collective-permute-start.7 = (f32[4,256,512]{2,1,0:T(8,128)}, f32[4,256,512]{2,1,0:T(8,128)}, u32[]{:S(2)}, u32[]{:S(2)}) collective-permute-start(f32[4,256,512]{2,1,0:T(8,128)} %item_columns.7), channel_id=1, source_target_pairs={{0,1},{1,0},{2,3},{3,2},{4,5},{5,4},{6,7},{7,6},{8,9},{9,8},{10,11... | collective-permute-start | bytes 6291464 | tf_op jit(solution)/shard_map/ppermute | solution.py:54
  83.9 14.8 %collective-permute-start.10 = (f32[256,512]{1,0:T(8,128)}, f32[256,512]{1,0:T(8,128)S(1)}, u32[]{:S(2)}, u32[]{:S(2)}) collective-permute-start(f32[256,512]{1,0:T(8,128)} %get-tuple-element.19), channel_id=1, source_target_pairs={{0,6},{1,25},{2,0},{3,27},{4,2},{5,29},{6,4},{7,31},{8,14},{9,1},{... | collective-permute-start | bytes 1572872 | tf_op jit(solution)/shard_map/ppermute | solution.py:54
  86.7 15.5 %collective-permute-start.9 = (f32[256,512]{1,0:T(8,128)}, f32[256,512]{1,0:T(8,128)}, u32[]{:S(2)}, u32[]{:S(2)}) collective-permute-start(f32[256,512]{1,0:T(8,128)} %get-tuple-element.20), channel_id=1, source_target_pairs={{0,2},{1,9},{2,4},{3,11},{4,6},{5,13},{6,0},{7,15},{8,10},{9,17},{... | collective-permute-start | bytes 1572872 | tf_op jit(solution)/shard_map/ppermute | solution.py:54
  86.7 15.5 %collective-permute-start.8 = (f32[256,512]{1,0:T(8,128)S(1)}, f32[256,512]{1,0:T(8,128)}, u32[]{:S(2)}, u32[]{:S(2)}) collective-permute-start(f32[256,512]{1,0:T(8,128)S(1)} %add_bitcast_fusion.2), channel_id=1, source_target_pairs={{0,4},{1,17},{2,6},{3,19},{4,0},{5,21},{6,2},{7,23},{8,12},{9,25},... | collective-permute-start | bytes 1572872 | tf_op jit(solution)/shard_map/ppermute | solution.py:54
  104.0 10.0 %collective-permute-start.11 = (f32[256,512]{1,0:T(8,128)S(1)}, f32[256,512]{1,0:T(8,128)S(1)}, u32[]{:S(2)}, u32[]{:S(2)}) collective-permute-start(f32[256,512]{1,0:T(8,128)S(1)} %fusion), channel_id=1, source_target_pairs={{0,16},{1,5},{2,18},{3,7},{4,20},{5,1},{6,22},{7,3},{8,24},{9,13},... | collective-permute-start | bytes 1572872 | tf_op jit(solution)/shard_map/ppermute | solution.py:54
  106.5 13.0 %collective-permute-start.12 = (f32[256,512]{1,0:T(8,128)S(1)}, f32[256,512]{1,0:T(8,128)S(1)}, u32[]{:S(2)}, u32[]{:S(2)}) collective-permute-start(f32[256,512]{1,0:T(8,128)S(1)} %fusion), channel_id=1, source_target_pairs={{0,8},{1,3},{2,10},{3,5},{4,12},{5,7},{6,14},{7,1},{8,16},{9,11},{... | collective-permute-start | bytes 1572872 | tf_op jit(solution)/shard_map/ppermute | solution.py:54
  106.8 12.7 %collective-permute-start.13 = (f32[256,512]{1,0:T(8,128)S(1)}, f32[256,512]{1,0:T(8,128)S(1)}, u32[]{:S(2)}, u32[]{:S(2)}) collective-permute-start(f32[256,512]{1,0:T(8,128)S(1)} %fusion), channel_id=1, source_target_pairs={{0,24},{1,7},{2,26},{3,1},{4,28},{5,3},{6,30},{7,5},{8,0},{9,15},{... | collective-permute-start | bytes 1572872 | tf_op jit(solution)/shard_map/ppermute | solution.py:54
  119.8 9.8 %collective-permute-start.15 = (f32[256,512]{1,0:T(8,128)S(1)}, f32[256,512]{1,0:T(8,128)S(1)}, u32[]{:S(2)}, u32[]{:S(2)}) collective-permute-start(f32[256,512]{1,0:T(8,128)S(1)} %bitcast_add_fusion.refs_0_), channel_id=1, source_target_pairs={{0,2},{1,9},{2,4},{3,11},{4,6},{5,13},{6,0},{7,15},{8,10},{9,17},{... | collective-permute-start | bytes 1572872 | tf_op jit(solution)/shard_map/ppermute | solution.py:54
  120.1 12.7 %collective-permute-start.16 = (f32[256,512]{1,0:T(8,128)S(1)}, f32[256,512]{1,0:T(8,128)S(1)}, u32[]{:S(2)}, u32[]{:S(2)}) collective-permute-start(f32[256,512]{1,0:T(8,128)S(1)} %bitcast_add_fusion.refs_0_), channel_id=1, source_target_pairs={{0,6},{1,25},{2,0},{3,27},{4,2},{5,29},{6,4},{7,31},{8,14},{9,1},{... | collective-permute-start | bytes 1572872 | tf_op jit(solution)/shard_map/ppermute | solution.py:54
  122.7 17.6 %collective-permute-start.14 = (f32[256,512]{1,0:T(8,128)S(1)}, f32[256,512]{1,0:T(8,128)S(1)}, u32[]{:S(2)}, u32[]{:S(2)}) collective-permute-start(f32[256,512]{1,0:T(8,128)S(1)} %bitcast_add_fusion.refs_0_), channel_id=1, source_target_pairs={{0,1},{1,0},{2,3},{3,2},{4,5},{5,4},{6,7},{7,6},{8,9},{9,8},{10,11... | collective-permute-start | bytes 1572872 | tf_op jit(solution)/shard_map/ppermute | solution.py:54
  129.7 11.7 %collective-permute-start.17 = (f32[256,512]{1,0:T(8,128)S(1)}, f32[256,512]{1,0:T(8,128)S(1)}, u32[]{:S(2)}, u32[]{:S(2)}) collective-permute-start(f32[256,512]{1,0:T(8,128)S(1)} %collective-permute-done.15.refs_0_.refs_1_), channel_id=1, source_target_pairs={{0,1},{1,0},{2,3},{3,2},{4,5},{5,4},{6,7},{7,6},{8,9},{9,8},{10,11... | collective-permute-start | bytes 1572872 | tf_op jit(solution)/shard_map/ppermute | solution.py:54
  132.7 8.7 %collective-permute-start.18 = (f32[256,512]{1,0:T(8,128)S(1)}, f32[256,512]{1,0:T(8,128)S(1)}, u32[]{:S(2)}, u32[]{:S(2)}) collective-permute-start(f32[256,512]{1,0:T(8,128)S(1)} %collective-permute-done.16.refs_1_.refs_2_), channel_id=1, source_target_pairs={{0,1},{1,0},{2,3},{3,2},{4,5},{5,4},{6,7},{7,6},{8,9},{9,8},{10,11... | collective-permute-start | bytes 1572872 | tf_op jit(solution)/shard_map/ppermute | solution.py:54
  132.8 7.4 %collective-permute-start.20 = (f32[128,512]{1,0:T(8,128)S(1)}, f32[128,512]{1,0:T(8,128)}, u32[]{:S(2)}, u32[]{:S(2)}) collective-permute-start(f32[128,512]{1,0:T(8,128)S(1)} %slice.19), channel_id=1, source_target_pairs={{0,6},{1,25},{2,0},{3,27},{4,2},{5,29},{6,4},{7,31},{8,14},{9,1},{... | collective-permute-start | bytes 786440 | tf_op jit(solution)/shard_map/ppermute | solution.py:54
  136.1 7.2 %collective-permute-start.21 = (f32[128,512]{1,0:T(8,128)S(1)}, f32[128,512]{1,0:T(8,128)}, u32[]{:S(2)}, u32[]{:S(2)}) collective-permute-start(f32[128,512]{1,0:T(8,128)S(1)} %collective-permute-done.19.refs_0_.refs_3_), channel_id=1, source_target_pairs={{0,1},{1,0},{2,3},{3,2},{4,5},{5,4},{6,7},{7,6},{8,9},{9,8},{10,11... | collective-permute-start | bytes 786440 | tf_op jit(solution)/shard_map/ppermute | solution.py:54
  145.6 7.9 %collective-permute-start.24 = (f32[192,128]{1,0:T(8,128)S(1)}, f32[192,128]{1,0:T(8,128)S(1)}, u32[]{:S(2)}, u32[]{:S(2)}) collective-permute-start(f32[192,128]{1,0:T(8,128)S(1)} %last_grams.1), channel_id=1, source_target_pairs={{0,32},{32,64},{64,96},{96,0},{1,33},{33,65},{65,97},{97,1},{2,34}... | collective-permute-start | bytes 294920 | tf_op jit(solution)/shard_map/ppermute | solution.py:53
  145.9 7.6 %collective-permute-start.25 = (f32[192,128]{1,0:T(8,128)S(1)}, f32[192,128]{1,0:T(8,128)S(1)}, u32[]{:S(2)}, u32[]{:S(2)}) collective-permute-start(f32[192,128]{1,0:T(8,128)S(1)} %last_grams.1), channel_id=1, source_target_pairs={{0,96},{32,0},{64,32},{96,64},{1,97},{33,1},{65,33},{97,65},{2,98}... | collective-permute-start | bytes 294920 | tf_op jit(solution)/shard_map/ppermute | solution.py:53
  174.2 8.0 %collective-permute-start.28 = (f32[192,128]{1,0:T(8,128)S(1)}, f32[192,128]{1,0:T(8,128)S(1)}, u32[]{:S(2)}, u32[]{:S(2)}) collective-permute-start(f32[192,128]{1,0:T(8,128)S(1)} %get-tuple-element.17), channel_id=1, source_target_pairs={{0,32},{32,64},{64,96},{96,0},{1,33},{33,65},{65,97},{97,1},{2,34}... | collective-permute-start | bytes 294920 | tf_op jit(solution)/shard_map/ppermute | solution.py:53
  (11 other events, 47.4 us)

commit v5 on v4

--- a/solution.py
+++ b/solution.py
@@ -108,7 +108,7 @@
 
 def columns_kernel(count, splits, adds, place_ref, *refs):
     ys, blocks = refs[: count * splits], refs[count * splits : count * splits + count]
-    z_ref, both = refs[-2], refs[-1]
+    outs, both = refs[count * splits + count + adds : -1], refs[-1]
     rows, span = ys[0].shape
     rank = rows * splits
 
@@ -119,18 +119,23 @@
             row = d % splits * rows
             both[row : row + rows, at], both[rank + row : rank + row + rows, at] = slices(ref[...])
 
-    out = None
+    total = None
     for d, ref in enumerate(blocks):
         term = fast_dot(both[:, d * span : d * span + span], ref[...])
-        out = term if out is None else out + term
-    z = out[:rank] + out[rank:]
-    width = z_ref.shape[2]
-    for k in range(z_ref.shape[0]):
-        part = z[:, k * width : k * width + width]
-        z_ref[k] = part + refs[-3][k] if adds else part
-
-
-def item_columns(place, start_at, ys, a, total=None, only=None, splits=1, block=1024):
+        total = term if total is None else total + term
+    z = total[:rank] + total[rank:]
+    width = outs[0].shape[2]
+    per = pl.num_programs(0) // len(outs)
+    for h, out in enumerate(outs):
+
+        @pl.when(pl.program_id(0) // per == h)
+        def _():
+            for k in range(out.shape[0]):
+                part = z[:, k * width : k * width + width]
+                out[k] = part + refs[count * splits + count][k] if adds else part
+
+
+def item_columns(place, at, ys, a, total=None, only=None, parts=1, splits=1, block=1024):
     _, items = a.shape
     rows, span = ys[0].shape
     rank = rows * splits
@@ -140,32 +145,36 @@
     grid = items // block // (1 if only is None else 2)
     start = 0 if not only else grid
     in_half = items // block // 2
+    of_part = grid // parts
 
     def of_items(i, s):
-        at = i + start
         core = s[place.shape[0] - 1]
-        return (at // in_half + 1 + core) % 2 * in_half + at % in_half
+        return ((i + start) // in_half + 1 + core) % 2 * in_half + (i + start) % in_half
 
     ins = [pl.BlockSpec((rows, span), lambda i, s: (0, 0), pipeline_mode=pl.Buffered(1))] * len(ys)
     for d in range(count):
-        ins.append(pl.BlockSpec((span, block), lambda i, s, d=d: (s[start_at + d], of_items(i, s))))
+        ins.append(pl.BlockSpec((span, block), lambda i, s, d=d: (s[at + d], of_items(i, s))))
     args = [*ys, *[a] * count]
     if total is not None:
-        ins.append(pl.BlockSpec((per, rank, width), lambda i, s: (i + start, 0, 0)))
+        ins.append(pl.BlockSpec((per, rank, width), lambda i, s: (i, 0, 0)))
         args.append(total)
-    return pl.pallas_call(
+    out = pl.pallas_call(
         lambda *refs: columns_kernel(count, splits, total is not None, *refs),
-        out_shape=jax.ShapeDtypeStruct((grid * per, rank, width), f32),
+        out_shape=(jax.ShapeDtypeStruct((of_part * per, rank, width), f32),) * parts,
         grid_spec=pltpu.PrefetchScalarGridSpec(
             num_scalar_prefetch=1,
             grid=(grid,),
             in_specs=ins,
-            out_specs=pl.BlockSpec((per, rank, width), lambda i, s: (i, 0, 0)),
+            out_specs=tuple(
+                pl.BlockSpec((per, rank, width), lambda i, s, h=h: (jnp.clip(i - h * of_part, 0, of_part - 1), 0, 0))
+                for h in range(parts)
+            ),
             scratch_shapes=[pltpu.VMEM((2 * rank, count * span), bf16)],
         ),
         name="item_columns",
         compiler_params=room(44),
     )(place, *args)
+    return out if parts > 1 else out[0]
 
 
 def inverse_factor_half(block):
@@ -269,41 +278,49 @@
 
 
 def grams_kernel(*refs):
-    for k, ref in enumerate(refs[:-1]):
-        part = ref[...]
-        refs[-1][k] = exact_dot(part, part, 1, 1)
-
-
-def grams_of(*parts):
-    rank = parts[0].shape[0]
+    grams = [exact_dot(ref[...], ref[...], 1, 1) for ref in refs[:-1]]
+    per = len(grams) // 2
+    for k in range(2):
+        refs[-1][k] = sum(grams[k * per + 1 : k * per + per], grams[k * per])
+
+
+def grams_of(near, far):
+    rank = near[0].shape[0]
     return pl.pallas_call(
         grams_kernel,
-        out_shape=jax.ShapeDtypeStruct((len(parts), rank, rank), f32),
-        in_specs=[vmem] * len(parts),
+        out_shape=jax.ShapeDtypeStruct((2, rank, rank), f32),
+        in_specs=[vmem] * (len(near) + len(far)),
         out_specs=vmem,
         name="part_grams",
         compiler_params=room(24),
-    )(*parts)
+    )(*near, *far)
 
 
 def last_grams_kernel(core_ref, own_ref, side_ref, *refs):
-    total = None
+    parts, out_ref, held, sems = refs[:4], refs[4], refs[5], refs[6]
+    copies = [pltpu.make_async_copy(ref, held.at[k], sems.at[k]) for k, ref in enumerate((own_ref, side_ref))]
+    for copy in copies:
+        copy.start()
+    lasts = []
     for k in range(2):
-        part = jnp.concatenate([refs[2 * k][...], refs[2 * k + 1][...]], axis=0)
-        half = of_ring(own_ref[k], side_ref[2 * k], side_ref[2 * k + 1], exact_dot(part, part, 1, 1))
-        total = half if total is None else total + half
-    refs[-1][...] = mine_of(core_ref, total)
+        part = jnp.concatenate([parts[2 * k][...], parts[2 * k + 1][...]], axis=0)
+        lasts.append(exact_dot(part, part, 1, 1))
+    for copy in copies:
+        copy.wait()
+    halves = [(held[0, k] + lasts[k]) + held[1, k] for k in range(2)]
+    out_ref[...] = mine_of(core_ref, halves[0] + halves[1])
 
 
 def first_gram(core, near, far):
     rank = near[0].shape[0]
-    own = grams_of(near[0], far[0])
-    sides = grams_of(*near[1:3], *far[1:3])
+    own = grams_of(near[:1], far[:1])
+    sides = grams_of(near[1:3], far[1:3])
     return pl.pallas_call(
         last_grams_kernel,
         out_shape=packed(rank),
-        in_specs=[smem] + [vmem] * 6,
+        in_specs=[smem] + [hbm] * 2 + [vmem] * 4,
         out_specs=vmem,
+        scratch_shapes=[pltpu.VMEM((2, 2, rank, rank), f32), pltpu.SemaphoreType.DMA((2,))],
         name="last_grams",
         compiler_params=room(24),
     )(core, own, sides, *near[3:], *far[3:])
@@ -412,9 +429,9 @@
     two = [shift(one[:half], "item", 1), shift(three[half:], "item", 3)]
 
     total = item_columns(place, 3, [own], interactions)
-    total = item_columns(place, 4, [one, three], interactions, total)
-    away = shift(item_columns(place, 6, two, interactions, total, 0, 2), "core")
-    kept = item_columns(place, 6, two, interactions, total, 1, 2)
+    sent, kept = item_columns(place, 4, [one, three], interactions, total, parts=2)
+    away = shift(item_columns(place, 6, two, interactions, sent, 0, splits=2), "core")
+    kept = item_columns(place, 6, two, interactions, kept, 1, splits=2)
 
     def block_at(d, halves):
         return sum(lax.dynamic_index_in_dim(h, (a + d) % side, 0, False) for h in halves)
@@ -423,7 +440,10 @@
     two, *halves = lax.optimization_barrier((two, kept, away))
     two = shift(two, "first", 2)
     one, three = block_at(1, halves), block_at(3, halves)
-    block = of_ring(block_at(0, halves), shift(one, "first", 1), shift(three, "first", 3), two)
+    one, three, *halves = lax.optimization_barrier((one, three, *halves))
+    one, three = shift(one, "first", 1), shift(three, "first", 3)
+    block = lax.optimization_barrier(block_at(0, halves))
+    block = of_ring(block, one, three, two)
     own_omega = lax.dynamic_slice_in_dim(omega, (core * side + a) * width, width, 0)
     block = of_ring(*from_ring(block, "second")) + ridge * own_omega.T
 

time: 192 us -> 191 us (level)
    add x2 -> x3, other arithmetic: 3.51 us -> 5.44 us  [block_at(): sum((lax.dynamic_index_in_dim(h, (a + d) % side, 0, False) for h in halves))]
where the time goes in v5:
time: 191 us; the launch traced here: 190 us
  Pallas kernels  73.4 us (38%)
  waiting for transfers between devices  59.2 us (31%)
  starting transfers between devices  47.2 us (25%)
  other arithmetic  7.35 us (4%)
  local copies, waits for them, and re-layouts  3.03 us (2%)
    ppermute x13, waiting for transfers between devices, shift(): lax.ppermute(a, 'item', [(i, (i + step) % side) for i in range(side)])  30.7 us
    ppermute x18, starting transfers between devices, shift(): return lax.ppermute(a, 'user', pairs_of(axis, step))  29.8 us
    ppermute x18, waiting for transfers between devices, shift(): return lax.ppermute(a, 'user', pairs_of(axis, step))  28.5 us
    pallas_call x4, Pallas kernels, item_columns(): pl.pallas_call(lambda *refs: columns_kernel(count, splits, total is not N...  21.8 us
    pallas_call x3, Pallas kernels, user_rows(): pl.pallas_call(lambda *refs: rows_kernel(count, *refs), out_shape=(jax.Sh...  21.3 us
    pallas_call x1, Pallas kernels, first_sweep(): pl.pallas_call(first_kernel, out_shape=(jax.ShapeDtypeStruct((8, rank, wi...  18.5 us
    ppermute x13, starting transfers between devices, shift(): lax.ppermute(a, 'item', [(i, (i + step) % side) for i in range(side)])  17.4 us
    pallas_call x1, Pallas kernels, second_sweep(): pl.pallas_call(lambda *refs: second_kernel(scale, *refs), out_shape=jax.S...  6.66 us
  transfers between devices with their start and end apart: 31, of which 14 were waited for; matrix products, arithmetic and copies ran while one was open for 1% of the time, Pallas kernels for 17%

profile of v5, /device:TPU:1, one launch (start us, length us, event | category | flops | bytes accessed | tf_op | source)
XLA Modules:
  0.0 190.4 jit_solution(15186348663550946013)
XLA Ops:
  0.1 8.7 %user_rows.5 = (f32[256,512]{1,0:T(8,128)S(1)}, f32[256,512]{1,0:T(8,128)S(1)}) custom-call(s32[8]{0:T(128)S(1)} %stack.23.refs_0_, bf16[2048,4096]{1,0:T(8,128)(2,1)} %refs_3_.7, bf16[2048,4096]{1,0:T(8,128)(2,1)} %refs_3_.7, f32[4096,256]{1,0:T(8,128)} %refs_3_.4), custom_call_target="tpu_custom_call" | custom-call | tf_op jit(solution)/shard_map/user_rows/pallas_call | solution.py:93
  13.5 6.3 %user_rows.4 = f32[256,512]{1,0:T(8,128)S(1)} custom-call(s32[8]{0:T(128)S(1)} %stack.23.refs_0_, bf16[2048,4096]{1,0:T(8,128)(2,1)} %refs_3_.7, f32[4096,256]{1,0:T(8,128)} %refs_3_.4), custom_call_target="tpu_custom_call" | custom-call | tf_op jit(solution)/shard_map/user_rows/pallas_call | solution.py:93
  21.1 6.3 %user_rows.3 = f32[256,512]{1,0:T(8,128)S(1)} custom-call(s32[8]{0:T(128)S(1)} %stack.23.refs_0_, bf16[2048,4096]{1,0:T(8,128)(2,1)} %refs_3_.7, f32[4096,256]{1,0:T(8,128)} %refs_3_.4), custom_call_target="tpu_custom_call" | custom-call | tf_op jit(solution)/shard_map/user_rows/pallas_call | solution.py:93
  27.4 9.8 %collective-permute-done = f32[256,512]{1,0:T(8,128)S(1)} collective-permute-done((f32[256,512]{1,0:T(8,128)S(1)}, f32[256,512]{1,0:T(8,128)S(1)}, u32[]{:S(2)}, u32[]{:S(2)}) %collective-permute-start) | collective-permute-done | bytes 524320 | tf_op jit(solution)/shard_map/ppermute | solution.py:53
  40.2 10.5 %collective-permute-done.3.refs_1_ = f32[256,512]{1,0:T(8,128)S(1)} collective-permute-done((f32[256,512]{1,0:T(8,128)S(1)}, f32[256,512]{1,0:T(8,128)S(1)}, u32[]{:S(2)}, u32[]{:S(2)}) %collective-permute-start.3) | collective-permute-done | bytes 524320 | tf_op jit(solution)/shard_map/ppermute | solution.py:53
  50.8 2.7 %collective-permute-start.6 = (f32[128,512]{1,0:T(8,128)S(1)}, f32[128,512]{1,0:T(8,128)S(1)}, u32[]{:S(2)}, u32[]{:S(2)}) collective-permute-start(f32[128,512]{1,0:T(8,128)S(1)} %slice.17), channel_id=1, source_target_pairs={{0,96},{32,0},{64,32},{96,64},{1,97},{33,1},{65,33},{97,65},{2,98}... | collective-permute-start | bytes 786440 | tf_op jit(solution)/shard_map/ppermute | solution.py:53
  53.5 5.5 %item_columns.4.refs_5_ = f32[8,256,512]{2,1,0:T(8,128)S(1)} custom-call(s32[8]{0:T(128)S(1)} %stack.23.refs_0_, f32[256,512]{1,0:T(8,128)S(1)} %add_add_fusion.1.refs_1_, bf16[2048,4096]{1,0:T(8,128)(2,1)} %refs_3_.7), custom_call_target="tpu_custom_call" | custom-call | tf_op jit(solution)/shard_map/item_columns/pallas_call | solution.py:161
  59.0 8.1 %item_columns.5 = (f32[4,256,512]{2,1,0:T(8,128)S(1)}, f32[4,256,512]{2,1,0:T(8,128)S(1)}) custom-call(s32[8]{0:T(128)S(1)} %stack.23.refs_0_, f32[256,512]{1,0:T(8,128)S(1)} %collective-permute-done.3.refs_1_, f32[256,512]{1,0:T(8,128)S(1)} %collective-permute-done.5.refs_2_, bf16[2048,4096]{1,0:T(8,128)(2,1)} %refs_3_.7, bf16[2048,4096]{1,0:T(8,128)(2,1)} %refs_3_.7, ...), custom_call_target="tpu_custom_call" | custom-call | tf_op jit(solution)/shard_map/item_columns/pallas_call | solution.py:161
  67.1 4.6 %item_columns.7 = f32[4,256,512]{2,1,0:T(8,128)} custom-call(s32[8]{0:T(128)S(1)} %stack.23.refs_0_, f32[128,512]{1,0:T(8,128)S(1)} %collective-permute-done.4.refs_1_, f32[128,512]{1,0:T(8,128)S(1)} %collective-permute-done.6.refs_2_, bf16[2048,4096]{1,0:T(8,128)(2,1)} %refs_3_.7, f32[4,256,512]{2,1,0:T(8,128)S(1)} %get-tuple-element.21.refs_4_), custom_call_target="tpu_custom_call" | custom-call | tf_op jit(solution)/shard_map/item_columns/pallas_call | solution.py:161
  71.8 3.0 %collective-permute-start.7 = (f32[4,256,512]{2,1,0:T(8,128)}, f32[4,256,512]{2,1,0:T(8,128)}, u32[]{:S(2)}, u32[]{:S(2)}) collective-permute-start(f32[4,256,512]{2,1,0:T(8,128)} %item_columns.7), channel_id=1, source_target_pairs={{0,1},{1,0},{2,3},{3,2},{4,5},{5,4},{6,7},{7,6},{8,9},{9,8},{10,11... | collective-permute-start | bytes 6291464 | tf_op jit(solution)/shard_map/ppermute | solution.py:54
  76.3 3.6 %item_columns.6 = f32[4,256,512]{2,1,0:T(8,128)S(1)} custom-call(s32[8]{0:T(128)S(1)} %stack.23.refs_0_, f32[128,512]{1,0:T(8,128)S(1)} %collective-permute-done.4.refs_1_, f32[128,512]{1,0:T(8,128)S(1)} %collective-permute-done.6.refs_2_, bf16[2048,4096]{1,0:T(8,128)(2,1)} %refs_3_.7, f32[4,256,512]{2,1,0:T(8,128)S(1)} %copy-done.1), custom_call_target="tpu_custom_call" | custom-call | tf_op jit(solution)/shard_map/item_columns/pallas_call | solution.py:161
  84.2 2.8 %collective-permute-start.10 = (f32[256,512]{1,0:T(8,128)}, f32[256,512]{1,0:T(8,128)S(1)}, u32[]{:S(2)}, u32[]{:S(2)}) collective-permute-start(f32[256,512]{1,0:T(8,128)} %get-tuple-element.28), channel_id=1, source_target_pairs={{0,6},{1,25},{2,0},{3,27},{4,2},{5,29},{6,4},{7,31},{8,14},{9,1},{... | collective-permute-start | bytes 1572872 | tf_op jit(solution)/shard_map/ppermute | solution.py:54
  89.8 9.3 %collective-permute-done.10 = f32[256,512]{1,0:T(8,128)S(1)} collective-permute-done((f32[256,512]{1,0:T(8,128)}, f32[256,512]{1,0:T(8,128)S(1)}, u32[]{:S(2)}, u32[]{:S(2)}) %collective-permute-start.10) | collective-permute-done | bytes 524320 | tf_op jit(solution)/shard_map/ppermute | solution.py:54
  99.0 3.3 %collective-permute-done.9 = f32[256,512]{1,0:T(8,128)S(1)} collective-permute-done((f32[256,512]{1,0:T(8,128)}, f32[256,512]{1,0:T(8,128)S(1)}, u32[]{:S(2)}, u32[]{:S(2)}) %collective-permute-start.9) | collective-permute-done | bytes 524320 | tf_op jit(solution)/shard_map/ppermute | solution.py:54
  110.1 3.5 %collective-permute-done.11 = f32[256,512]{1,0:T(8,128)S(1)} collective-permute-done((f32[256,512]{1,0:T(8,128)S(1)}, f32[256,512]{1,0:T(8,128)S(1)}, u32[]{:S(2)}, u32[]{:S(2)}) %collective-permute-start.11) | collective-permute-done | bytes 524320 | tf_op jit(solution)/shard_map/ppermute | solution.py:54
  113.6 5.6 %collective-permute-done.12 = f32[256,512]{1,0:T(8,128)S(1)} collective-permute-done((f32[256,512]{1,0:T(8,128)S(1)}, f32[256,512]{1,0:T(8,128)S(1)}, u32[]{:S(2)}, u32[]{:S(2)}) %collective-permute-start.12) | collective-permute-done | bytes 524320 | tf_op jit(solution)/shard_map/ppermute | solution.py:54
  119.5 2.7 %collective-permute-start.16 = (f32[256,512]{1,0:T(8,128)S(1)}, f32[256,512]{1,0:T(8,128)S(1)}, u32[]{:S(2)}, u32[]{:S(2)}) collective-permute-start(f32[256,512]{1,0:T(8,128)S(1)} %bitcast_add_fusion.refs_0_), channel_id=1, source_target_pairs={{0,6},{1,25},{2,0},{3,27},{4,2},{5,29},{6,4},{7,31},{8,14},{9,1},{... | collective-permute-start | bytes 1572872 | tf_op jit(solution)/shard_map/ppermute | solution.py:54
  122.2 2.7 %collective-permute-start.14 = (f32[256,512]{1,0:T(8,128)S(1)}, f32[256,512]{1,0:T(8,128)S(1)}, u32[]{:S(2)}, u32[]{:S(2)}) collective-permute-start(f32[256,512]{1,0:T(8,128)S(1)} %bitcast_add_fusion.refs_0_), channel_id=1, source_target_pairs={{0,1},{1,0},{2,3},{3,2},{4,5},{5,4},{6,7},{7,6},{8,9},{9,8},{10,11... | collective-permute-start | bytes 1572872 | tf_op jit(solution)/shard_map/ppermute | solution.py:54
  124.9 4.2 %collective-permute-done.15.refs_0_.refs_1_ = f32[256,512]{1,0:T(8,128)S(1)} collective-permute-done((f32[256,512]{1,0:T(8,128)S(1)}, f32[256,512]{1,0:T(8,128)S(1)}, u32[]{:S(2)}, u32[]{:S(2)}) %collective-permute-start.15) | collective-permute-done | bytes 524320 | tf_op jit(solution)/shard_map/ppermute | solution.py:54
  129.2 3.0 %collective-permute-start.17 = (f32[256,512]{1,0:T(8,128)S(1)}, f32[256,512]{1,0:T(8,128)S(1)}, u32[]{:S(2)}, u32[]{:S(2)}) collective-permute-start(f32[256,512]{1,0:T(8,128)S(1)} %collective-permute-done.15.refs_0_.refs_1_), channel_id=1, source_target_pairs={{0,1},{1,0},{2,3},{3,2},{4,5},{5,4},{6,7},{7,6},{8,9},{9,8},{10,11... | collective-permute-start | bytes 1572872 | tf_op jit(solution)/shard_map/ppermute | solution.py:54
  135.6 4.1 %collective-permute-start.21 = (f32[128,512]{1,0:T(8,128)S(1)}, f32[128,512]{1,0:T(8,128)}, u32[]{:S(2)}, u32[]{:S(2)}) collective-permute-start(f32[128,512]{1,0:T(8,128)S(1)} %collective-permute-done.19.refs_0_.refs_3_), channel_id=1, source_target_pairs={{0,1},{1,0},{2,3},{3,2},{4,5},{5,4},{6,7},{7,6},{8,9},{9,8},{10,11... | collective-permute-start | bytes 786440 | tf_op jit(solution)/shard_map/ppermute | solution.py:54
  147.9 2.8 %collective-permute-done.23 = f32[192,128]{1,0:T(8,128)S(1)} collective-permute-done((f32[192,128]{1,0:T(8,128)S(1)}, f32[192,128]{1,0:T(8,128)S(1)}, u32[]{:S(2)}, u32[]{:S(2)}) %collective-permute-start.23) | collective-permute-done | bytes 98336 | tf_op jit(solution)/shard_map/ppermute | solution.py:53
  155.1 18.5 %first_sweep.1 = (f32[8,256,512]{2,1,0:T(8,128)S(1)}, f32[192,128]{1,0:T(8,128)S(1)}) custom-call(s32[1]{0:T(128)} %bitcast.core_ref.refs_0_, s32[8]{0:T(128)S(1)} %pad_add_fusion.slot_ref, f32[192,128]{1,0:T(8,128)S(1)} %add_add_fusion.3.mine_ref, f32[192,128]{1,0:T(8,128)S(1)} %collective-permute-done.26.other_ref, ...), custom_call_target="tpu_custom_call" | custom-call | tf_op jit(solution)/shard_map/first_sweep/pallas_call | solution.py:368
  183.7 6.7 %second_sweep.1 = f32[4096,256]{1,0:T(8,128)} custom-call(s32[1]{0:T(128)} %bitcast.core_ref.refs_0_, f32[192,128]{1,0:T(8,128)S(1)} %add_add_fusion.2.refs_1_, f32[192,128]{1,0:T(8,128)S(1)} %collective-permute-done.30.refs_2_, f32[8,256,512]{2,1,0:T(8,128)S(1)} %get-tuple-element.30.refs_3_), custom_call_target="tpu_custom_call" | custom-call | tf_op jit(solution)/shard_map/second_sweep/pallas_call | solution.py:396
  (73 shorter events, 52.1 us)
Async XLA Ops:
  8.8 18.6 %collective-permute-start.1 = (f32[256,512]{1,0:T(8,128)S(1)}, f32[256,512]{1,0:T(8,128)S(1)}, u32[]{:S(2)}, u32[]{:S(2)}) collective-permute-start(f32[256,512]{1,0:T(8,128)S(1)} %get-tuple-element.18), channel_id=1, source_target_pairs={{0,32},{32,64},{64,96},{96,0},{1,33},{33,65},{65,97},{97,1},{2,34}... | collective-permute-start | bytes 1572872 | tf_op jit(solution)/shard_map/ppermute | solution.py:53
  11.3 16.1 %collective-permute-start.2 = (f32[256,512]{1,0:T(8,128)S(1)}, f32[256,512]{1,0:T(8,128)S(1)}, u32[]{:S(2)}, u32[]{:S(2)}) collective-permute-start(f32[256,512]{1,0:T(8,128)S(1)} %get-tuple-element.19), channel_id=1, source_target_pairs={{0,96},{32,0},{64,32},{96,64},{1,97},{33,1},{65,33},{97,65},{2,98}... | collective-permute-start | bytes 1572872 | tf_op jit(solution)/shard_map/ppermute | solution.py:53
  19.8 17.4 %collective-permute-start = (f32[256,512]{1,0:T(8,128)S(1)}, f32[256,512]{1,0:T(8,128)S(1)}, u32[]{:S(2)}, u32[]{:S(2)}) collective-permute-start(f32[256,512]{1,0:T(8,128)S(1)} %user_rows.4), channel_id=1, source_target_pairs={{0,64},{32,96},{64,0},{96,32},{1,65},{33,97},{65,1},{97,33},{2,66}... | collective-permute-start | bytes 1572872 | tf_op jit(solution)/shard_map/ppermute | solution.py:53
  37.4 13.2 %collective-permute-start.3 = (f32[256,512]{1,0:T(8,128)S(1)}, f32[256,512]{1,0:T(8,128)S(1)}, u32[]{:S(2)}, u32[]{:S(2)}) collective-permute-start(f32[256,512]{1,0:T(8,128)S(1)} %add_add_fusion.1.refs_1_), channel_id=1, source_target_pairs={{0,32},{32,64},{64,96},{96,0},{1,33},{33,65},{65,97},{97,1},{2,34}... | collective-permute-start | bytes 1572872 | tf_op jit(solution)/shard_map/ppermute | solution.py:53
  38.1 12.7 %collective-permute-start.5 = (f32[256,512]{1,0:T(8,128)S(1)}, f32[256,512]{1,0:T(8,128)S(1)}, u32[]{:S(2)}, u32[]{:S(2)}) collective-permute-start(f32[256,512]{1,0:T(8,128)S(1)} %add_add_fusion.1.refs_1_), channel_id=1, source_target_pairs={{0,96},{32,0},{64,32},{96,64},{1,97},{33,1},{65,33},{97,65},{2,98}... | collective-permute-start | bytes 1572872 | tf_op jit(solution)/shard_map/ppermute | solution.py:53
  50.7 16.4 %collective-permute-start.4 = (f32[128,512]{1,0:T(8,128)S(1)}, f32[128,512]{1,0:T(8,128)S(1)}, u32[]{:S(2)}, u32[]{:S(2)}) collective-permute-start(f32[128,512]{1,0:T(8,128)S(1)} %slice.16), channel_id=1, source_target_pairs={{0,32},{32,64},{64,96},{96,0},{1,33},{33,65},{65,97},{97,1},{2,34}... | collective-permute-start | bytes 786440 | tf_op jit(solution)/shard_map/ppermute | solution.py:53
  50.8 16.3 %collective-permute-start.6 = (f32[128,512]{1,0:T(8,128)S(1)}, f32[128,512]{1,0:T(8,128)S(1)}, u32[]{:S(2)}, u32[]{:S(2)}) collective-permute-start(f32[128,512]{1,0:T(8,128)S(1)} %slice.17), channel_id=1, source_target_pairs={{0,96},{32,0},{64,32},{96,64},{1,97},{33,1},{65,33},{97,65},{2,98}... | collective-permute-start | bytes 786440 | tf_op jit(solution)/shard_map/ppermute | solution.py:53
  71.8 8.1 %collective-permute-start.7 = (f32[4,256,512]{2,1,0:T(8,128)}, f32[4,256,512]{2,1,0:T(8,128)}, u32[]{:S(2)}, u32[]{:S(2)}) collective-permute-start(f32[4,256,512]{2,1,0:T(8,128)} %item_columns.7), channel_id=1, source_target_pairs={{0,1},{1,0},{2,3},{3,2},{4,5},{5,4},{6,7},{7,6},{8,9},{9,8},{10,11... | collective-permute-start | bytes 6291464 | tf_op jit(solution)/shard_map/ppermute | solution.py:54
  84.2 14.8 %collective-permute-start.10 = (f32[256,512]{1,0:T(8,128)}, f32[256,512]{1,0:T(8,128)S(1)}, u32[]{:S(2)}, u32[]{:S(2)}) collective-permute-start(f32[256,512]{1,0:T(8,128)} %get-tuple-element.28), channel_id=1, source_target_pairs={{0,6},{1,25},{2,0},{3,27},{4,2},{5,29},{6,4},{7,31},{8,14},{9,1},{... | collective-permute-start | bytes 1572872 | tf_op jit(solution)/shard_map/ppermute | solution.py:54
  87.0 15.4 %collective-permute-start.9 = (f32[256,512]{1,0:T(8,128)}, f32[256,512]{1,0:T(8,128)S(1)}, u32[]{:S(2)}, u32[]{:S(2)}) collective-permute-start(f32[256,512]{1,0:T(8,128)} %get-tuple-element.27), channel_id=1, source_target_pairs={{0,2},{1,9},{2,4},{3,11},{4,6},{5,13},{6,0},{7,15},{8,10},{9,17},{... | collective-permute-start | bytes 1572872 | tf_op jit(solution)/shard_map/ppermute | solution.py:54
  87.0 15.4 %collective-permute-start.8 = (f32[256,512]{1,0:T(8,128)}, f32[256,512]{1,0:T(8,128)}, u32[]{:S(2)}, u32[]{:S(2)}) collective-permute-start(f32[256,512]{1,0:T(8,128)} %add_bitcast_fusion.3), channel_id=1, source_target_pairs={{0,4},{1,17},{2,6},{3,19},{4,0},{5,21},{6,2},{7,23},{8,12},{9,25},... | collective-permute-start | bytes 1572872 | tf_op jit(solution)/shard_map/ppermute | solution.py:54
  103.6 10.0 %collective-permute-start.11 = (f32[256,512]{1,0:T(8,128)S(1)}, f32[256,512]{1,0:T(8,128)S(1)}, u32[]{:S(2)}, u32[]{:S(2)}) collective-permute-start(f32[256,512]{1,0:T(8,128)S(1)} %add_add_fusion), channel_id=1, source_target_pairs={{0,16},{1,5},{2,18},{3,7},{4,20},{5,1},{6,22},{7,3},{8,24},{9,13},... | collective-permute-start | bytes 1572872 | tf_op jit(solution)/shard_map/ppermute | solution.py:54
  106.2 13.0 %collective-permute-start.12 = (f32[256,512]{1,0:T(8,128)S(1)}, f32[256,512]{1,0:T(8,128)S(1)}, u32[]{:S(2)}, u32[]{:S(2)}) collective-permute-start(f32[256,512]{1,0:T(8,128)S(1)} %add_add_fusion), channel_id=1, source_target_pairs={{0,8},{1,3},{2,10},{3,5},{4,12},{5,7},{6,14},{7,1},{8,16},{9,11},{... | collective-permute-start | bytes 1572872 | tf_op jit(solution)/shard_map/ppermute | solution.py:54
  106.5 12.7 %collective-permute-start.13 = (f32[256,512]{1,0:T(8,128)S(1)}, f32[256,512]{1,0:T(8,128)S(1)}, u32[]{:S(2)}, u32[]{:S(2)}) collective-permute-start(f32[256,512]{1,0:T(8,128)S(1)} %add_add_fusion), channel_id=1, source_target_pairs={{0,24},{1,7},{2,26},{3,1},{4,28},{5,3},{6,30},{7,5},{8,0},{9,15},{... | collective-permute-start | bytes 1572872 | tf_op jit(solution)/shard_map/ppermute | solution.py:54
  119.5 9.6 %collective-permute-start.15 = (f32[256,512]{1,0:T(8,128)S(1)}, f32[256,512]{1,0:T(8,128)S(1)}, u32[]{:S(2)}, u32[]{:S(2)}) collective-permute-start(f32[256,512]{1,0:T(8,128)S(1)} %bitcast_add_fusion.refs_0_), channel_id=1, source_target_pairs={{0,2},{1,9},{2,4},{3,11},{4,6},{5,13},{6,0},{7,15},{8,10},{9,17},{... | collective-permute-start | bytes 1572872 | tf_op jit(solution)/shard_map/ppermute | solution.py:54
  119.5 12.7 %collective-permute-start.16 = (f32[256,512]{1,0:T(8,128)S(1)}, f32[256,512]{1,0:T(8,128)S(1)}, u32[]{:S(2)}, u32[]{:S(2)}) collective-permute-start(f32[256,512]{1,0:T(8,128)S(1)} %bitcast_add_fusion.refs_0_), channel_id=1, source_target_pairs={{0,6},{1,25},{2,0},{3,27},{4,2},{5,29},{6,4},{7,31},{8,14},{9,1},{... | collective-permute-start | bytes 1572872 | tf_op jit(solution)/shard_map/ppermute | solution.py:54
  122.2 17.6 %collective-permute-start.14 = (f32[256,512]{1,0:T(8,128)S(1)}, f32[256,512]{1,0:T(8,128)S(1)}, u32[]{:S(2)}, u32[]{:S(2)}) collective-permute-start(f32[256,512]{1,0:T(8,128)S(1)} %bitcast_add_fusion.refs_0_), channel_id=1, source_target_pairs={{0,1},{1,0},{2,3},{3,2},{4,5},{5,4},{6,7},{7,6},{8,9},{9,8},{10,11... | collective-permute-start | bytes 1572872 | tf_op jit(solution)/shard_map/ppermute | solution.py:54
  129.2 11.7 %collective-permute-start.17 = (f32[256,512]{1,0:T(8,128)S(1)}, f32[256,512]{1,0:T(8,128)S(1)}, u32[]{:S(2)}, u32[]{:S(2)}) collective-permute-start(f32[256,512]{1,0:T(8,128)S(1)} %collective-permute-done.15.refs_0_.refs_1_), channel_id=1, source_target_pairs={{0,1},{1,0},{2,3},{3,2},{4,5},{5,4},{6,7},{7,6},{8,9},{9,8},{10,11... | collective-permute-start | bytes 1572872 | tf_op jit(solution)/shard_map/ppermute | solution.py:54
  132.2 8.7 %collective-permute-start.18 = (f32[256,512]{1,0:T(8,128)S(1)}, f32[256,512]{1,0:T(8,128)S(1)}, u32[]{:S(2)}, u32[]{:S(2)}) collective-permute-start(f32[256,512]{1,0:T(8,128)S(1)} %collective-permute-done.16.refs_1_.refs_2_), channel_id=1, source_target_pairs={{0,1},{1,0},{2,3},{3,2},{4,5},{5,4},{6,7},{7,6},{8,9},{9,8},{10,11... | collective-permute-start | bytes 1572872 | tf_op jit(solution)/shard_map/ppermute | solution.py:54
  132.3 7.4 %collective-permute-start.20 = (f32[128,512]{1,0:T(8,128)S(1)}, f32[128,512]{1,0:T(8,128)}, u32[]{:S(2)}, u32[]{:S(2)}) collective-permute-start(f32[128,512]{1,0:T(8,128)S(1)} %slice.19), channel_id=1, source_target_pairs={{0,6},{1,25},{2,0},{3,27},{4,2},{5,29},{6,4},{7,31},{8,14},{9,1},{... | collective-permute-start | bytes 786440 | tf_op jit(solution)/shard_map/ppermute | solution.py:54
  135.6 7.2 %collective-permute-start.21 = (f32[128,512]{1,0:T(8,128)S(1)}, f32[128,512]{1,0:T(8,128)}, u32[]{:S(2)}, u32[]{:S(2)}) collective-permute-start(f32[128,512]{1,0:T(8,128)S(1)} %collective-permute-done.19.refs_0_.refs_3_), channel_id=1, source_target_pairs={{0,1},{1,0},{2,3},{3,2},{4,5},{5,4},{6,7},{7,6},{8,9},{9,8},{10,11... | collective-permute-start | bytes 786440 | tf_op jit(solution)/shard_map/ppermute | solution.py:54
  145.2 7.9 %collective-permute-start.24 = (f32[192,128]{1,0:T(8,128)S(1)}, f32[192,128]{1,0:T(8,128)S(1)}, u32[]{:S(2)}, u32[]{:S(2)}) collective-permute-start(f32[192,128]{1,0:T(8,128)S(1)} %last_grams.1), channel_id=1, source_target_pairs={{0,32},{32,64},{64,96},{96,0},{1,33},{33,65},{65,97},{97,1},{2,34}... | collective-permute-start | bytes 294920 | tf_op jit(solution)/shard_map/ppermute | solution.py:53
  145.5 7.6 %collective-permute-start.25 = (f32[192,128]{1,0:T(8,128)S(1)}, f32[192,128]{1,0:T(8,128)S(1)}, u32[]{:S(2)}, u32[]{:S(2)}) collective-permute-start(f32[192,128]{1,0:T(8,128)S(1)} %last_grams.1), channel_id=1, source_target_pairs={{0,96},{32,0},{64,32},{96,64},{1,97},{33,1},{65,33},{97,65},{2,98}... | collective-permute-start | bytes 294920 | tf_op jit(solution)/shard_map/ppermute | solution.py:53
  173.9 8.0 %collective-permute-start.28 = (f32[192,128]{1,0:T(8,128)S(1)}, f32[192,128]{1,0:T(8,128)S(1)}, u32[]{:S(2)}, u32[]{:S(2)}) collective-permute-start(f32[192,128]{1,0:T(8,128)S(1)} %get-tuple-element.29), channel_id=1, source_target_pairs={{0,32},{32,64},{64,96},{96,0},{1,33},{33,65},{65,97},{97,1},{2,34}... | collective-permute-start | bytes 294920 | tf_op jit(solution)/shard_map/ppermute | solution.py:53
  (10 other events, 44.9 us)

commit v6 on v5

--- a/solution.py
+++ b/solution.py
@@ -318,12 +318,12 @@
     return pl.pallas_call(
         last_grams_kernel,
         out_shape=packed(rank),
-        in_specs=[smem] + [hbm] * 2 + [vmem] * 4,
+        in_specs=[smem] + [pl.BlockSpec(memory_space=pltpu.HBM)] * 2 + [vmem] * 4,
         out_specs=vmem,
         scratch_shapes=[pltpu.VMEM((2, 2, rank, rank), f32), pltpu.SemaphoreType.DMA((2,))],
         name="last_grams",
         compiler_params=room(24),
-    )(core, own, sides, *near[3:], *far[3:])
+    )(core, *(pltpu.with_memory_space_constraint(g, pltpu.HBM) for g in (own, sides)), *near[3:], *far[3:])
 
 
 def whole_gram(core_ref, mine_ref, other_ref, gram):
@@ -431,6 +431,7 @@
     total = item_columns(place, 3, [own], interactions)
     sent, kept = item_columns(place, 4, [one, three], interactions, total, parts=2)
     away = shift(item_columns(place, 6, two, interactions, sent, 0, splits=2), "core")
+    kept = pltpu.with_memory_space_constraint(kept, pltpu.HBM)
     kept = item_columns(place, 6, two, interactions, kept, 1, splits=2)
 
     def block_at(d, halves):
@@ -440,10 +441,7 @@
     two, *halves = lax.optimization_barrier((two, kept, away))
     two = shift(two, "first", 2)
     one, three = block_at(1, halves), block_at(3, halves)
-    one, three, *halves = lax.optimization_barrier((one, three, *halves))
-    one, three = shift(one, "first", 1), shift(three, "first", 3)
-    block = lax.optimization_barrier(block_at(0, halves))
-    block = of_ring(block, one, three, two)
+    block = of_ring(block_at(0, halves), shift(one, "first", 1), shift(three, "first", 3), two)
     own_omega = lax.dynamic_slice_in_dim(omega, (core * side + a) * width, width, 0)
     block = of_ring(*from_ring(block, "second")) + ridge * own_omega.T
 

time: 191 us -> 192 us (level)
    add x3 -> x2, other arithmetic: 5.44 us -> 3.5 us  [block_at(): sum((lax.dynamic_index_in_dim(h, (a + d) % side, 0, False) for h in halves))]
  transfers between devices with their start and end apart: 31 -> 31, of which waited for: 14 -> 15; matrix products, arithmetic and copies ran while one was open for 1% -> 1% of each run, Pallas kernels for 17% -> 17%
where the time goes in v6:
time: 192 us
  Pallas kernels  74.3 us (39%)
  waiting for transfers between devices  59.9 us (31%)
  starting transfers between devices  48.3 us (25%)
  other arithmetic  5.96 us (3%)
  local copies, waits for them, and re-layouts  3.02 us (2%)
    ppermute x18, starting transfers between devices, shift(): return lax.ppermute(a, 'user', pairs_of(axis, step))  30.9 us
    ppermute x13, waiting for transfers between devices, shift(): lax.ppermute(a, 'item', [(i, (i + step) % side) for i in range(side)])  30.7 us
    ppermute x18, waiting for transfers between devices, shift(): return lax.ppermute(a, 'user', pairs_of(axis, step))  29.2 us
    pallas_call x4, Pallas kernels, item_columns(): pl.pallas_call(lambda *refs: columns_kernel(count, splits, total is not N...  22.1 us
    pallas_call x3, Pallas kernels, user_rows(): pl.pallas_call(lambda *refs: rows_kernel(count, *refs), out_shape=(jax.Sh...  21.3 us
    pallas_call x1, Pallas kernels, first_sweep(): pl.pallas_call(first_kernel, out_shape=(jax.ShapeDtypeStruct((8, rank, wi...  18.5 us
    ppermute x13, starting transfers between devices, shift(): lax.ppermute(a, 'item', [(i, (i + step) % side) for i in range(side)])  17.4 us
    pallas_call x1, Pallas kernels, second_sweep(): pl.pallas_call(lambda *refs: second_kernel(scale, *refs), out_shape=jax.S...  6.66 us
  transfers between devices with their start and end apart: 31, of which 15 were waited for; matrix products, arithmetic and copies ran while one was open for 1% of the time, Pallas kernels for 17%

profile of v6, /device:TPU:1, one launch (start us, length us, event | category | flops | bytes accessed | tf_op | source)
XLA Modules:
  0.0 191.7 jit_solution(9481021163248870487)
XLA Ops:
  0.1 8.7 %user_rows.5 = (f32[256,512]{1,0:T(8,128)S(1)}, f32[256,512]{1,0:T(8,128)S(1)}) custom-call(s32[8]{0:T(128)S(1)} %stack.23.refs_0_, bf16[2048,4096]{1,0:T(8,128)(2,1)} %refs_3_.7, bf16[2048,4096]{1,0:T(8,128)(2,1)} %refs_3_.7, f32[4096,256]{1,0:T(8,128)} %refs_3_.4), custom_call_target="tpu_custom_call" | custom-call | tf_op jit(solution)/shard_map/user_rows/pallas_call | solution.py:93
  13.5 6.3 %user_rows.4 = f32[256,512]{1,0:T(8,128)S(1)} custom-call(s32[8]{0:T(128)S(1)} %stack.23.refs_0_, bf16[2048,4096]{1,0:T(8,128)(2,1)} %refs_3_.7, f32[4096,256]{1,0:T(8,128)} %refs_3_.4), custom_call_target="tpu_custom_call" | custom-call | tf_op jit(solution)/shard_map/user_rows/pallas_call | solution.py:93
  21.1 6.3 %user_rows.3 = f32[256,512]{1,0:T(8,128)S(1)} custom-call(s32[8]{0:T(128)S(1)} %stack.23.refs_0_, bf16[2048,4096]{1,0:T(8,128)(2,1)} %refs_3_.7, f32[4096,256]{1,0:T(8,128)} %refs_3_.4), custom_call_target="tpu_custom_call" | custom-call | tf_op jit(solution)/shard_map/user_rows/pallas_call | solution.py:93
  27.4 9.8 %collective-permute-done = f32[256,512]{1,0:T(8,128)S(1)} collective-permute-done((f32[256,512]{1,0:T(8,128)S(1)}, f32[256,512]{1,0:T(8,128)S(1)}, u32[]{:S(2)}, u32[]{:S(2)}) %collective-permute-start) | collective-permute-done | bytes 524320 | tf_op jit(solution)/shard_map/ppermute | solution.py:53
  40.2 10.5 %collective-permute-done.3.refs_1_ = f32[256,512]{1,0:T(8,128)S(1)} collective-permute-done((f32[256,512]{1,0:T(8,128)S(1)}, f32[256,512]{1,0:T(8,128)S(1)}, u32[]{:S(2)}, u32[]{:S(2)}) %collective-permute-start.3) | collective-permute-done | bytes 524320 | tf_op jit(solution)/shard_map/ppermute | solution.py:53
  50.8 2.7 %collective-permute-start.6 = (f32[128,512]{1,0:T(8,128)S(1)}, f32[128,512]{1,0:T(8,128)S(1)}, u32[]{:S(2)}, u32[]{:S(2)}) collective-permute-start(f32[128,512]{1,0:T(8,128)S(1)} %slice.17), channel_id=1, source_target_pairs={{0,96},{32,0},{64,32},{96,64},{1,97},{33,1},{65,33},{97,65},{2,98}... | collective-permute-start | bytes 786440 | tf_op jit(solution)/shard_map/ppermute | solution.py:53
  53.5 5.5 %item_columns.4.refs_5_ = f32[8,256,512]{2,1,0:T(8,128)S(1)} custom-call(s32[8]{0:T(128)S(1)} %stack.23.refs_0_, f32[256,512]{1,0:T(8,128)S(1)} %add_add_fusion.refs_1_, bf16[2048,4096]{1,0:T(8,128)(2,1)} %refs_3_.7), custom_call_target="tpu_custom_call" | custom-call | tf_op jit(solution)/shard_map/item_columns/pallas_call | solution.py:161
  59.0 8.1 %item_columns.5 = (f32[4,256,512]{2,1,0:T(8,128)S(1)}, f32[4,256,512]{2,1,0:T(8,128)S(1)}) custom-call(s32[8]{0:T(128)S(1)} %stack.23.refs_0_, f32[256,512]{1,0:T(8,128)S(1)} %collective-permute-done.3.refs_1_, f32[256,512]{1,0:T(8,128)S(1)} %collective-permute-done.5.refs_2_, bf16[2048,4096]{1,0:T(8,128)(2,1)} %refs_3_.7, bf16[2048,4096]{1,0:T(8,128)(2,1)} %refs_3_.7, ...), custom_call_target="tpu_custom_call" | custom-call | tf_op jit(solution)/shard_map/item_columns/pallas_call | solution.py:161
  67.1 4.6 %item_columns.7 = f32[4,256,512]{2,1,0:T(8,128)} custom-call(s32[8]{0:T(128)S(1)} %stack.23.refs_0_, f32[128,512]{1,0:T(8,128)S(1)} %collective-permute-done.4.refs_1_, f32[128,512]{1,0:T(8,128)S(1)} %collective-permute-done.6.refs_2_, bf16[2048,4096]{1,0:T(8,128)(2,1)} %refs_3_.7, f32[4,256,512]{2,1,0:T(8,128)S(1)} %get-tuple-element.17.refs_4_), custom_call_target="tpu_custom_call" | custom-call | tf_op jit(solution)/shard_map/item_columns/pallas_call | solution.py:161
  71.8 3.0 %collective-permute-start.7 = (f32[4,256,512]{2,1,0:T(8,128)}, f32[4,256,512]{2,1,0:T(8,128)}, u32[]{:S(2)}, u32[]{:S(2)}) collective-permute-start(f32[4,256,512]{2,1,0:T(8,128)} %item_columns.7), channel_id=1, source_target_pairs={{0,1},{1,0},{2,3},{3,2},{4,5},{5,4},{6,7},{7,6},{8,9},{9,8},{10,11... | collective-permute-start | bytes 6291464 | tf_op jit(solution)/shard_map/ppermute | solution.py:54
  74.7 3.9 %item_columns.6 = f32[4,256,512]{2,1,0:T(8,128)S(1)} custom-call(s32[8]{0:T(128)S(1)} %stack.23.refs_0_, f32[128,512]{1,0:T(8,128)S(1)} %collective-permute-done.4.refs_1_, f32[128,512]{1,0:T(8,128)S(1)} %collective-permute-done.6.refs_2_, bf16[2048,4096]{1,0:T(8,128)(2,1)} %refs_3_.7, f32[4,256,512]{2,1,0:T(8,128)} %copy-done), custom_call_target="tpu_custom_call" | custom-call | tf_op jit(solution)/shard_map/item_columns/pallas_call | solution.py:161
  82.4 2.8 %collective-permute-start.10 = (f32[256,512]{1,0:T(8,128)}, f32[256,512]{1,0:T(8,128)S(1)}, u32[]{:S(2)}, u32[]{:S(2)}) collective-permute-start(f32[256,512]{1,0:T(8,128)} %get-tuple-element.23), channel_id=1, source_target_pairs={{0,6},{1,25},{2,0},{3,27},{4,2},{5,29},{6,4},{7,31},{8,14},{9,1},{... | collective-permute-start | bytes 1572872 | tf_op jit(solution)/shard_map/ppermute | solution.py:54
  86.8 10.4 %collective-permute-done.10 = f32[256,512]{1,0:T(8,128)S(1)} collective-permute-done((f32[256,512]{1,0:T(8,128)}, f32[256,512]{1,0:T(8,128)S(1)}, u32[]{:S(2)}, u32[]{:S(2)}) %collective-permute-start.10) | collective-permute-done | bytes 524320 | tf_op jit(solution)/shard_map/ppermute | solution.py:54
  97.2 3.4 %collective-permute-done.9 = f32[256,512]{1,0:T(8,128)} collective-permute-done((f32[256,512]{1,0:T(8,128)}, f32[256,512]{1,0:T(8,128)}, u32[]{:S(2)}, u32[]{:S(2)}) %collective-permute-start.9) | collective-permute-done | bytes 524320 | tf_op jit(solution)/shard_map/ppermute | solution.py:54
  108.9 3.5 %collective-permute-done.11 = f32[256,512]{1,0:T(8,128)S(1)} collective-permute-done((f32[256,512]{1,0:T(8,128)S(1)}, f32[256,512]{1,0:T(8,128)S(1)}, u32[]{:S(2)}, u32[]{:S(2)}) %collective-permute-start.11) | collective-permute-done | bytes 524320 | tf_op jit(solution)/shard_map/ppermute | solution.py:54
  112.4 5.6 %collective-permute-done.12 = f32[256,512]{1,0:T(8,128)S(1)} collective-permute-done((f32[256,512]{1,0:T(8,128)S(1)}, f32[256,512]{1,0:T(8,128)S(1)}, u32[]{:S(2)}, u32[]{:S(2)}) %collective-permute-start.12) | collective-permute-done | bytes 524320 | tf_op jit(solution)/shard_map/ppermute | solution.py:54
  121.0 3.0 %collective-permute-start.14 = (f32[256,512]{1,0:T(8,128)S(1)}, f32[256,512]{1,0:T(8,128)S(1)}, u32[]{:S(2)}, u32[]{:S(2)}) collective-permute-start(f32[256,512]{1,0:T(8,128)S(1)} %bitcast_add_fusion.refs_0_), channel_id=1, source_target_pairs={{0,1},{1,0},{2,3},{3,2},{4,5},{5,4},{6,7},{7,6},{8,9},{9,8},{10,11... | collective-permute-start | bytes 1572872 | tf_op jit(solution)/shard_map/ppermute | solution.py:54
  124.0 3.8 %collective-permute-done.15.refs_0_.refs_1_ = f32[256,512]{1,0:T(8,128)S(1)} collective-permute-done((f32[256,512]{1,0:T(8,128)S(1)}, f32[256,512]{1,0:T(8,128)S(1)}, u32[]{:S(2)}, u32[]{:S(2)}) %collective-permute-start.15) | collective-permute-done | bytes 524320 | tf_op jit(solution)/shard_map/ppermute | solution.py:54
  128.0 3.4 %collective-permute-start.17 = (f32[256,512]{1,0:T(8,128)S(1)}, f32[256,512]{1,0:T(8,128)S(1)}, u32[]{:S(2)}, u32[]{:S(2)}) collective-permute-start(f32[256,512]{1,0:T(8,128)S(1)} %collective-permute-done.15.refs_0_.refs_1_), channel_id=1, source_target_pairs={{0,1},{1,0},{2,3},{3,2},{4,5},{5,4},{6,7},{7,6},{8,9},{9,8},{10,11... | collective-permute-start | bytes 1572872 | tf_op jit(solution)/shard_map/ppermute | solution.py:54
  134.4 4.5 %collective-permute-start.21 = (f32[128,512]{1,0:T(8,128)S(1)}, f32[128,512]{1,0:T(8,128)}, u32[]{:S(2)}, u32[]{:S(2)}) collective-permute-start(f32[128,512]{1,0:T(8,128)S(1)} %collective-permute-done.19.refs_0_.refs_3_), channel_id=1, source_target_pairs={{0,1},{1,0},{2,3},{3,2},{4,5},{5,4},{6,7},{7,6},{8,9},{9,8},{10,11... | collective-permute-start | bytes 786440 | tf_op jit(solution)/shard_map/ppermute | solution.py:54
  143.5 2.9 %last_grams.1 = f32[192,128]{1,0:T(8,128)S(1)} custom-call(s32[1]{0:T(128)} %bitcast.core_ref.refs_0_, f32[2,256,256]{2,1,0:T(8,128)} %copy-done.1, f32[2,256,256]{2,1,0:T(8,128)} %copy-done.2, f32[128,512]{1,0:T(8,128)S(1)} %collective-permute-done.19.refs_0_.refs_3_, f32[128,512]{1,0:T(8,128)} %collective-permute-done.20.refs_1_.refs_4_, ...), custom_call_target="tpu_custom_call" | custom-call | tf_op jit(solution)/shard_map/last_grams/pallas_call | solution.py:318
  149.3 2.8 %collective-permute-done.23 = f32[192,128]{1,0:T(8,128)S(1)} collective-permute-done((f32[192,128]{1,0:T(8,128)S(1)}, f32[192,128]{1,0:T(8,128)S(1)}, u32[]{:S(2)}, u32[]{:S(2)}) %collective-permute-start.23) | collective-permute-done | bytes 98336 | tf_op jit(solution)/shard_map/ppermute | solution.py:53
  156.4 18.5 %first_sweep.1 = (f32[8,256,512]{2,1,0:T(8,128)S(1)}, f32[192,128]{1,0:T(8,128)S(1)}) custom-call(s32[1]{0:T(128)} %bitcast.core_ref.refs_0_, s32[8]{0:T(128)S(1)} %pad_add_fusion.slot_ref, f32[192,128]{1,0:T(8,128)S(1)} %add_add_fusion.2.mine_ref, f32[192,128]{1,0:T(8,128)S(1)} %collective-permute-done.26.other_ref, ...), custom_call_target="tpu_custom_call" | custom-call | tf_op jit(solution)/shard_map/first_sweep/pallas_call | solution.py:368
  185.0 6.7 %second_sweep.1 = f32[4096,256]{1,0:T(8,128)} custom-call(s32[1]{0:T(128)} %bitcast.core_ref.refs_0_, f32[192,128]{1,0:T(8,128)S(1)} %add_add_fusion.1.refs_1_, f32[192,128]{1,0:T(8,128)S(1)} %collective-permute-done.30.refs_2_, f32[8,256,512]{2,1,0:T(8,128)S(1)} %get-tuple-element.22.refs_3_), custom_call_target="tpu_custom_call" | custom-call | tf_op jit(solution)/shard_map/second_sweep/pallas_call | solution.py:396
  (76 shorter events, 51.0 us)
Async XLA Ops:
  8.8 18.6 %collective-permute-start.1 = (f32[256,512]{1,0:T(8,128)S(1)}, f32[256,512]{1,0:T(8,128)S(1)}, u32[]{:S(2)}, u32[]{:S(2)}) collective-permute-start(f32[256,512]{1,0:T(8,128)S(1)} %get-tuple-element.14), channel_id=1, source_target_pairs={{0,32},{32,64},{64,96},{96,0},{1,33},{33,65},{65,97},{97,1},{2,34}... | collective-permute-start | bytes 1572872 | tf_op jit(solution)/shard_map/ppermute | solution.py:53
  11.3 16.1 %collective-permute-start.2 = (f32[256,512]{1,0:T(8,128)S(1)}, f32[256,512]{1,0:T(8,128)S(1)}, u32[]{:S(2)}, u32[]{:S(2)}) collective-permute-start(f32[256,512]{1,0:T(8,128)S(1)} %get-tuple-element.15), channel_id=1, source_target_pairs={{0,96},{32,0},{64,32},{96,64},{1,97},{33,1},{65,33},{97,65},{2,98}... | collective-permute-start | bytes 1572872 | tf_op jit(solution)/shard_map/ppermute | solution.py:53
  19.8 17.4 %collective-permute-start = (f32[256,512]{1,0:T(8,128)S(1)}, f32[256,512]{1,0:T(8,128)S(1)}, u32[]{:S(2)}, u32[]{:S(2)}) collective-permute-start(f32[256,512]{1,0:T(8,128)S(1)} %user_rows.4), channel_id=1, source_target_pairs={{0,64},{32,96},{64,0},{96,32},{1,65},{33,97},{65,1},{97,33},{2,66}... | collective-permute-start | bytes 1572872 | tf_op jit(solution)/shard_map/ppermute | solution.py:53
  37.4 13.2 %collective-permute-start.3 = (f32[256,512]{1,0:T(8,128)S(1)}, f32[256,512]{1,0:T(8,128)S(1)}, u32[]{:S(2)}, u32[]{:S(2)}) collective-permute-start(f32[256,512]{1,0:T(8,128)S(1)} %add_add_fusion.refs_1_), channel_id=1, source_target_pairs={{0,32},{32,64},{64,96},{96,0},{1,33},{33,65},{65,97},{97,1},{2,34}... | collective-permute-start | bytes 1572872 | tf_op jit(solution)/shard_map/ppermute | solution.py:53
  38.1 12.7 %collective-permute-start.5 = (f32[256,512]{1,0:T(8,128)S(1)}, f32[256,512]{1,0:T(8,128)S(1)}, u32[]{:S(2)}, u32[]{:S(2)}) collective-permute-start(f32[256,512]{1,0:T(8,128)S(1)} %add_add_fusion.refs_1_), channel_id=1, source_target_pairs={{0,96},{32,0},{64,32},{96,64},{1,97},{33,1},{65,33},{97,65},{2,98}... | collective-permute-start | bytes 1572872 | tf_op jit(solution)/shard_map/ppermute | solution.py:53
  50.7 16.4 %collective-permute-start.4 = (f32[128,512]{1,0:T(8,128)S(1)}, f32[128,512]{1,0:T(8,128)S(1)}, u32[]{:S(2)}, u32[]{:S(2)}) collective-permute-start(f32[128,512]{1,0:T(8,128)S(1)} %slice.16), channel_id=1, source_target_pairs={{0,32},{32,64},{64,96},{96,0},{1,33},{33,65},{65,97},{97,1},{2,34}... | collective-permute-start | bytes 786440 | tf_op jit(solution)/shard_map/ppermute | solution.py:53
  50.8 16.3 %collective-permute-start.6 = (f32[128,512]{1,0:T(8,128)S(1)}, f32[128,512]{1,0:T(8,128)S(1)}, u32[]{:S(2)}, u32[]{:S(2)}) collective-permute-start(f32[128,512]{1,0:T(8,128)S(1)} %slice.17), channel_id=1, source_target_pairs={{0,96},{32,0},{64,32},{96,64},{1,97},{33,1},{65,33},{97,65},{2,98}... | collective-permute-start | bytes 786440 | tf_op jit(solution)/shard_map/ppermute | solution.py:53
  71.8 7.1 %collective-permute-start.7 = (f32[4,256,512]{2,1,0:T(8,128)}, f32[4,256,512]{2,1,0:T(8,128)}, u32[]{:S(2)}, u32[]{:S(2)}) collective-permute-start(f32[4,256,512]{2,1,0:T(8,128)} %item_columns.7), channel_id=1, source_target_pairs={{0,1},{1,0},{2,3},{3,2},{4,5},{5,4},{6,7},{7,6},{8,9},{9,8},{10,11... | collective-permute-start | bytes 6291464 | tf_op jit(solution)/shard_map/ppermute | solution.py:54
  82.4 14.8 %collective-permute-start.10 = (f32[256,512]{1,0:T(8,128)}, f32[256,512]{1,0:T(8,128)S(1)}, u32[]{:S(2)}, u32[]{:S(2)}) collective-permute-start(f32[256,512]{1,0:T(8,128)} %get-tuple-element.23), channel_id=1, source_target_pairs={{0,6},{1,25},{2,0},{3,27},{4,2},{5,29},{6,4},{7,31},{8,14},{9,1},{... | collective-permute-start | bytes 1572872 | tf_op jit(solution)/shard_map/ppermute | solution.py:54
  85.1 15.5 %collective-permute-start.9 = (f32[256,512]{1,0:T(8,128)}, f32[256,512]{1,0:T(8,128)}, u32[]{:S(2)}, u32[]{:S(2)}) collective-permute-start(f32[256,512]{1,0:T(8,128)} %get-tuple-element.24), channel_id=1, source_target_pairs={{0,2},{1,9},{2,4},{3,11},{4,6},{5,13},{6,0},{7,15},{8,10},{9,17},{... | collective-permute-start | bytes 1572872 | tf_op jit(solution)/shard_map/ppermute | solution.py:54
  85.1 15.5 %collective-permute-start.8 = (f32[256,512]{1,0:T(8,128)S(1)}, f32[256,512]{1,0:T(8,128)}, u32[]{:S(2)}, u32[]{:S(2)}) collective-permute-start(f32[256,512]{1,0:T(8,128)S(1)} %add_bitcast_fusion.2), channel_id=1, source_target_pairs={{0,4},{1,17},{2,6},{3,19},{4,0},{5,21},{6,2},{7,23},{8,12},{9,25},... | collective-permute-start | bytes 1572872 | tf_op jit(solution)/shard_map/ppermute | solution.py:54
  102.4 10.0 %collective-permute-start.11 = (f32[256,512]{1,0:T(8,128)S(1)}, f32[256,512]{1,0:T(8,128)S(1)}, u32[]{:S(2)}, u32[]{:S(2)}) collective-permute-start(f32[256,512]{1,0:T(8,128)S(1)} %fusion), channel_id=1, source_target_pairs={{0,16},{1,5},{2,18},{3,7},{4,20},{5,1},{6,22},{7,3},{8,24},{9,13},... | collective-permute-start | bytes 1572872 | tf_op jit(solution)/shard_map/ppermute | solution.py:54
  104.9 13.0 %collective-permute-start.12 = (f32[256,512]{1,0:T(8,128)S(1)}, f32[256,512]{1,0:T(8,128)S(1)}, u32[]{:S(2)}, u32[]{:S(2)}) collective-permute-start(f32[256,512]{1,0:T(8,128)S(1)} %fusion), channel_id=1, source_target_pairs={{0,8},{1,3},{2,10},{3,5},{4,12},{5,7},{6,14},{7,1},{8,16},{9,11},{... | collective-permute-start | bytes 1572872 | tf_op jit(solution)/shard_map/ppermute | solution.py:54
  105.2 12.7 %collective-permute-start.13 = (f32[256,512]{1,0:T(8,128)S(1)}, f32[256,512]{1,0:T(8,128)S(1)}, u32[]{:S(2)}, u32[]{:S(2)}) collective-permute-start(f32[256,512]{1,0:T(8,128)S(1)} %fusion), channel_id=1, source_target_pairs={{0,24},{1,7},{2,26},{3,1},{4,28},{5,3},{6,30},{7,5},{8,0},{9,15},{... | collective-permute-start | bytes 1572872 | tf_op jit(solution)/shard_map/ppermute | solution.py:54
  118.2 9.6 %collective-permute-start.15 = (f32[256,512]{1,0:T(8,128)S(1)}, f32[256,512]{1,0:T(8,128)S(1)}, u32[]{:S(2)}, u32[]{:S(2)}) collective-permute-start(f32[256,512]{1,0:T(8,128)S(1)} %bitcast_add_fusion.refs_0_), channel_id=1, source_target_pairs={{0,2},{1,9},{2,4},{3,11},{4,6},{5,13},{6,0},{7,15},{8,10},{9,17},{... | collective-permute-start | bytes 1572872 | tf_op jit(solution)/shard_map/ppermute | solution.py:54
  118.3 13.0 %collective-permute-start.16 = (f32[256,512]{1,0:T(8,128)S(1)}, f32[256,512]{1,0:T(8,128)S(1)}, u32[]{:S(2)}, u32[]{:S(2)}) collective-permute-start(f32[256,512]{1,0:T(8,128)S(1)} %bitcast_add_fusion.refs_0_), channel_id=1, source_target_pairs={{0,6},{1,25},{2,0},{3,27},{4,2},{5,29},{6,4},{7,31},{8,14},{9,1},{... | collective-permute-start | bytes 1572872 | tf_op jit(solution)/shard_map/ppermute | solution.py:54
  121.0 18.0 %collective-permute-start.14 = (f32[256,512]{1,0:T(8,128)S(1)}, f32[256,512]{1,0:T(8,128)S(1)}, u32[]{:S(2)}, u32[]{:S(2)}) collective-permute-start(f32[256,512]{1,0:T(8,128)S(1)} %bitcast_add_fusion.refs_0_), channel_id=1, source_target_pairs={{0,1},{1,0},{2,3},{3,2},{4,5},{5,4},{6,7},{7,6},{8,9},{9,8},{10,11... | collective-permute-start | bytes 1572872 | tf_op jit(solution)/shard_map/ppermute | solution.py:54
  128.0 12.9 %collective-permute-start.17 = (f32[256,512]{1,0:T(8,128)S(1)}, f32[256,512]{1,0:T(8,128)S(1)}, u32[]{:S(2)}, u32[]{:S(2)}) collective-permute-start(f32[256,512]{1,0:T(8,128)S(1)} %collective-permute-done.15.refs_0_.refs_1_), channel_id=1, source_target_pairs={{0,1},{1,0},{2,3},{3,2},{4,5},{5,4},{6,7},{7,6},{8,9},{9,8},{10,11... | collective-permute-start | bytes 1572872 | tf_op jit(solution)/shard_map/ppermute | solution.py:54
  131.4 9.5 %collective-permute-start.18 = (f32[256,512]{1,0:T(8,128)S(1)}, f32[256,512]{1,0:T(8,128)S(1)}, u32[]{:S(2)}, u32[]{:S(2)}) collective-permute-start(f32[256,512]{1,0:T(8,128)S(1)} %collective-permute-done.16.refs_1_.refs_2_), channel_id=1, source_target_pairs={{0,1},{1,0},{2,3},{3,2},{4,5},{5,4},{6,7},{7,6},{8,9},{9,8},{10,11... | collective-permute-start | bytes 1572872 | tf_op jit(solution)/shard_map/ppermute | solution.py:54
  131.5 7.4 %collective-permute-start.20 = (f32[128,512]{1,0:T(8,128)S(1)}, f32[128,512]{1,0:T(8,128)}, u32[]{:S(2)}, u32[]{:S(2)}) collective-permute-start(f32[128,512]{1,0:T(8,128)S(1)} %slice.19), channel_id=1, source_target_pairs={{0,6},{1,25},{2,0},{3,27},{4,2},{5,29},{6,4},{7,31},{8,14},{9,1},{... | collective-permute-start | bytes 786440 | tf_op jit(solution)/shard_map/ppermute | solution.py:54
  134.4 9.1 %collective-permute-start.21 = (f32[128,512]{1,0:T(8,128)S(1)}, f32[128,512]{1,0:T(8,128)}, u32[]{:S(2)}, u32[]{:S(2)}) collective-permute-start(f32[128,512]{1,0:T(8,128)S(1)} %collective-permute-done.19.refs_0_.refs_3_), channel_id=1, source_target_pairs={{0,1},{1,0},{2,3},{3,2},{4,5},{5,4},{6,7},{7,6},{8,9},{9,8},{10,11... | collective-permute-start | bytes 786440 | tf_op jit(solution)/shard_map/ppermute | solution.py:54
  146.5 7.9 %collective-permute-start.24 = (f32[192,128]{1,0:T(8,128)S(1)}, f32[192,128]{1,0:T(8,128)S(1)}, u32[]{:S(2)}, u32[]{:S(2)}) collective-permute-start(f32[192,128]{1,0:T(8,128)S(1)} %last_grams.1), channel_id=1, source_target_pairs={{0,32},{32,64},{64,96},{96,0},{1,33},{33,65},{65,97},{97,1},{2,34}... | collective-permute-start | bytes 294920 | tf_op jit(solution)/shard_map/ppermute | solution.py:53
  146.8 7.6 %collective-permute-start.25 = (f32[192,128]{1,0:T(8,128)S(1)}, f32[192,128]{1,0:T(8,128)S(1)}, u32[]{:S(2)}, u32[]{:S(2)}) collective-permute-start(f32[192,128]{1,0:T(8,128)S(1)} %last_grams.1), channel_id=1, source_target_pairs={{0,96},{32,0},{64,32},{96,64},{1,97},{33,1},{65,33},{97,65},{2,98}... | collective-permute-start | bytes 294920 | tf_op jit(solution)/shard_map/ppermute | solution.py:53
  175.2 8.0 %collective-permute-start.28 = (f32[192,128]{1,0:T(8,128)S(1)}, f32[192,128]{1,0:T(8,128)S(1)}, u32[]{:S(2)}, u32[]{:S(2)}) collective-permute-start(f32[192,128]{1,0:T(8,128)S(1)} %get-tuple-element.21), channel_id=1, source_target_pairs={{0,32},{32,64},{64,96},{96,0},{1,33},{33,65},{65,97},{97,1},{2,34}... | collective-permute-start | bytes 294920 | tf_op jit(solution)/shard_map/ppermute | solution.py:53
  (12 other events, 51.3 us)
